TPU v7x, 32 devices: a whole 2x2x4 slice. The times are simulated.
32 devices in a mesh: groups: 2 (over y), tiles: 4 (over z), section: 4 (over x, core).
Axes of the slice: x: 2, y: 2, z: 4, core: 2. Of those that a mesh axis runs over, the one named last changes fastest.
Arguments:
- latents: float32 [4, 192, 8, 128], P('groups', None, 'tiles'), parts along dimension 0, may hold values from -6 to 6
- conv_weight: float32 [4, 27, 192, 192], P('section'), may hold values from -0.078125 to 0.078125
- gain: float32 [4, 192], P('section'), may hold values from 0.1 to 1.9
Outputs:
- decoded: float32 [4, 192, 8, 128], P('groups', 'section', 'tiles'), parts along dimension 0
There are 2 independent parts, one for each index of `groups`. A program takes and returns all parts, laid end to end along the dimension named above; an argument that names none is the same for every part. Nothing has to cross between parts.
All inputs are finite; a program needn't handle non-finite values.
Results may differ from a plain program's by a relative error of at most 0.00013.
Values sent between devices are 32-bit elements; how exact they have to be, the bound alone decides.
No kernel may reach another device: no remote copies, remote signals or barrier semaphores. Data moves between devices by JAX's collectives and lax.ppermute only.
A program may use at most 64 MiB of HBM per device.

v0:
```python
import jax
import jax.numpy as jnp
from jax import lax
from jax.experimental import pallas as pl
from jax.experimental.pallas import tpu as pltpu
from jax.sharding import PartitionSpec as P


EPSILON = 1e-06
GRANT = pltpu.CompilerParams(vmem_limit_bytes=12 * 2**20)
VMEM = pl.BlockSpec(memory_space=pltpu.VMEM)
ANY = pl.BlockSpec(memory_space=pl.ANY)


def partner_a(tile, tiles):
    other = tile ^ 1
    return other if other < tiles else tile


def partner_b(tile, tiles):
    other = ((tile - 1) ^ 1) + 1 if tile > 0 else tile
    return other if other < tiles else tile


def idle_cycle(where, names):
    for k, name in enumerate(names):
        where[name] = names[(k + 1) % len(names)]


def section_hop(layer, sections):
    where = {}
    if layer % 2 == 0:
        idle_cycle(where, [layer, layer + 1])
    elif layer + 2 < sections:
        idle_cycle(where, [layer - 1, layer, layer + 1, layer + 2])
    else:
        idle_cycle(where, [layer - 1, layer, layer + 1])
    taken = set(where)
    for s in range(sections):
        if s not in taken:
            where[s] = s ^ 1 if (s ^ 1) not in taken and (s ^ 1) < sections else s
    return where


def hop_pairs(layer, tiles, sections, tile_of):
    hop = section_hop(layer, sections)
    pairs = []
    for t in range(tiles):
        for s in range(sections):
            goal = tile_of(t) if s == layer else t
            pairs.append((t * sections + s, goal * sections + hop[s]))
    return pairs


def rim_pairs(tiles, sections, tile_of):
    pairs = []
    for t in range(tiles):
        where = {}
        if tile_of(t) == t:
            for s in range(sections):
                where[s] = s ^ 1 if (s ^ 1) < sections else s
        else:
            idle_cycle(where, list(range(1, sections)))
        for s in range(sections):
            if s == 0 and tile_of(t) != t:
                pairs.append((t * sections, tile_of(t) * sections))
            else:
                pairs.append((t * sections + s, t * sections + where[s]))
    return pairs


def share_pairs(target, tiles, sections):
    last = sections - 1
    where = {}
    if target == last - 1 or (target ^ 1) >= last - 1:
        idle_cycle(where, [last, target])
    else:
        idle_cycle(where, [last, target, target ^ 1, last - 1])
    taken = set(where)
    for s in range(sections):
        if s not in taken:
            where[s] = s ^ 1 if (s ^ 1) not in taken and (s ^ 1) < sections else s
    return [
        (t * sections + s, t * sections + where[s])
        for t in range(tiles)
        for s in range(sections)
    ]


def send(value, pairs):
    return lax.ppermute(value, ("tiles", "section"), pairs)


def split(values):
    high = values.astype(jnp.bfloat16)
    low = (values - high.astype(jnp.float32)).astype(jnp.bfloat16)
    return high, low


def held(shape, dtype=jnp.float32):
    return pltpu.VMEM(shape, dtype)


def prepare(weight, gain, steps, depth, width):
    channels = weight.shape[1]
    first = 9 * (3 - steps)
    groups = [(k, min(2, 9 - k)) for k in range(0, 9, 2)]

    def kernel(weight_ref, gain_ref, high, low, gains, staged, sems):
        copies = {}
        for a in reversed(range(steps)):
            for n, (k, size) in enumerate(groups):
                at = 9 * a + k
                copies[a, k] = pltpu.make_async_copy(
                    weight_ref.at[pl.ds(first + at, size)],
                    staged.at[pl.ds(at, size)],
                    sems.at[a, n],
                )
                copies[a, k].start()
        square = (channels, channels)
        lane = lax.broadcasted_iota(jnp.int32, square, 1)
        sublane = lax.broadcasted_iota(jnp.int32, square, 0)
        spread = jnp.broadcast_to(gain_ref[...], square)
        column = jnp.sum(jnp.where(lane == sublane, spread, 0.0), axis=1, keepdims=True)
        gains[...] = jnp.broadcast_to(column, (channels, width))
        for a in reversed(range(steps)):
            for k, size in groups:
                copies[a, k].wait()
                parts = [staged[9 * a + k + n] for n in range(size)]
                span = size * channels
                if k + size == 9 and depth > 9 * channels:
                    extra = depth - 9 * channels
                    parts.append(jnp.zeros((channels, extra), jnp.float32))
                    span += extra
                upper, lower = split(jnp.concatenate(parts, axis=1))
                high[a, :, k * channels : k * channels + span] = upper
                low[a, :, k * channels : k * channels + span] = lower

    shape = (steps, channels, depth)
    return pl.pallas_call(
        kernel,
        out_shape=(
            held(shape, jnp.bfloat16),
            held(shape, jnp.bfloat16),
            held((channels, width)),
        ),
        in_specs=[pl.BlockSpec(memory_space=pltpu.HBM), VMEM],
        out_specs=(VMEM, VMEM, VMEM),
        scratch_shapes=[
            pltpu.VMEM((9 * steps, channels, channels), jnp.float32),
            pltpu.SemaphoreType.DMA((steps, len(groups))),
        ],
        compiler_params=GRANT,
        name="prepare",
    )(pltpu.with_memory_space_constraint(weight, pltpu.HBM), gain)


def edges(latents, rows):
    frames, lines, width = latents.shape
    channels = lines // rows

    def kernel(ref, *outs):
        even = lax.rem(lax.axis_index("tiles"), 2) == 0
        for f in range(frames):
            top = ref[f, pl.ds(0, channels, stride=rows), :]
            bottom = ref[f, pl.ds(rows - 1, channels, stride=rows), :]
            outs[2 * f][...] = jnp.where(even, bottom, top)
            outs[2 * f + 1][...] = jnp.where(even, top, bottom)

    return pl.pallas_call(
        kernel,
        out_shape=tuple([held((channels, width))] * (2 * frames)),
        in_specs=[VMEM],
        out_specs=tuple([VMEM] * (2 * frames)),
        compiler_params=GRANT,
        name="edges",
    )(latents)


def normalize(values, gain):
    meansq = jnp.mean(values * values, axis=0, keepdims=True)
    scaled = values * lax.rsqrt(meansq + EPSILON) * gain
    return scaled / (1.0 + jnp.exp(-scaled))


def shifted(values, col_off):
    if col_off == 1:
        return values
    width = values.shape[1]
    lane = lax.broadcasted_iota(jnp.int32, values.shape, 1)
    if col_off == 0:
        return jnp.where(lane == 0, 0.0, pltpu.roll(values, 1, 1))
    return jnp.where(lane == width - 1, 0.0, pltpu.roll(values, width - 1, 1))


def product(high, low, patch_high, patch_low):
    def dot(a, b):
        return jnp.dot(a, b, preferred_element_type=jnp.float32)

    return dot(high, patch_high) + dot(low, patch_high) + dot(high, patch_low)


def frame_step(layer, tiles, sections, main, frame, near_a, near_b, gain, weights, partial, keep):
    channels, width = near_a.shape
    lines = main.shape[-2]
    rows = lines // channels
    steps, _, depth = weights[0].shape
    last = layer == sections - 1
    share = lines // sections
    count = sections if last else 3

    def kernel(*refs):
        main_ref, a_ref, b_ref, gain_ref, high_ref, low_ref = refs[:6]
        refs = refs[6:]
        if partial is not None:
            partial_ref, refs = refs[0], refs[1:]
        outs, (patch_high, patch_low) = refs[:count], refs[count:]
        tile = lax.axis_index("tiles")
        even = lax.rem(tile, 2) == 0

        @pl.when(lax.axis_index("section") == layer)
        def _():
            gains = gain_ref[...]
            near_one, near_two = a_ref[...], b_ref[...]
            above = jnp.where(even, near_two, near_one)
            below = jnp.where(even, near_one, near_two)
            above = jnp.where(tile == 0, 0.0, above)
            below = jnp.where(tile == tiles - 1, 0.0, below)
            own = []
            for r in range(rows):
                line = pl.ds(r, channels, stride=rows)
                own.append(main_ref[line, :] if frame is None else main_ref[frame, line, :])
            if depth > 9 * channels:
                pad = jnp.zeros((depth - 9 * channels, rows * width), jnp.bfloat16)
                patch_high[9 * channels :, :] = pad
                patch_low[9 * channels :, :] = pad
            for q, source in enumerate([above] + own + [below]):
                normed = normalize(source, gains)
                for e in range(3):
                    upper, lower = split(shifted(normed, e))
                    for b in range(3):
                        r = q - b
                        if 0 <= r < rows:
                            k = (3 * b + e) * channels
                            cols = slice(r * width, (r + 1) * width)
                            patch_high[k : k + channels, cols] = upper
                            patch_low[k : k + channels, cols] = lower
            total = product(
                high_ref[steps - 1], low_ref[steps - 1], patch_high[...], patch_low[...]
            )
            if partial is not None:
                total = total + partial_ref[...]
            results = [
                own[r] + total[:, r * width : (r + 1) * width] for r in range(rows)
            ]
            if last:
                part = share // rows
                for s in range(sections):
                    for r in range(rows):
                        outs[s][pl.ds(r, part, stride=rows), :] = results[r][
                            s * part : (s + 1) * part
                        ]
            else:
                for r in range(rows):
                    outs[0][pl.ds(r, channels, stride=rows), :] = results[r]
                outs[1][...] = jnp.where(even, results[-1], results[0])
                outs[2][...] = jnp.where(even, results[0], results[-1])

    operands = [main, near_a, near_b, gain, *weights]
    if partial is not None:
        operands.append(partial)
    if last:
        out_shape = [held((share, width))] * sections
    else:
        out_shape = [held((lines, width)), held(near_a.shape), held(near_a.shape)]
    patch = held((depth, rows * width), jnp.bfloat16)
    scratch = []
    if keep:
        out_shape += [patch, patch]
    else:
        scratch = [patch, patch]
    return pl.pallas_call(
        kernel,
        out_shape=tuple(out_shape),
        in_specs=[VMEM] * len(operands),
        out_specs=tuple([VMEM] * len(out_shape)),
        scratch_shapes=scratch,
        cost_estimate=pl.CostEstimate(
            flops=6 * channels * depth * rows * width,
            bytes_accessed=2**20,
            transcendentals=0,
        ),
        compiler_params=GRANT,
        name="frame_step",
    )(*operands)


def earlier_frames(layer, weights, patches):
    steps, channels, depth = weights[0].shape
    count = len(patches)
    columns = patches[0][0].shape[1]

    def kernel(high_ref, low_ref, *refs):
        out_ref = refs[-1]

        @pl.when(lax.axis_index("section") == layer)
        def _():
            total = None
            for n in range(count):
                a = steps - 1 - (count - n)
                term = product(
                    high_ref[a], low_ref[a], refs[2 * n][...], refs[2 * n + 1][...]
                )
                total = term if total is None else total + term
            out_ref[...] = total

    operands = [*weights]
    for pair in patches:
        operands += list(pair)
    return pl.pallas_call(
        kernel,
        out_shape=held((channels, columns)),
        in_specs=[VMEM] * len(operands),
        out_specs=VMEM,
        cost_estimate=pl.CostEstimate(
            flops=6 * channels * depth * columns * count,
            bytes_accessed=2**20,
            transcendentals=0,
        ),
        compiler_params=GRANT,
        name="earlier_frames",
    )(*operands)


def local(latents, conv_weight, gain):
    frames, channels, rows, width = latents.shape
    tiles, sections = lax.axis_size("tiles"), lax.axis_size("section")
    section = lax.axis_index("section")
    depth = -(-9 * channels // 256) * 256
    steps = min(frames, 3)
    of_a = lambda t: partner_a(t, tiles)
    of_b = lambda t: partner_b(t, tiles)

    flat = latents.reshape(frames, channels * rows, width)
    edge = edges(flat, rows)
    edge_a, edge_b = edge[0::2], edge[1::2]
    rim_a, rim_b = (rim_pairs(tiles, sections, of) for of in (of_a, of_b))
    near_a, near_b = [], []
    for f in range(frames):
        near_a.append(send(edge_a[f], rim_a))
        near_b.append(send(edge_b[f], rim_b))
    *weights, gains = prepare(conv_weight[0], gain, steps, depth, width)
    main = [flat] * frames

    for layer in range(sections):
        if layer > 0:
            straight = hop_pairs(layer - 1, tiles, sections, lambda t: t)
            cross_a = hop_pairs(layer - 1, tiles, sections, of_a)
            cross_b = hop_pairs(layer - 1, tiles, sections, of_b)
            main = [send(main[f], straight) for f in range(frames)]
            near_a = [send(edge_a[f], cross_a) for f in range(frames)]
            near_b = [send(edge_b[f], cross_b) for f in range(frames)]
        patches, next_main, edge_a, edge_b = [], [], [], []
        for f in range(frames):
            partial = None
            if f > 0:
                partial = earlier_frames(layer, weights, patches[-2:])
            keep = f < frames - 1
            done = frame_step(
                layer, tiles, sections, main[f], f if layer == 0 else None,
                near_a[f], near_b[f], gains, weights, partial, keep,
            )
            if keep:
                patches.append(done[-2:])
                done = done[:-2]
            next_main.append(done if layer == sections - 1 else done[0])
            edge_a.append(done[1])
            edge_b.append(done[2])
        main = next_main

    outs = []
    for f in range(frames):
        own = main[f][sections - 1]
        for target in range(sections - 1):
            pairs = share_pairs(target, tiles, sections)
            got = send(main[f][target], pairs)
            own = jnp.where(section == target, got, own)
        outs.append(own)
    return jnp.stack(outs).reshape(frames, channels // sections, rows, width)


def solution(mesh):
    return jax.shard_map(
        local,
        mesh=mesh,
        in_specs=(
            P("groups", None, "tiles", None),
            P("section", None, None, None),
            P("section", None),
        ),
        out_specs=P("groups", "section", "tiles", None),
        check_vma=False,
    )
```

profile of v0, /device:TPU:0, one launch (start us, length us, event | category | flops | bytes accessed | tf_op | source)
XLA Modules:
  0.0 43.4 jit_solution(3086914867170947993)
XLA Ops:
  0.0 1.0 %copy-done = f32[2,192,2,128]{3,2,1,0:T(2,128)S(1)} copy-done((f32[2,192,2,128]{3,2,1,0:T(2,128)S(1)}, f32[2,192,2,128]{3,2,1,0:T(2,128)}, u32[]{:S(2)}) %copy-start) | copy-done | bytes 393240
  1.0 3.1 %collective-permute-start = (f32[192,128]{1,0:T(8,128)S(1)}, f32[192,128]{1,0:T(8,128)S(1)}, u32[]{:S(2)}, u32[]{:S(2)}) collective-permute-start(f32[192,128]{1,0:T(8,128)S(1)} %get-tuple-element.46), channel_id=1, source_target_pairs={{0,4},{1,2},{2,3},{3,1},{4,0},{5,6},{6,7},{7,5},{8,12},{9,10},{10,... | collective-permute-start | bytes 294920 | tf_op jit(solution)/shard_map/ppermute | solution.py:91
  4.2 3.1 %collective-permute-start.14 = (f32[192,128]{1,0:T(8,128)S(1)}, f32[192,128]{1,0:T(8,128)S(1)}, u32[]{:S(2)}, u32[]{:S(2)}) collective-permute-start(f32[192,128]{1,0:T(8,128)S(1)} %get-tuple-element.64), channel_id=1, source_target_pairs={{0,4},{1,2},{2,3},{3,1},{4,0},{5,6},{6,7},{7,5},{8,12},{9,10},{10,... | collective-permute-start | bytes 294920 | tf_op jit(solution)/shard_map/ppermute | solution.py:91
  7.3 0.7 %copy-done.2 = f32[1,192]{1,0:T(1,128)S(1)} copy-done((f32[1,192]{1,0:T(1,128)S(1)}, f32[1,192]{1,0:T(1,128)}, u32[]{:S(2)}) %copy-start.2) | copy-done | bytes 792
  8.0 2.2 %prepare.1 = (bf16[2,192,1792]{2,1,0:T(8,128)(2,1)S(1)}, bf16[2,192,1792]{2,1,0:T(8,128)(2,1)S(1)}, f32[192,128]{1,0:T(8,128)S(1)}) custom-call(f32[27,192,192]{2,1,0:T(8,128)} %bitcast.7, f32[1,192]{1,0:T(1,128)S(1)} %copy-done.2), custom_call_target="tpu_custom_call" | custom-call | tf_op jit(solution)/shard_map/prepare/pallas_call | solution.py:140
  10.2 1.1 %frame_step.8 = (f32[384,128]{1,0:T(8,128)S(1)}, f32[192,128]{1,0:T(8,128)S(1)}, f32[192,128]{1,0:T(8,128)S(1)}, bf16[1792,256]{1,0:T(8,128)(2,1)S(1)}, bf16[1792,256]{1,0:T(8,128)(2,1)S(1)}) custom-call(f32[2,384,128]{2,1,0:T(8,128)S(1)} %bitcast.5, f32[192,128]{1,0:T(8,128)S(1)} %collective-permute-done.refs_1_, ...), custom_call_target="tpu_custom_call" | custom-call | flops 528482304 | bytes 1048576 | tf_op jit(solution)/shard_map/frame_step/pallas_call | solution.py:282
  11.4 1.7 %collective-permute-start.3 = (f32[192,128]{1,0:T(8,128)S(1)}, f32[192,128]{1,0:T(8,128)S(1)}, u32[]{:S(2)}, u32[]{:S(2)}) collective-permute-start(f32[192,128]{1,0:T(8,128)S(1)} %get-tuple-element.52), channel_id=1, source_target_pairs={{0,5},{1,0},{2,3},{3,2},{4,1},{5,4},{6,7},{7,6},{8,13},{9,8},{10,1... | collective-permute-start | bytes 294920 | tf_op jit(solution)/shard_map/ppermute | solution.py:91
  13.1 0.7 %earlier_frames.4.refs_6_ = f32[192,256]{1,0:T(8,128)S(1)} custom-call(bf16[2,192,1792]{2,1,0:T(8,128)(2,1)S(1)} %get-tuple-element.49.refs_4_.high_ref, bf16[2,192,1792]{2,1,0:T(8,128)(2,1)S(1)} %get-tuple-element.50.refs_5_.low_ref, bf16[1792,256]{1,0:T(8,128)(2,1)S(1)} %get-tuple-element.66.refs_0_, bf16[1792,256]{1,0:T(8,128)(2,1)S(1)} %get-tuple-element.67.refs_1_), custom_call_target="tpu_custom_call" | custom-call | flops 528482304 | bytes 1048576 | tf_op jit(solution)/shard_map/earlier_frames/pallas_call | solution.py:320
  13.8 1.1 %frame_step.12 = (f32[384,128]{1,0:T(8,128)S(1)}, f32[192,128]{1,0:T(8,128)S(1)}, f32[192,128]{1,0:T(8,128)S(1)}) custom-call(f32[2,384,128]{2,1,0:T(8,128)S(1)} %bitcast.6, f32[192,128]{1,0:T(8,128)S(1)} %collective-permute-done.14.refs_1_, f32[192,128]{1,0:T(8,128)S(1)} %collective-permute-done.15.refs_2_, f32[192,128]{1,0:T(8,128)S(1)} %get-tuple-element.48.refs_3_, ...), custom_call_target="tpu_custom_call" | custom-call | flops 528482304 | bytes 1048576 | tf_op jit(solution)/shard_map/frame_step/pallas_call | solution.py:282
  15.0 0.1 collective-permute-start.16
  15.0 0.6 %collective-permute-start.17 = (f32[192,128]{1,0:T(8,128)S(1)}, f32[192,128]{1,0:T(8,128)S(1)}, u32[]{:S(2)}, u32[]{:S(2)}) collective-permute-start(f32[192,128]{1,0:T(8,128)S(1)} %get-tuple-element.69), channel_id=1, source_target_pairs={{0,5},{1,0},{2,3},{3,2},{4,1},{5,4},{6,7},{7,6},{8,13},{9,8},{10,1... | collective-permute-start | bytes 294920 | tf_op jit(solution)/shard_map/ppermute | solution.py:91
  15.6 0.3 collective-permute-start.18
  16.0 1.3 %collective-permute-start.5 = (f32[384,128]{1,0:T(8,128)S(1)}, f32[384,128]{1,0:T(8,128)S(1)}, u32[]{:S(2)}, u32[]{:S(2)}) collective-permute-start(f32[384,128]{1,0:T(8,128)S(1)} %get-tuple-element.54), channel_id=1, source_target_pairs={{0,1},{1,2},{2,3},{3,0},{4,5},{5,6},{6,7},{7,4},{8,9},{9,10},{10,1... | collective-permute-start | bytes 589832 | tf_op jit(solution)/shard_map/ppermute | solution.py:91
  17.4 0.5 %collective-permute-done.17.refs_1_ = f32[192,128]{1,0:T(8,128)S(1)} collective-permute-done((f32[192,128]{1,0:T(8,128)S(1)}, f32[192,128]{1,0:T(8,128)S(1)}, u32[]{:S(2)}, u32[]{:S(2)}) %collective-permute-start.17) | collective-permute-done | bytes 98336 | tf_op jit(solution)/shard_map/ppermute | solution.py:91
  17.8 2.0 %collective-permute-start.7 = (f32[192,128]{1,0:T(8,128)S(1)}, f32[192,128]{1,0:T(8,128)S(1)}, u32[]{:S(2)}, u32[]{:S(2)}) collective-permute-start(f32[192,128]{1,0:T(8,128)S(1)} %get-tuple-element.56), channel_id=1, source_target_pairs={{0,1},{1,2},{2,3},{3,0},{4,5},{5,10},{6,7},{7,4},{8,9},{9,6},{10,1... | collective-permute-start | bytes 294920 | tf_op jit(solution)/shard_map/ppermute | solution.py:91
  19.9 1.2 %collective-permute-start.19 = (f32[384,128]{1,0:T(8,128)S(1)}, f32[384,128]{1,0:T(8,128)S(1)}, u32[]{:S(2)}, u32[]{:S(2)}) collective-permute-start(f32[384,128]{1,0:T(8,128)S(1)} %get-tuple-element.73), channel_id=1, source_target_pairs={{0,1},{1,2},{2,3},{3,0},{4,5},{5,6},{6,7},{7,4},{8,9},{9,10},{10,1... | collective-permute-start | bytes 589832 | tf_op jit(solution)/shard_map/ppermute | solution.py:91
  21.1 1.0 %collective-permute-done.6.refs_1_ = f32[192,128]{1,0:T(8,128)S(1)} collective-permute-done((f32[192,128]{1,0:T(8,128)S(1)}, f32[192,128]{1,0:T(8,128)S(1)}, u32[]{:S(2)}, u32[]{:S(2)}) %collective-permute-start.6) | collective-permute-done | bytes 98336 | tf_op jit(solution)/shard_map/ppermute | solution.py:91
  22.1 1.1 %collective-permute-done.7.refs_2_ = f32[192,128]{1,0:T(8,128)S(1)} collective-permute-done((f32[192,128]{1,0:T(8,128)S(1)}, f32[192,128]{1,0:T(8,128)S(1)}, u32[]{:S(2)}, u32[]{:S(2)}) %collective-permute-start.7) | collective-permute-done | bytes 98336 | tf_op jit(solution)/shard_map/ppermute | solution.py:91
  23.2 0.5 %collective-permute-start.9 = (f32[192,128]{1,0:T(8,128)S(1)}, f32[192,128]{1,0:T(8,128)S(1)}, u32[]{:S(2)}, u32[]{:S(2)}) collective-permute-start(f32[192,128]{1,0:T(8,128)S(1)} %get-tuple-element.58), channel_id=1, source_target_pairs={{0,1},{1,0},{2,7},{3,2},{4,5},{5,4},{6,3},{7,6},{8,9},{9,8},{10,15... | collective-permute-start | bytes 294920 | tf_op jit(solution)/shard_map/ppermute | solution.py:91
  23.7 2.6 %collective-permute-done.20.refs_1_ = f32[192,128]{1,0:T(8,128)S(1)} collective-permute-done((f32[192,128]{1,0:T(8,128)S(1)}, f32[192,128]{1,0:T(8,128)S(1)}, u32[]{:S(2)}, u32[]{:S(2)}) %collective-permute-start.20) | collective-permute-done | bytes 98336 | tf_op jit(solution)/shard_map/ppermute | solution.py:91
  26.3 1.0 %collective-permute-done.21.refs_2_ = f32[192,128]{1,0:T(8,128)S(1)} collective-permute-done((f32[192,128]{1,0:T(8,128)S(1)}, f32[192,128]{1,0:T(8,128)S(1)}, u32[]{:S(2)}, u32[]{:S(2)}) %collective-permute-start.21) | collective-permute-done | bytes 98336 | tf_op jit(solution)/shard_map/ppermute | solution.py:91
  27.4 0.5 %collective-permute-start.23 = (f32[192,128]{1,0:T(8,128)S(1)}, f32[192,128]{1,0:T(8,128)S(1)}, u32[]{:S(2)}, u32[]{:S(2)}) collective-permute-start(f32[192,128]{1,0:T(8,128)S(1)} %get-tuple-element.79), channel_id=1, source_target_pairs={{0,1},{1,0},{2,7},{3,2},{4,5},{5,4},{6,3},{7,6},{8,9},{9,8},{10,15... | collective-permute-start | bytes 294920 | tf_op jit(solution)/shard_map/ppermute | solution.py:91
  28.0 1.0 %collective-permute-done.23.refs_1_ = f32[192,128]{1,0:T(8,128)S(1)} collective-permute-done((f32[192,128]{1,0:T(8,128)S(1)}, f32[192,128]{1,0:T(8,128)S(1)}, u32[]{:S(2)}, u32[]{:S(2)}) %collective-permute-start.23) | collective-permute-done | bytes 98336 | tf_op jit(solution)/shard_map/ppermute | solution.py:91
  29.0 0.2 collective-permute-done.24.refs_2_
  29.2 0.2 collective-permute-start.25
  29.4 7.6 %collective-permute-start.26 = (f32[96,128]{1,0:T(8,128)S(1)}, f32[96,128]{1,0:T(8,128)S(1)}, u32[]{:S(2)}, u32[]{:S(2)}) collective-permute-start(f32[96,128]{1,0:T(8,128)S(1)} %get-tuple-element.84), channel_id=1, source_target_pairs={{0,2},{1,0},{2,3},{3,1},{4,6},{5,4},{6,7},{7,5},{8,10},{9,8},{10,1... | collective-permute-start | bytes 147464 | tf_op jit(solution)/shard_map/ppermute | solution.py:91
  37.0 0.1 collective-permute-start.11
  37.1 2.0 %collective-permute-start.12 = (f32[96,128]{1,0:T(8,128)S(1)}, f32[96,128]{1,0:T(8,128)S(1)}, u32[]{:S(2)}, u32[]{:S(2)}) collective-permute-start(f32[96,128]{1,0:T(8,128)S(1)} %get-tuple-element.61), channel_id=1, source_target_pairs={{0,2},{1,0},{2,3},{3,1},{4,6},{5,4},{6,7},{7,5},{8,10},{9,8},{10,1... | collective-permute-start | bytes 147464 | tf_op jit(solution)/shard_map/ppermute | solution.py:91
  39.1 1.4 %collective-permute-done.27 = f32[96,128]{1,0:T(8,128)S(1)} collective-permute-done((f32[96,128]{1,0:T(8,128)S(1)}, f32[96,128]{1,0:T(8,128)S(1)}, u32[]{:S(2)}, u32[]{:S(2)}) %collective-permute-start.27) | collective-permute-done | bytes 49184 | tf_op jit(solution)/shard_map/ppermute | solution.py:91
  40.5 0.4 collective-permute-done.12
  40.9 1.8 %collective-permute-done.13 = f32[96,128]{1,0:T(8,128)S(1)} collective-permute-done((f32[96,128]{1,0:T(8,128)S(1)}, f32[96,128]{1,0:T(8,128)S(1)}, u32[]{:S(2)}, u32[]{:S(2)}) %collective-permute-start.13) | collective-permute-done | bytes 49184 | tf_op jit(solution)/shard_map/ppermute | solution.py:91
  42.7 0.7 %pad_maximum_fusion = f32[2,48,2,128]{3,2,1,0:T(2,128)} fusion(f32[1,48,2,128]{3,2,1,0:T(2,128)S(1)} %bitcast.8, f32[1,48,2,128]{3,2,1,0:T(2,128)S(1)} %bitcast.9), kind=kLoop, calls=%fused_computation | loop fusion | flops 24576 | bytes 196608 | tf_op jit(solution)/shard_map/stack | solution.py:389
  (47 shorter events, 0.4 us)
Async XLA Ops:
  0.0 1.0 %copy-start = (f32[2,192,2,128]{3,2,1,0:T(2,128)S(1)}, f32[2,192,2,128]{3,2,1,0:T(2,128)}, u32[]{:S(2)}) copy-start(f32[2,192,2,128]{3,2,1,0:T(2,128)} %param.3) | copy-start | bytes 1179652
  1.0 9.1 %collective-permute-start = (f32[192,128]{1,0:T(8,128)S(1)}, f32[192,128]{1,0:T(8,128)S(1)}, u32[]{:S(2)}, u32[]{:S(2)}) collective-permute-start(f32[192,128]{1,0:T(8,128)S(1)} %get-tuple-element.46), channel_id=1, source_target_pairs={{0,4},{1,2},{2,3},{3,1},{4,0},{5,6},{6,7},{7,5},{8,12},{9,10},{10,... | collective-permute-start | bytes 294920 | tf_op jit(solution)/shard_map/ppermute | solution.py:91
  4.2 6.1 %collective-permute-start.1 = (f32[192,128]{1,0:T(8,128)S(1)}, f32[192,128]{1,0:T(8,128)S(1)}, u32[]{:S(2)}, u32[]{:S(2)}) collective-permute-start(f32[192,128]{1,0:T(8,128)S(1)} %get-tuple-element.47), channel_id=1, source_target_pairs={{0,1},{1,0},{2,3},{3,2},{4,8},{5,6},{6,7},{7,5},{8,4},{9,10},{10,1... | collective-permute-start | bytes 294920 | tf_op jit(solution)/shard_map/ppermute | solution.py:91
  4.2 9.7 %collective-permute-start.14 = (f32[192,128]{1,0:T(8,128)S(1)}, f32[192,128]{1,0:T(8,128)S(1)}, u32[]{:S(2)}, u32[]{:S(2)}) collective-permute-start(f32[192,128]{1,0:T(8,128)S(1)} %get-tuple-element.64), channel_id=1, source_target_pairs={{0,4},{1,2},{2,3},{3,1},{4,0},{5,6},{6,7},{7,5},{8,12},{9,10},{10,... | collective-permute-start | bytes 294920 | tf_op jit(solution)/shard_map/ppermute | solution.py:91
  7.3 6.5 %collective-permute-start.15 = (f32[192,128]{1,0:T(8,128)S(1)}, f32[192,128]{1,0:T(8,128)S(1)}, u32[]{:S(2)}, u32[]{:S(2)}) collective-permute-start(f32[192,128]{1,0:T(8,128)S(1)} %get-tuple-element.65), channel_id=1, source_target_pairs={{0,1},{1,0},{2,3},{3,2},{4,8},{5,6},{6,7},{7,5},{8,4},{9,10},{10,1... | collective-permute-start | bytes 294920 | tf_op jit(solution)/shard_map/ppermute | solution.py:91
  7.3 0.7 %copy-start.2 = (f32[1,192]{1,0:T(1,128)S(1)}, f32[1,192]{1,0:T(1,128)}, u32[]{:S(2)}) copy-start(f32[1,192]{1,0:T(1,128)} %gain_ref.1) | copy-start | bytes 2308
  8.0 2.2 %copy-start.1 = (f32[2,192,2,128]{3,2,1,0:T(2,128)S(1)}, f32[2,192,2,128]{3,2,1,0:T(2,128)}, u32[]{:S(2)}) copy-start(f32[2,192,2,128]{3,2,1,0:T(2,128)} %param.3) | copy-start | bytes 1179652
  11.3 4.6 %collective-permute-start.2 = (f32[384,128]{1,0:T(8,128)S(1)}, f32[384,128]{1,0:T(8,128)S(1)}, u32[]{:S(2)}, u32[]{:S(2)}) collective-permute-start(f32[384,128]{1,0:T(8,128)S(1)} %get-tuple-element.51), channel_id=1, source_target_pairs={{0,1},{1,0},{2,3},{3,2},{4,5},{5,4},{6,7},{7,6},{8,9},{9,8},{10,11... | collective-permute-start | bytes 589832 | tf_op jit(solution)/shard_map/ppermute | solution.py:91
  11.4 4.2 %collective-permute-start.3 = (f32[192,128]{1,0:T(8,128)S(1)}, f32[192,128]{1,0:T(8,128)S(1)}, u32[]{:S(2)}, u32[]{:S(2)}) collective-permute-start(f32[192,128]{1,0:T(8,128)S(1)} %get-tuple-element.52), channel_id=1, source_target_pairs={{0,5},{1,0},{2,3},{3,2},{4,1},{5,4},{6,7},{7,6},{8,13},{9,8},{10,1... | collective-permute-start | bytes 294920 | tf_op jit(solution)/shard_map/ppermute | solution.py:91
  13.1 2.8 %collective-permute-start.4 = (f32[192,128]{1,0:T(8,128)S(1)}, f32[192,128]{1,0:T(8,128)S(1)}, u32[]{:S(2)}, u32[]{:S(2)}) collective-permute-start(f32[192,128]{1,0:T(8,128)S(1)} %get-tuple-element.53), channel_id=1, source_target_pairs={{0,1},{1,0},{2,3},{3,2},{4,9},{5,4},{6,7},{7,6},{8,5},{9,8},{10,11... | collective-permute-start | bytes 294920 | tf_op jit(solution)/shard_map/ppermute | solution.py:91
  15.0 4.9 %collective-permute-start.16 = (f32[384,128]{1,0:T(8,128)S(1)}, f32[384,128]{1,0:T(8,128)S(1)}, u32[]{:S(2)}, u32[]{:S(2)}) collective-permute-start(f32[384,128]{1,0:T(8,128)S(1)} %get-tuple-element.68), channel_id=1, source_target_pairs={{0,1},{1,0},{2,3},{3,2},{4,5},{5,4},{6,7},{7,6},{8,9},{9,8},{10,11... | collective-permute-start | bytes 589832 | tf_op jit(solution)/shard_map/ppermute | solution.py:91
  15.0 2.8 %collective-permute-start.17 = (f32[192,128]{1,0:T(8,128)S(1)}, f32[192,128]{1,0:T(8,128)S(1)}, u32[]{:S(2)}, u32[]{:S(2)}) collective-permute-start(f32[192,128]{1,0:T(8,128)S(1)} %get-tuple-element.69), channel_id=1, source_target_pairs={{0,5},{1,0},{2,3},{3,2},{4,1},{5,4},{6,7},{7,6},{8,13},{9,8},{10,1... | collective-permute-start | bytes 294920 | tf_op jit(solution)/shard_map/ppermute | solution.py:91
  15.6 4.2 %collective-permute-start.18 = (f32[192,128]{1,0:T(8,128)S(1)}, f32[192,128]{1,0:T(8,128)S(1)}, u32[]{:S(2)}, u32[]{:S(2)}) collective-permute-start(f32[192,128]{1,0:T(8,128)S(1)} %get-tuple-element.70), channel_id=1, source_target_pairs={{0,1},{1,0},{2,3},{3,2},{4,9},{5,4},{6,7},{7,6},{8,5},{9,8},{10,11... | collective-permute-start | bytes 294920 | tf_op jit(solution)/shard_map/ppermute | solution.py:91
  16.0 7.2 %collective-permute-start.5 = (f32[384,128]{1,0:T(8,128)S(1)}, f32[384,128]{1,0:T(8,128)S(1)}, u32[]{:S(2)}, u32[]{:S(2)}) collective-permute-start(f32[384,128]{1,0:T(8,128)S(1)} %get-tuple-element.54), channel_id=1, source_target_pairs={{0,1},{1,2},{2,3},{3,0},{4,5},{5,6},{6,7},{7,4},{8,9},{9,10},{10,1... | collective-permute-start | bytes 589832 | tf_op jit(solution)/shard_map/ppermute | solution.py:91
  17.3 4.8 %collective-permute-start.6 = (f32[192,128]{1,0:T(8,128)S(1)}, f32[192,128]{1,0:T(8,128)S(1)}, u32[]{:S(2)}, u32[]{:S(2)}) collective-permute-start(f32[192,128]{1,0:T(8,128)S(1)} %get-tuple-element.55), channel_id=1, source_target_pairs={{0,1},{1,6},{2,3},{3,0},{4,5},{5,2},{6,7},{7,4},{8,9},{9,14},{10,1... | collective-permute-start | bytes 294920 | tf_op jit(solution)/shard_map/ppermute | solution.py:91
  17.8 5.3 %collective-permute-start.7 = (f32[192,128]{1,0:T(8,128)S(1)}, f32[192,128]{1,0:T(8,128)S(1)}, u32[]{:S(2)}, u32[]{:S(2)}) collective-permute-start(f32[192,128]{1,0:T(8,128)S(1)} %get-tuple-element.56), channel_id=1, source_target_pairs={{0,1},{1,2},{2,3},{3,0},{4,5},{5,10},{6,7},{7,4},{8,9},{9,6},{10,1... | collective-permute-start | bytes 294920 | tf_op jit(solution)/shard_map/ppermute | solution.py:91
  19.9 7.5 %collective-permute-start.19 = (f32[384,128]{1,0:T(8,128)S(1)}, f32[384,128]{1,0:T(8,128)S(1)}, u32[]{:S(2)}, u32[]{:S(2)}) collective-permute-start(f32[384,128]{1,0:T(8,128)S(1)} %get-tuple-element.73), channel_id=1, source_target_pairs={{0,1},{1,2},{2,3},{3,0},{4,5},{5,6},{6,7},{7,4},{8,9},{9,10},{10,1... | collective-permute-start | bytes 589832 | tf_op jit(solution)/shard_map/ppermute | solution.py:91
  21.0 5.3 %collective-permute-start.20 = (f32[192,128]{1,0:T(8,128)S(1)}, f32[192,128]{1,0:T(8,128)S(1)}, u32[]{:S(2)}, u32[]{:S(2)}) collective-permute-start(f32[192,128]{1,0:T(8,128)S(1)} %get-tuple-element.74), channel_id=1, source_target_pairs={{0,1},{1,6},{2,3},{3,0},{4,5},{5,2},{6,7},{7,4},{8,9},{9,14},{10,1... | collective-permute-start | bytes 294920 | tf_op jit(solution)/shard_map/ppermute | solution.py:91
  22.1 5.3 %collective-permute-start.21 = (f32[192,128]{1,0:T(8,128)S(1)}, f32[192,128]{1,0:T(8,128)S(1)}, u32[]{:S(2)}, u32[]{:S(2)}) collective-permute-start(f32[192,128]{1,0:T(8,128)S(1)} %get-tuple-element.75), channel_id=1, source_target_pairs={{0,1},{1,2},{2,3},{3,0},{4,5},{5,10},{6,7},{7,4},{8,9},{9,6},{10,1... | collective-permute-start | bytes 294920 | tf_op jit(solution)/shard_map/ppermute | solution.py:91
  23.2 4.8 %collective-permute-start.8 = (f32[384,128]{1,0:T(8,128)S(1)}, f32[384,128]{1,0:T(8,128)S(1)}, u32[]{:S(2)}, u32[]{:S(2)}) collective-permute-start(f32[384,128]{1,0:T(8,128)S(1)} %get-tuple-element.57), channel_id=1, source_target_pairs={{0,1},{1,0},{2,3},{3,2},{4,5},{5,4},{6,7},{7,6},{8,9},{9,8},{10,11... | collective-permute-start | bytes 589832 | tf_op jit(solution)/shard_map/ppermute | solution.py:91
  23.2 4.7 %collective-permute-start.9 = (f32[192,128]{1,0:T(8,128)S(1)}, f32[192,128]{1,0:T(8,128)S(1)}, u32[]{:S(2)}, u32[]{:S(2)}) collective-permute-start(f32[192,128]{1,0:T(8,128)S(1)} %get-tuple-element.58), channel_id=1, source_target_pairs={{0,1},{1,0},{2,7},{3,2},{4,5},{5,4},{6,3},{7,6},{8,9},{9,8},{10,15... | collective-permute-start | bytes 294920 | tf_op jit(solution)/shard_map/ppermute | solution.py:91
  26.3 1.6 %collective-permute-start.10 = (f32[192,128]{1,0:T(8,128)S(1)}, f32[192,128]{1,0:T(8,128)S(1)}, u32[]{:S(2)}, u32[]{:S(2)}) collective-permute-start(f32[192,128]{1,0:T(8,128)S(1)} %get-tuple-element.59), channel_id=1, source_target_pairs={{0,1},{1,0},{2,3},{3,2},{4,5},{5,4},{6,11},{7,6},{8,9},{9,8},{10,7... | collective-permute-start | bytes 294920 | tf_op jit(solution)/shard_map/ppermute | solution.py:91
  27.4 1.8 %collective-permute-start.22 = (f32[384,128]{1,0:T(8,128)S(1)}, f32[384,128]{1,0:T(8,128)S(1)}, u32[]{:S(2)}, u32[]{:S(2)}) collective-permute-start(f32[384,128]{1,0:T(8,128)S(1)} %get-tuple-element.78), channel_id=1, source_target_pairs={{0,1},{1,0},{2,3},{3,2},{4,5},{5,4},{6,7},{7,6},{8,9},{9,8},{10,11... | collective-permute-start | bytes 589832 | tf_op jit(solution)/shard_map/ppermute | solution.py:91
  27.4 1.6 %collective-permute-start.23 = (f32[192,128]{1,0:T(8,128)S(1)}, f32[192,128]{1,0:T(8,128)S(1)}, u32[]{:S(2)}, u32[]{:S(2)}) collective-permute-start(f32[192,128]{1,0:T(8,128)S(1)} %get-tuple-element.79), channel_id=1, source_target_pairs={{0,1},{1,0},{2,7},{3,2},{4,5},{5,4},{6,3},{7,6},{8,9},{9,8},{10,15... | collective-permute-start | bytes 294920 | tf_op jit(solution)/shard_map/ppermute | solution.py:91
  27.9 1.3 %collective-permute-start.24 = (f32[192,128]{1,0:T(8,128)S(1)}, f32[192,128]{1,0:T(8,128)S(1)}, u32[]{:S(2)}, u32[]{:S(2)}) collective-permute-start(f32[192,128]{1,0:T(8,128)S(1)} %get-tuple-element.80), channel_id=1, source_target_pairs={{0,1},{1,0},{2,3},{3,2},{4,5},{5,4},{6,11},{7,6},{8,9},{9,8},{10,7... | collective-permute-start | bytes 294920 | tf_op jit(solution)/shard_map/ppermute | solution.py:91
  29.2 9.9 %collective-permute-start.25 = (f32[96,128]{1,0:T(8,128)S(1)}, f32[96,128]{1,0:T(8,128)S(1)}, u32[]{:S(2)}, u32[]{:S(2)}) collective-permute-start(f32[96,128]{1,0:T(8,128)S(1)} %get-tuple-element.83), channel_id=1, source_target_pairs={{0,1},{1,0},{2,3},{3,2},{4,5},{5,4},{6,7},{7,6},{8,9},{9,8},{10,11... | collective-permute-start | bytes 147464 | tf_op jit(solution)/shard_map/ppermute | solution.py:91
  29.4 9.8 %collective-permute-start.26 = (f32[96,128]{1,0:T(8,128)S(1)}, f32[96,128]{1,0:T(8,128)S(1)}, u32[]{:S(2)}, u32[]{:S(2)}) collective-permute-start(f32[96,128]{1,0:T(8,128)S(1)} %get-tuple-element.84), channel_id=1, source_target_pairs={{0,2},{1,0},{2,3},{3,1},{4,6},{5,4},{6,7},{7,5},{8,10},{9,8},{10,1... | collective-permute-start | bytes 147464 | tf_op jit(solution)/shard_map/ppermute | solution.py:91
  37.0 3.5 %collective-permute-start.27 = (f32[96,128]{1,0:T(8,128)S(1)}, f32[96,128]{1,0:T(8,128)S(1)}, u32[]{:S(2)}, u32[]{:S(2)}) collective-permute-start(f32[96,128]{1,0:T(8,128)S(1)} %get-tuple-element.85), channel_id=1, source_target_pairs={{0,1},{1,2},{2,3},{3,0},{4,5},{5,6},{6,7},{7,4},{8,9},{9,10},{10,1... | collective-permute-start | bytes 147464 | tf_op jit(solution)/shard_map/ppermute | solution.py:91
  37.0 3.5 %collective-permute-start.11 = (f32[96,128]{1,0:T(8,128)S(1)}, f32[96,128]{1,0:T(8,128)S(1)}, u32[]{:S(2)}, u32[]{:S(2)}) collective-permute-start(f32[96,128]{1,0:T(8,128)S(1)} %get-tuple-element.60), channel_id=1, source_target_pairs={{0,1},{1,0},{2,3},{3,2},{4,5},{5,4},{6,7},{7,6},{8,9},{9,8},{10,11... | collective-permute-start | bytes 147464 | tf_op jit(solution)/shard_map/ppermute | solution.py:91
  37.1 3.8 %collective-permute-start.12 = (f32[96,128]{1,0:T(8,128)S(1)}, f32[96,128]{1,0:T(8,128)S(1)}, u32[]{:S(2)}, u32[]{:S(2)}) collective-permute-start(f32[96,128]{1,0:T(8,128)S(1)} %get-tuple-element.61), channel_id=1, source_target_pairs={{0,2},{1,0},{2,3},{3,1},{4,6},{5,4},{6,7},{7,5},{8,10},{9,8},{10,1... | collective-permute-start | bytes 147464 | tf_op jit(solution)/shard_map/ppermute | solution.py:91
  39.1 3.5 %collective-permute-start.13 = (f32[96,128]{1,0:T(8,128)S(1)}, f32[96,128]{1,0:T(8,128)S(1)}, u32[]{:S(2)}, u32[]{:S(2)}) collective-permute-start(f32[96,128]{1,0:T(8,128)S(1)} %get-tuple-element.62), channel_id=1, source_target_pairs={{0,1},{1,2},{2,3},{3,0},{4,5},{5,6},{6,7},{7,4},{8,9},{9,10},{10,1... | collective-permute-start | bytes 147464 | tf_op jit(solution)/shard_map/ppermute | solution.py:91
where the time goes:
time: 43.5 us; the launch traced here: 43.4 us
  starting transfers between devices  24.7 us (57%)
  waiting for transfers between devices  11 us (25%)
  Pallas kernels  5.15 us (12%)
  local copies, waits for them, and re-layouts  1.68 us (4%)
  other arithmetic  0.71 us (2%)
    ppermute x28, starting transfers between devices, send(): return lax.ppermute(value, ('tiles', 'section'), pairs)  24.7 us
    ppermute x28, waiting for transfers between devices, send(): return lax.ppermute(value, ('tiles', 'section'), pairs)  11 us
    pallas_call x8, Pallas kernels, frame_step(): pl.pallas_call(kernel, out_shape=tuple(out_shape), in_specs=[VMEM] * len(...  2.21 us
    pallas_call x1, Pallas kernels, prepare(): pl.pallas_call(kernel, out_shape=(held(shape, jnp.bfloat16), held(shape,...  2.19 us
    unnamed x6, local copies, waits for them, and re-layouts  1.68 us
  transfers between devices with their start and end apart: 28, of which 10 were waited for; matrix products, arithmetic and copies ran while one was open for 0% of the time, Pallas kernels for 12%

commit v1 on v0

--- a/solution.py
+++ b/solution.py
@@ -9,7 +9,7 @@
 EPSILON = 1e-06
 GRANT = pltpu.CompilerParams(vmem_limit_bytes=12 * 2**20)
 VMEM = pl.BlockSpec(memory_space=pltpu.VMEM)
-ANY = pl.BlockSpec(memory_space=pl.ANY)
+HBM = pl.BlockSpec(memory_space=pltpu.HBM)
 
 
 def partner_a(tile, tiles):
@@ -106,7 +106,9 @@
     first = 9 * (3 - steps)
     groups = [(k, min(2, 9 - k)) for k in range(0, 9, 2)]
 
-    def kernel(weight_ref, gain_ref, high, low, gains, staged, sems):
+    def kernel(weight_ref, gain_ref, high, low, gains, staged, row, sems, gain_sem):
+        gain_copy = pltpu.make_async_copy(gain_ref, row, gain_sem)
+        gain_copy.start()
         copies = {}
         for a in reversed(range(steps)):
             for n, (k, size) in enumerate(groups):
@@ -117,10 +119,11 @@
                     sems.at[a, n],
                 )
                 copies[a, k].start()
+        gain_copy.wait()
         square = (channels, channels)
         lane = lax.broadcasted_iota(jnp.int32, square, 1)
         sublane = lax.broadcasted_iota(jnp.int32, square, 0)
-        spread = jnp.broadcast_to(gain_ref[...], square)
+        spread = jnp.broadcast_to(row[...], square)
         column = jnp.sum(jnp.where(lane == sublane, spread, 0.0), axis=1, keepdims=True)
         gains[...] = jnp.broadcast_to(column, (channels, width))
         for a in reversed(range(steps)):
@@ -144,34 +147,39 @@
             held(shape, jnp.bfloat16),
             held((channels, width)),
         ),
-        in_specs=[pl.BlockSpec(memory_space=pltpu.HBM), VMEM],
+        in_specs=[HBM, HBM],
         out_specs=(VMEM, VMEM, VMEM),
         scratch_shapes=[
             pltpu.VMEM((9 * steps, channels, channels), jnp.float32),
+            pltpu.VMEM(gain.shape, jnp.float32),
             pltpu.SemaphoreType.DMA((steps, len(groups))),
+            pltpu.SemaphoreType.DMA,
         ],
         compiler_params=GRANT,
         name="prepare",
-    )(pltpu.with_memory_space_constraint(weight, pltpu.HBM), gain)
+    )(
+        pltpu.with_memory_space_constraint(weight, pltpu.HBM),
+        pltpu.with_memory_space_constraint(gain, pltpu.HBM),
+    )
 
 
 def edges(latents, rows):
     frames, lines, width = latents.shape
     channels = lines // rows
 
-    def kernel(ref, *outs):
+    def kernel(ref, out_a, out_b):
         even = lax.rem(lax.axis_index("tiles"), 2) == 0
         for f in range(frames):
             top = ref[f, pl.ds(0, channels, stride=rows), :]
             bottom = ref[f, pl.ds(rows - 1, channels, stride=rows), :]
-            outs[2 * f][...] = jnp.where(even, bottom, top)
-            outs[2 * f + 1][...] = jnp.where(even, top, bottom)
+            out_a[f] = jnp.where(even, bottom, top)
+            out_b[f] = jnp.where(even, top, bottom)
 
     return pl.pallas_call(
         kernel,
-        out_shape=tuple([held((channels, width))] * (2 * frames)),
+        out_shape=tuple([held((frames, channels, width))] * 2),
         in_specs=[VMEM],
-        out_specs=tuple([VMEM] * (2 * frames)),
+        out_specs=(VMEM, VMEM),
         compiler_params=GRANT,
         name="edges",
     )(latents)
@@ -201,7 +209,7 @@
 
 
 def frame_step(layer, tiles, sections, main, frame, near_a, near_b, gain, weights, partial, keep):
-    channels, width = near_a.shape
+    channels, width = near_a.shape[-2:]
     lines = main.shape[-2]
     rows = lines // channels
     steps, _, depth = weights[0].shape
@@ -221,7 +229,9 @@
         @pl.when(lax.axis_index("section") == layer)
         def _():
             gains = gain_ref[...]
-            near_one, near_two = a_ref[...], b_ref[...]
+            near_one, near_two = (
+                ref[...] if frame is None else ref[frame] for ref in (a_ref, b_ref)
+            )
             above = jnp.where(even, near_two, near_one)
             below = jnp.where(even, near_one, near_two)
             above = jnp.where(tile == 0, 0.0, above)
@@ -272,7 +282,8 @@
     if last:
         out_shape = [held((share, width))] * sections
     else:
-        out_shape = [held((lines, width)), held(near_a.shape), held(near_a.shape)]
+        edge = held((channels, width))
+        out_shape = [held((lines, width)), edge, edge]
     patch = held((depth, rows * width), jnp.bfloat16)
     scratch = []
     if keep:
@@ -342,13 +353,10 @@
     of_b = lambda t: partner_b(t, tiles)
 
     flat = latents.reshape(frames, channels * rows, width)
-    edge = edges(flat, rows)
-    edge_a, edge_b = edge[0::2], edge[1::2]
+    edge_a, edge_b = edges(flat, rows)
     rim_a, rim_b = (rim_pairs(tiles, sections, of) for of in (of_a, of_b))
-    near_a, near_b = [], []
-    for f in range(frames):
-        near_a.append(send(edge_a[f], rim_a))
-        near_b.append(send(edge_b[f], rim_b))
+    near_a = [send(edge_a, rim_a)] * frames
+    near_b = [send(edge_b, rim_b)] * frames
     *weights, gains = prepare(conv_weight[0], gain, steps, depth, width)
     main = [flat] * frames
 

time: 43.5 us -> 42.2 us (0.970)
  starting transfers between devices: 24.7 us -> 21.4 us
  waiting for transfers between devices: 11 us -> 13 us
  Pallas kernels: 5.15 us -> 5.88 us
  local copies, waits for them, and re-layouts: 1.68 us -> 1 us
    ppermute x28 -> x26, starting transfers between devices: 24.7 us -> 21.4 us  [send(): return lax.ppermute(value, ('tiles', 'section'), pairs)]
    ppermute x28 -> x26, waiting for transfers between devices: 11 us -> 13 us  [send(): return lax.ppermute(value, ('tiles', 'section'), pairs)]
    pallas_call x1, Pallas kernels: 2.19 us -> 2.93 us  [prepare(): pl.pallas_call(kernel, out_shape=(held(shape, jnp.bfloat16), held(shape,...]
    unnamed x6 -> x2, local copies, waits for them, and re-layouts: 1.68 us -> 1 us
  transfers between devices with their start and end apart: 28 -> 26, of which waited for: 10 -> 11; matrix products, arithmetic and copies ran while one was open for 0% -> 0% of each run, Pallas kernels for 12% -> 11%
where the time goes in v1:
time: 42.2 us; the launch traced here: 42 us
  starting transfers between devices  21.4 us (51%)
  waiting for transfers between devices  13 us (31%)
  Pallas kernels  5.88 us (14%)
  local copies, waits for them, and re-layouts  1 us (2%)
  other arithmetic  0.71 us (2%)
    ppermute x26, starting transfers between devices, send(): return lax.ppermute(value, ('tiles', 'section'), pairs)  21.4 us
    ppermute x26, waiting for transfers between devices, send(): return lax.ppermute(value, ('tiles', 'section'), pairs)  13 us
    pallas_call x1, Pallas kernels, prepare(): pl.pallas_call(kernel, out_shape=(held(shape, jnp.bfloat16), held(shape,...  2.93 us
    pallas_call x8, Pallas kernels, frame_step(): pl.pallas_call(kernel, out_shape=tuple(out_shape), in_specs=[VMEM] * len(...  2.2 us
    unnamed x2, local copies, waits for them, and re-layouts  1 us
  transfers between devices with their start and end apart: 26, of which 11 were waited for; matrix products, arithmetic and copies ran while one was open for 0% of the time, Pallas kernels for 11%

profile of v1, /device:TPU:0, one launch (start us, length us, event | category | flops | bytes accessed | tf_op | source)
XLA Modules:
  0.0 42.0 jit_solution(5358315743211985078)
XLA Ops:
  0.0 1.0 %copy-done = f32[2,192,2,128]{3,2,1,0:T(2,128)S(1)} copy-done((f32[2,192,2,128]{3,2,1,0:T(2,128)S(1)}, f32[2,192,2,128]{3,2,1,0:T(2,128)}, u32[]{:S(2)}) %copy-start) | copy-done | bytes 393240
  1.0 3.1 %collective-permute-start = (f32[2,192,128]{2,1,0:T(8,128)S(1)}, f32[2,192,128]{2,1,0:T(8,128)S(1)}, u32[]{:S(2)}, u32[]{:S(2)}) collective-permute-start(f32[2,192,128]{2,1,0:T(8,128)S(1)} %get-tuple-element.44), channel_id=1, source_target_pairs={{0,4},{1,2},{2,3},{3,1},{4,0},{5,6},{6,7},{7,5},{8,12},{9,10},{10,... | collective-permute-start | bytes 589832 | tf_op jit(solution)/shard_map/ppermute | solution.py:91
  4.2 2.9 %prepare.1 = (bf16[2,192,1792]{2,1,0:T(8,128)(2,1)S(1)}, bf16[2,192,1792]{2,1,0:T(8,128)(2,1)S(1)}, f32[192,128]{1,0:T(8,128)S(1)}) custom-call(f32[27,192,192]{2,1,0:T(8,128)} %bitcast.7, f32[1,192]{1,0:T(1,128)} %gain_ref.1), custom_call_target="tpu_custom_call" | custom-call | tf_op jit(solution)/shard_map/prepare/pallas_call | solution.py:143
  7.1 0.7 %collective-permute-done.refs_1_ = f32[2,192,128]{2,1,0:T(8,128)S(1)} collective-permute-done((f32[2,192,128]{2,1,0:T(8,128)S(1)}, f32[2,192,128]{2,1,0:T(8,128)S(1)}, u32[]{:S(2)}, u32[]{:S(2)}) %collective-permute-start) | collective-permute-done | bytes 196640 | tf_op jit(solution)/shard_map/ppermute | solution.py:91
  7.8 1.1 %frame_step.8 = (f32[384,128]{1,0:T(8,128)S(1)}, f32[192,128]{1,0:T(8,128)S(1)}, f32[192,128]{1,0:T(8,128)S(1)}, bf16[1792,256]{1,0:T(8,128)(2,1)S(1)}, bf16[1792,256]{1,0:T(8,128)(2,1)S(1)}) custom-call(f32[2,384,128]{2,1,0:T(8,128)S(1)} %bitcast.5, f32[2,192,128]{2,1,0:T(8,128)S(1)} %collective-permute-done.refs_1_, ...), custom_call_target="tpu_custom_call" | custom-call | flops 528482304 | bytes 1048576 | tf_op jit(solution)/shard_map/frame_step/pallas_call | solution.py:293
  8.9 0.1 collective-permute-start.2
  9.0 3.3 %collective-permute-start.3 = (f32[192,128]{1,0:T(8,128)S(1)}, f32[192,128]{1,0:T(8,128)S(1)}, u32[]{:S(2)}, u32[]{:S(2)}) collective-permute-start(f32[192,128]{1,0:T(8,128)S(1)} %get-tuple-element.50), channel_id=1, source_target_pairs={{0,5},{1,0},{2,3},{3,2},{4,1},{5,4},{6,7},{7,6},{8,13},{9,8},{10,1... | collective-permute-start | bytes 294920 | tf_op jit(solution)/shard_map/ppermute | solution.py:91
  12.2 0.7 %earlier_frames.4.refs_6_ = f32[192,256]{1,0:T(8,128)S(1)} custom-call(bf16[2,192,1792]{2,1,0:T(8,128)(2,1)S(1)} %get-tuple-element.47.refs_4_.high_ref, bf16[2,192,1792]{2,1,0:T(8,128)(2,1)S(1)} %get-tuple-element.48.refs_5_.low_ref, bf16[1792,256]{1,0:T(8,128)(2,1)S(1)} %get-tuple-element.62.refs_0_, bf16[1792,256]{1,0:T(8,128)(2,1)S(1)} %get-tuple-element.63.refs_1_), custom_call_target="tpu_custom_call" | custom-call | flops 528482304 | bytes 1048576 | tf_op jit(solution)/shard_map/earlier_frames/pallas_call | solution.py:331
  12.9 1.1 %frame_step.12 = (f32[384,128]{1,0:T(8,128)S(1)}, f32[192,128]{1,0:T(8,128)S(1)}, f32[192,128]{1,0:T(8,128)S(1)}) custom-call(f32[2,384,128]{2,1,0:T(8,128)S(1)} %bitcast.6, f32[2,192,128]{2,1,0:T(8,128)S(1)} %collective-permute-done.refs_1_, f32[2,192,128]{2,1,0:T(8,128)S(1)} %collective-permute-done.1.refs_2_, f32[192,128]{1,0:T(8,128)S(1)} %get-tuple-element.46.refs_3_, ...), custom_call_target="tpu_custom_call" | custom-call | flops 528482304 | bytes 1048576 | tf_op jit(solution)/shard_map/frame_step/pallas_call | solution.py:293
  14.0 0.1 collective-permute-start.14
  14.1 2.2 %collective-permute-start.15 = (f32[192,128]{1,0:T(8,128)S(1)}, f32[192,128]{1,0:T(8,128)S(1)}, u32[]{:S(2)}, u32[]{:S(2)}) collective-permute-start(f32[192,128]{1,0:T(8,128)S(1)} %get-tuple-element.65), channel_id=1, source_target_pairs={{0,5},{1,0},{2,3},{3,2},{4,1},{5,4},{6,7},{7,6},{8,13},{9,8},{10,1... | collective-permute-start | bytes 294920 | tf_op jit(solution)/shard_map/ppermute | solution.py:91
  16.4 1.6 %collective-permute-start.5 = (f32[384,128]{1,0:T(8,128)S(1)}, f32[384,128]{1,0:T(8,128)S(1)}, u32[]{:S(2)}, u32[]{:S(2)}) collective-permute-start(f32[384,128]{1,0:T(8,128)S(1)} %get-tuple-element.52), channel_id=1, source_target_pairs={{0,1},{1,2},{2,3},{3,0},{4,5},{5,6},{6,7},{7,4},{8,9},{9,10},{10,1... | collective-permute-start | bytes 589832 | tf_op jit(solution)/shard_map/ppermute | solution.py:91
  18.0 0.5 %collective-permute-done.15.refs_1_ = f32[192,128]{1,0:T(8,128)S(1)} collective-permute-done((f32[192,128]{1,0:T(8,128)S(1)}, f32[192,128]{1,0:T(8,128)S(1)}, u32[]{:S(2)}, u32[]{:S(2)}) %collective-permute-start.15) | collective-permute-done | bytes 98336 | tf_op jit(solution)/shard_map/ppermute | solution.py:91
  18.5 0.3 collective-permute-start.7
  18.8 1.2 %collective-permute-start.17 = (f32[384,128]{1,0:T(8,128)S(1)}, f32[384,128]{1,0:T(8,128)S(1)}, u32[]{:S(2)}, u32[]{:S(2)}) collective-permute-start(f32[384,128]{1,0:T(8,128)S(1)} %get-tuple-element.69), channel_id=1, source_target_pairs={{0,1},{1,2},{2,3},{3,0},{4,5},{5,6},{6,7},{7,4},{8,9},{9,10},{10,1... | collective-permute-start | bytes 589832 | tf_op jit(solution)/shard_map/ppermute | solution.py:91
  20.0 0.2 collective-permute-start.18
  20.2 2.3 %collective-permute-done.6.refs_1_ = f32[192,128]{1,0:T(8,128)S(1)} collective-permute-done((f32[192,128]{1,0:T(8,128)S(1)}, f32[192,128]{1,0:T(8,128)S(1)}, u32[]{:S(2)}, u32[]{:S(2)}) %collective-permute-start.6) | collective-permute-done | bytes 98336 | tf_op jit(solution)/shard_map/ppermute | solution.py:91
  22.6 1.1 %collective-permute-done.7.refs_2_ = f32[192,128]{1,0:T(8,128)S(1)} collective-permute-done((f32[192,128]{1,0:T(8,128)S(1)}, f32[192,128]{1,0:T(8,128)S(1)}, u32[]{:S(2)}, u32[]{:S(2)}) %collective-permute-start.7) | collective-permute-done | bytes 98336 | tf_op jit(solution)/shard_map/ppermute | solution.py:91
  23.6 0.5 %collective-permute-start.9 = (f32[192,128]{1,0:T(8,128)S(1)}, f32[192,128]{1,0:T(8,128)S(1)}, u32[]{:S(2)}, u32[]{:S(2)}) collective-permute-start(f32[192,128]{1,0:T(8,128)S(1)} %get-tuple-element.56), channel_id=1, source_target_pairs={{0,1},{1,0},{2,7},{3,2},{4,5},{5,4},{6,3},{7,6},{8,9},{9,8},{10,15... | collective-permute-start | bytes 294920 | tf_op jit(solution)/shard_map/ppermute | solution.py:91
  24.1 2.6 %collective-permute-done.18.refs_1_ = f32[192,128]{1,0:T(8,128)S(1)} collective-permute-done((f32[192,128]{1,0:T(8,128)S(1)}, f32[192,128]{1,0:T(8,128)S(1)}, u32[]{:S(2)}, u32[]{:S(2)}) %collective-permute-start.18) | collective-permute-done | bytes 98336 | tf_op jit(solution)/shard_map/ppermute | solution.py:91
  26.8 1.0 %collective-permute-done.19.refs_2_ = f32[192,128]{1,0:T(8,128)S(1)} collective-permute-done((f32[192,128]{1,0:T(8,128)S(1)}, f32[192,128]{1,0:T(8,128)S(1)}, u32[]{:S(2)}, u32[]{:S(2)}) %collective-permute-start.19) | collective-permute-done | bytes 98336 | tf_op jit(solution)/shard_map/ppermute | solution.py:91
  27.8 0.5 %collective-permute-start.21 = (f32[192,128]{1,0:T(8,128)S(1)}, f32[192,128]{1,0:T(8,128)S(1)}, u32[]{:S(2)}, u32[]{:S(2)}) collective-permute-start(f32[192,128]{1,0:T(8,128)S(1)} %get-tuple-element.75), channel_id=1, source_target_pairs={{0,1},{1,0},{2,7},{3,2},{4,5},{5,4},{6,3},{7,6},{8,9},{9,8},{10,15... | collective-permute-start | bytes 294920 | tf_op jit(solution)/shard_map/ppermute | solution.py:91
  28.4 1.0 %collective-permute-done.21.refs_1_ = f32[192,128]{1,0:T(8,128)S(1)} collective-permute-done((f32[192,128]{1,0:T(8,128)S(1)}, f32[192,128]{1,0:T(8,128)S(1)}, u32[]{:S(2)}, u32[]{:S(2)}) %collective-permute-start.21) | collective-permute-done | bytes 98336 | tf_op jit(solution)/shard_map/ppermute | solution.py:91
  29.4 0.2 collective-permute-done.22.refs_2_
  29.6 0.2 collective-permute-start.23
  29.8 5.9 %collective-permute-start.24 = (f32[96,128]{1,0:T(8,128)S(1)}, f32[96,128]{1,0:T(8,128)S(1)}, u32[]{:S(2)}, u32[]{:S(2)}) collective-permute-start(f32[96,128]{1,0:T(8,128)S(1)} %get-tuple-element.80), channel_id=1, source_target_pairs={{0,2},{1,0},{2,3},{3,1},{4,6},{5,4},{6,7},{7,5},{8,10},{9,8},{10,1... | collective-permute-start | bytes 147464 | tf_op jit(solution)/shard_map/ppermute | solution.py:91
  35.7 0.1 collective-permute-start.11
  35.8 2.0 %collective-permute-start.12 = (f32[96,128]{1,0:T(8,128)S(1)}, f32[96,128]{1,0:T(8,128)S(1)}, u32[]{:S(2)}, u32[]{:S(2)}) collective-permute-start(f32[96,128]{1,0:T(8,128)S(1)} %get-tuple-element.59), channel_id=1, source_target_pairs={{0,2},{1,0},{2,3},{3,1},{4,6},{5,4},{6,7},{7,5},{8,10},{9,8},{10,1... | collective-permute-start | bytes 147464 | tf_op jit(solution)/shard_map/ppermute | solution.py:91
  37.8 1.4 %collective-permute-done.25 = f32[96,128]{1,0:T(8,128)S(1)} collective-permute-done((f32[96,128]{1,0:T(8,128)S(1)}, f32[96,128]{1,0:T(8,128)S(1)}, u32[]{:S(2)}, u32[]{:S(2)}) %collective-permute-start.25) | collective-permute-done | bytes 49184 | tf_op jit(solution)/shard_map/ppermute | solution.py:91
  39.2 0.4 collective-permute-done.12
  39.6 1.8 %collective-permute-done.13 = f32[96,128]{1,0:T(8,128)S(1)} collective-permute-done((f32[96,128]{1,0:T(8,128)S(1)}, f32[96,128]{1,0:T(8,128)S(1)}, u32[]{:S(2)}, u32[]{:S(2)}) %collective-permute-start.13) | collective-permute-done | bytes 49184 | tf_op jit(solution)/shard_map/ppermute | solution.py:91
  41.4 0.7 %pad_maximum_fusion = f32[2,48,2,128]{3,2,1,0:T(2,128)} fusion(f32[1,48,2,128]{3,2,1,0:T(2,128)S(1)} %bitcast.8, f32[1,48,2,128]{3,2,1,0:T(2,128)S(1)} %bitcast.9), kind=kLoop, calls=%fused_computation | loop fusion | flops 24576 | bytes 196608 | tf_op jit(solution)/shard_map/stack | solution.py:397
  (39 shorter events, 0.3 us)
Async XLA Ops:
  0.0 1.0 %copy-start = (f32[2,192,2,128]{3,2,1,0:T(2,128)S(1)}, f32[2,192,2,128]{3,2,1,0:T(2,128)}, u32[]{:S(2)}) copy-start(f32[2,192,2,128]{3,2,1,0:T(2,128)} %param.3) | copy-start | bytes 1179652
  1.0 6.8 %collective-permute-start = (f32[2,192,128]{2,1,0:T(8,128)S(1)}, f32[2,192,128]{2,1,0:T(8,128)S(1)}, u32[]{:S(2)}, u32[]{:S(2)}) collective-permute-start(f32[2,192,128]{2,1,0:T(8,128)S(1)} %get-tuple-element.44), channel_id=1, source_target_pairs={{0,4},{1,2},{2,3},{3,1},{4,0},{5,6},{6,7},{7,5},{8,12},{9,10},{10,... | collective-permute-start | bytes 589832 | tf_op jit(solution)/shard_map/ppermute | solution.py:91
  4.2 3.7 %collective-permute-start.1 = (f32[2,192,128]{2,1,0:T(8,128)S(1)}, f32[2,192,128]{2,1,0:T(8,128)S(1)}, u32[]{:S(2)}, u32[]{:S(2)}) collective-permute-start(f32[2,192,128]{2,1,0:T(8,128)S(1)} %get-tuple-element.45), channel_id=1, source_target_pairs={{0,1},{1,0},{2,3},{3,2},{4,8},{5,6},{6,7},{7,5},{8,4},{9,10},{10,1... | collective-permute-start | bytes 589832 | tf_op jit(solution)/shard_map/ppermute | solution.py:91
  8.9 7.4 %collective-permute-start.2 = (f32[384,128]{1,0:T(8,128)S(1)}, f32[384,128]{1,0:T(8,128)S(1)}, u32[]{:S(2)}, u32[]{:S(2)}) collective-permute-start(f32[384,128]{1,0:T(8,128)S(1)} %get-tuple-element.49), channel_id=1, source_target_pairs={{0,1},{1,0},{2,3},{3,2},{4,5},{5,4},{6,7},{7,6},{8,9},{9,8},{10,11... | collective-permute-start | bytes 589832 | tf_op jit(solution)/shard_map/ppermute | solution.py:91
  9.0 7.3 %collective-permute-start.3 = (f32[192,128]{1,0:T(8,128)S(1)}, f32[192,128]{1,0:T(8,128)S(1)}, u32[]{:S(2)}, u32[]{:S(2)}) collective-permute-start(f32[192,128]{1,0:T(8,128)S(1)} %get-tuple-element.50), channel_id=1, source_target_pairs={{0,5},{1,0},{2,3},{3,2},{4,1},{5,4},{6,7},{7,6},{8,13},{9,8},{10,1... | collective-permute-start | bytes 294920 | tf_op jit(solution)/shard_map/ppermute | solution.py:91
  12.2 4.1 %collective-permute-start.4 = (f32[192,128]{1,0:T(8,128)S(1)}, f32[192,128]{1,0:T(8,128)S(1)}, u32[]{:S(2)}, u32[]{:S(2)}) collective-permute-start(f32[192,128]{1,0:T(8,128)S(1)} %get-tuple-element.51), channel_id=1, source_target_pairs={{0,1},{1,0},{2,3},{3,2},{4,9},{5,4},{6,7},{7,6},{8,5},{9,8},{10,11... | collective-permute-start | bytes 294920 | tf_op jit(solution)/shard_map/ppermute | solution.py:91
  14.0 4.8 %collective-permute-start.14 = (f32[384,128]{1,0:T(8,128)S(1)}, f32[384,128]{1,0:T(8,128)S(1)}, u32[]{:S(2)}, u32[]{:S(2)}) collective-permute-start(f32[384,128]{1,0:T(8,128)S(1)} %get-tuple-element.64), channel_id=1, source_target_pairs={{0,1},{1,0},{2,3},{3,2},{4,5},{5,4},{6,7},{7,6},{8,9},{9,8},{10,11... | collective-permute-start | bytes 589832 | tf_op jit(solution)/shard_map/ppermute | solution.py:91
  14.1 4.4 %collective-permute-start.15 = (f32[192,128]{1,0:T(8,128)S(1)}, f32[192,128]{1,0:T(8,128)S(1)}, u32[]{:S(2)}, u32[]{:S(2)}) collective-permute-start(f32[192,128]{1,0:T(8,128)S(1)} %get-tuple-element.65), channel_id=1, source_target_pairs={{0,5},{1,0},{2,3},{3,2},{4,1},{5,4},{6,7},{7,6},{8,13},{9,8},{10,1... | collective-permute-start | bytes 294920 | tf_op jit(solution)/shard_map/ppermute | solution.py:91
  16.3 2.5 %collective-permute-start.16 = (f32[192,128]{1,0:T(8,128)S(1)}, f32[192,128]{1,0:T(8,128)S(1)}, u32[]{:S(2)}, u32[]{:S(2)}) collective-permute-start(f32[192,128]{1,0:T(8,128)S(1)} %get-tuple-element.66), channel_id=1, source_target_pairs={{0,1},{1,0},{2,3},{3,2},{4,9},{5,4},{6,7},{7,6},{8,5},{9,8},{10,11... | collective-permute-start | bytes 294920 | tf_op jit(solution)/shard_map/ppermute | solution.py:91
  16.4 7.3 %collective-permute-start.5 = (f32[384,128]{1,0:T(8,128)S(1)}, f32[384,128]{1,0:T(8,128)S(1)}, u32[]{:S(2)}, u32[]{:S(2)}) collective-permute-start(f32[384,128]{1,0:T(8,128)S(1)} %get-tuple-element.52), channel_id=1, source_target_pairs={{0,1},{1,2},{2,3},{3,0},{4,5},{5,6},{6,7},{7,4},{8,9},{9,10},{10,1... | collective-permute-start | bytes 589832 | tf_op jit(solution)/shard_map/ppermute | solution.py:91
  18.0 4.6 %collective-permute-start.6 = (f32[192,128]{1,0:T(8,128)S(1)}, f32[192,128]{1,0:T(8,128)S(1)}, u32[]{:S(2)}, u32[]{:S(2)}) collective-permute-start(f32[192,128]{1,0:T(8,128)S(1)} %get-tuple-element.53), channel_id=1, source_target_pairs={{0,1},{1,6},{2,3},{3,0},{4,5},{5,2},{6,7},{7,4},{8,9},{9,14},{10,1... | collective-permute-start | bytes 294920 | tf_op jit(solution)/shard_map/ppermute | solution.py:91
  18.5 5.1 %collective-permute-start.7 = (f32[192,128]{1,0:T(8,128)S(1)}, f32[192,128]{1,0:T(8,128)S(1)}, u32[]{:S(2)}, u32[]{:S(2)}) collective-permute-start(f32[192,128]{1,0:T(8,128)S(1)} %get-tuple-element.54), channel_id=1, source_target_pairs={{0,1},{1,2},{2,3},{3,0},{4,5},{5,10},{6,7},{7,4},{8,9},{9,6},{10,1... | collective-permute-start | bytes 294920 | tf_op jit(solution)/shard_map/ppermute | solution.py:91
  18.8 9.0 %collective-permute-start.17 = (f32[384,128]{1,0:T(8,128)S(1)}, f32[384,128]{1,0:T(8,128)S(1)}, u32[]{:S(2)}, u32[]{:S(2)}) collective-permute-start(f32[384,128]{1,0:T(8,128)S(1)} %get-tuple-element.69), channel_id=1, source_target_pairs={{0,1},{1,2},{2,3},{3,0},{4,5},{5,6},{6,7},{7,4},{8,9},{9,10},{10,1... | collective-permute-start | bytes 589832 | tf_op jit(solution)/shard_map/ppermute | solution.py:91
  20.0 6.7 %collective-permute-start.18 = (f32[192,128]{1,0:T(8,128)S(1)}, f32[192,128]{1,0:T(8,128)S(1)}, u32[]{:S(2)}, u32[]{:S(2)}) collective-permute-start(f32[192,128]{1,0:T(8,128)S(1)} %get-tuple-element.70), channel_id=1, source_target_pairs={{0,1},{1,6},{2,3},{3,0},{4,5},{5,2},{6,7},{7,4},{8,9},{9,14},{10,1... | collective-permute-start | bytes 294920 | tf_op jit(solution)/shard_map/ppermute | solution.py:91
  22.6 5.3 %collective-permute-start.19 = (f32[192,128]{1,0:T(8,128)S(1)}, f32[192,128]{1,0:T(8,128)S(1)}, u32[]{:S(2)}, u32[]{:S(2)}) collective-permute-start(f32[192,128]{1,0:T(8,128)S(1)} %get-tuple-element.71), channel_id=1, source_target_pairs={{0,1},{1,2},{2,3},{3,0},{4,5},{5,10},{6,7},{7,4},{8,9},{9,6},{10,1... | collective-permute-start | bytes 294920 | tf_op jit(solution)/shard_map/ppermute | solution.py:91
  23.6 4.8 %collective-permute-start.8 = (f32[384,128]{1,0:T(8,128)S(1)}, f32[384,128]{1,0:T(8,128)S(1)}, u32[]{:S(2)}, u32[]{:S(2)}) collective-permute-start(f32[384,128]{1,0:T(8,128)S(1)} %get-tuple-element.55), channel_id=1, source_target_pairs={{0,1},{1,0},{2,3},{3,2},{4,5},{5,4},{6,7},{7,6},{8,9},{9,8},{10,11... | collective-permute-start | bytes 589832 | tf_op jit(solution)/shard_map/ppermute | solution.py:91
  23.6 4.7 %collective-permute-start.9 = (f32[192,128]{1,0:T(8,128)S(1)}, f32[192,128]{1,0:T(8,128)S(1)}, u32[]{:S(2)}, u32[]{:S(2)}) collective-permute-start(f32[192,128]{1,0:T(8,128)S(1)} %get-tuple-element.56), channel_id=1, source_target_pairs={{0,1},{1,0},{2,7},{3,2},{4,5},{5,4},{6,3},{7,6},{8,9},{9,8},{10,15... | collective-permute-start | bytes 294920 | tf_op jit(solution)/shard_map/ppermute | solution.py:91
  26.8 1.6 %collective-permute-start.10 = (f32[192,128]{1,0:T(8,128)S(1)}, f32[192,128]{1,0:T(8,128)S(1)}, u32[]{:S(2)}, u32[]{:S(2)}) collective-permute-start(f32[192,128]{1,0:T(8,128)S(1)} %get-tuple-element.57), channel_id=1, source_target_pairs={{0,1},{1,0},{2,3},{3,2},{4,5},{5,4},{6,11},{7,6},{8,9},{9,8},{10,7... | collective-permute-start | bytes 294920 | tf_op jit(solution)/shard_map/ppermute | solution.py:91
  27.8 1.8 %collective-permute-start.20 = (f32[384,128]{1,0:T(8,128)S(1)}, f32[384,128]{1,0:T(8,128)S(1)}, u32[]{:S(2)}, u32[]{:S(2)}) collective-permute-start(f32[384,128]{1,0:T(8,128)S(1)} %get-tuple-element.74), channel_id=1, source_target_pairs={{0,1},{1,0},{2,3},{3,2},{4,5},{5,4},{6,7},{7,6},{8,9},{9,8},{10,11... | collective-permute-start | bytes 589832 | tf_op jit(solution)/shard_map/ppermute | solution.py:91
  27.8 1.6 %collective-permute-start.21 = (f32[192,128]{1,0:T(8,128)S(1)}, f32[192,128]{1,0:T(8,128)S(1)}, u32[]{:S(2)}, u32[]{:S(2)}) collective-permute-start(f32[192,128]{1,0:T(8,128)S(1)} %get-tuple-element.75), channel_id=1, source_target_pairs={{0,1},{1,0},{2,7},{3,2},{4,5},{5,4},{6,3},{7,6},{8,9},{9,8},{10,15... | collective-permute-start | bytes 294920 | tf_op jit(solution)/shard_map/ppermute | solution.py:91
  28.3 1.3 %collective-permute-start.22 = (f32[192,128]{1,0:T(8,128)S(1)}, f32[192,128]{1,0:T(8,128)S(1)}, u32[]{:S(2)}, u32[]{:S(2)}) collective-permute-start(f32[192,128]{1,0:T(8,128)S(1)} %get-tuple-element.76), channel_id=1, source_target_pairs={{0,1},{1,0},{2,3},{3,2},{4,5},{5,4},{6,11},{7,6},{8,9},{9,8},{10,7... | collective-permute-start | bytes 294920 | tf_op jit(solution)/shard_map/ppermute | solution.py:91
  29.6 8.2 %collective-permute-start.23 = (f32[96,128]{1,0:T(8,128)S(1)}, f32[96,128]{1,0:T(8,128)S(1)}, u32[]{:S(2)}, u32[]{:S(2)}) collective-permute-start(f32[96,128]{1,0:T(8,128)S(1)} %get-tuple-element.79), channel_id=1, source_target_pairs={{0,1},{1,0},{2,3},{3,2},{4,5},{5,4},{6,7},{7,6},{8,9},{9,8},{10,11... | collective-permute-start | bytes 147464 | tf_op jit(solution)/shard_map/ppermute | solution.py:91
  29.8 8.0 %collective-permute-start.24 = (f32[96,128]{1,0:T(8,128)S(1)}, f32[96,128]{1,0:T(8,128)S(1)}, u32[]{:S(2)}, u32[]{:S(2)}) collective-permute-start(f32[96,128]{1,0:T(8,128)S(1)} %get-tuple-element.80), channel_id=1, source_target_pairs={{0,2},{1,0},{2,3},{3,1},{4,6},{5,4},{6,7},{7,5},{8,10},{9,8},{10,1... | collective-permute-start | bytes 147464 | tf_op jit(solution)/shard_map/ppermute | solution.py:91
  35.7 3.5 %collective-permute-start.25 = (f32[96,128]{1,0:T(8,128)S(1)}, f32[96,128]{1,0:T(8,128)S(1)}, u32[]{:S(2)}, u32[]{:S(2)}) collective-permute-start(f32[96,128]{1,0:T(8,128)S(1)} %get-tuple-element.81), channel_id=1, source_target_pairs={{0,1},{1,2},{2,3},{3,0},{4,5},{5,6},{6,7},{7,4},{8,9},{9,10},{10,1... | collective-permute-start | bytes 147464 | tf_op jit(solution)/shard_map/ppermute | solution.py:91
  35.7 3.5 %collective-permute-start.11 = (f32[96,128]{1,0:T(8,128)S(1)}, f32[96,128]{1,0:T(8,128)S(1)}, u32[]{:S(2)}, u32[]{:S(2)}) collective-permute-start(f32[96,128]{1,0:T(8,128)S(1)} %get-tuple-element.58), channel_id=1, source_target_pairs={{0,1},{1,0},{2,3},{3,2},{4,5},{5,4},{6,7},{7,6},{8,9},{9,8},{10,11... | collective-permute-start | bytes 147464 | tf_op jit(solution)/shard_map/ppermute | solution.py:91
  35.8 3.8 %collective-permute-start.12 = (f32[96,128]{1,0:T(8,128)S(1)}, f32[96,128]{1,0:T(8,128)S(1)}, u32[]{:S(2)}, u32[]{:S(2)}) collective-permute-start(f32[96,128]{1,0:T(8,128)S(1)} %get-tuple-element.59), channel_id=1, source_target_pairs={{0,2},{1,0},{2,3},{3,1},{4,6},{5,4},{6,7},{7,5},{8,10},{9,8},{10,1... | collective-permute-start | bytes 147464 | tf_op jit(solution)/shard_map/ppermute | solution.py:91
  37.8 3.5 %collective-permute-start.13 = (f32[96,128]{1,0:T(8,128)S(1)}, f32[96,128]{1,0:T(8,128)S(1)}, u32[]{:S(2)}, u32[]{:S(2)}) collective-permute-start(f32[96,128]{1,0:T(8,128)S(1)} %get-tuple-element.60), channel_id=1, source_target_pairs={{0,1},{1,2},{2,3},{3,0},{4,5},{5,6},{6,7},{7,4},{8,9},{9,10},{10,1... | collective-permute-start | bytes 147464 | tf_op jit(solution)/shard_map/ppermute | solution.py:91

commit v2 on v1

--- a/solution.py
+++ b/solution.py
@@ -42,53 +42,66 @@
     return where
 
 
-def hop_pairs(layer, tiles, sections, tile_of):
-    hop = section_hop(layer, sections)
+def all_pairs(shape, goal):
+    groups, tiles, sections = shape
     pairs = []
-    for t in range(tiles):
-        for s in range(sections):
-            goal = tile_of(t) if s == layer else t
-            pairs.append((t * sections + s, goal * sections + hop[s]))
+    for g in range(groups):
+        for t in range(tiles):
+            for s in range(sections):
+                to_g, to_t, to_s = goal(g, t, s)
+                pairs.append(
+                    ((g * tiles + t) * sections + s, (to_g * tiles + to_t) * sections + to_s)
+                )
     return pairs
 
 
-def rim_pairs(tiles, sections, tile_of):
-    pairs = []
-    for t in range(tiles):
-        where = {}
-        if tile_of(t) == t:
-            for s in range(sections):
-                where[s] = s ^ 1 if (s ^ 1) < sections else s
-        else:
-            idle_cycle(where, list(range(1, sections)))
-        for s in range(sections):
-            if s == 0 and tile_of(t) != t:
-                pairs.append((t * sections, tile_of(t) * sections))
-            else:
-                pairs.append((t * sections + s, t * sections + where[s]))
-    return pairs
-
-
-def share_pairs(target, tiles, sections):
+def other_group(g, groups):
+    return g ^ 1 if (g ^ 1) < groups else g
+
+
+def hop_pairs(layer, shape, tile_of):
+    hop = section_hop(layer, shape[2])
+    return all_pairs(
+        shape, lambda g, t, s: (g, tile_of(t) if s == layer else t, hop[s])
+    )
+
+
+def rim_pairs(shape, tile_of):
+    groups, _, sections = shape
+
+    def goal(g, t, s):
+        if tile_of(t) == t and sections % 2 == 0:
+            return g, t, s ^ 1
+        if s == 0:
+            return g, tile_of(t), s
+        if s == 1 or s ^ 1 >= sections:
+            return other_group(g, groups), t, s
+        return g, t, s ^ 1
+
+    return all_pairs(shape, goal)
+
+
+def share_pairs(target, shape):
+    groups, _, sections = shape
     last = sections - 1
     where = {}
-    if target == last - 1 or (target ^ 1) >= last - 1:
+    if target == last - 1 or target == 0:
         idle_cycle(where, [last, target])
     else:
-        idle_cycle(where, [last, target, target ^ 1, last - 1])
-    taken = set(where)
-    for s in range(sections):
-        if s not in taken:
-            where[s] = s ^ 1 if (s ^ 1) not in taken and (s ^ 1) < sections else s
-    return [
-        (t * sections + s, t * sections + where[s])
-        for t in range(tiles)
-        for s in range(sections)
-    ]
+        idle_cycle(where, [last, target, last - 1])
+
+    def goal(g, t, s):
+        if s in where:
+            return g, t, where[s]
+        if target == last - 1 and s ^ 1 < last - 1:
+            return g, t, s ^ 1
+        return other_group(g, groups), t, s
+
+    return all_pairs(shape, goal)
 
 
 def send(value, pairs):
-    return lax.ppermute(value, ("tiles", "section"), pairs)
+    return lax.ppermute(value, ("groups", "tiles", "section"), pairs)
 
 
 def split(values):
@@ -119,13 +132,6 @@
                     sems.at[a, n],
                 )
                 copies[a, k].start()
-        gain_copy.wait()
-        square = (channels, channels)
-        lane = lax.broadcasted_iota(jnp.int32, square, 1)
-        sublane = lax.broadcasted_iota(jnp.int32, square, 0)
-        spread = jnp.broadcast_to(row[...], square)
-        column = jnp.sum(jnp.where(lane == sublane, spread, 0.0), axis=1, keepdims=True)
-        gains[...] = jnp.broadcast_to(column, (channels, width))
         for a in reversed(range(steps)):
             for k, size in groups:
                 copies[a, k].wait()
@@ -138,6 +144,13 @@
                 upper, lower = split(jnp.concatenate(parts, axis=1))
                 high[a, :, k * channels : k * channels + span] = upper
                 low[a, :, k * channels : k * channels + span] = lower
+        gain_copy.wait()
+        square = (channels, channels)
+        lane = lax.broadcasted_iota(jnp.int32, square, 1)
+        sublane = lax.broadcasted_iota(jnp.int32, square, 0)
+        spread = jnp.broadcast_to(row[...], square)
+        column = jnp.sum(jnp.where(lane == sublane, spread, 0.0), axis=1, keepdims=True)
+        gains[...] = jnp.broadcast_to(column, (channels, width))
 
     shape = (steps, channels, depth)
     return pl.pallas_call(
@@ -346,7 +359,7 @@
 def local(latents, conv_weight, gain):
     frames, channels, rows, width = latents.shape
     tiles, sections = lax.axis_size("tiles"), lax.axis_size("section")
-    section = lax.axis_index("section")
+    shape = (lax.axis_size("groups"), tiles, sections)
     depth = -(-9 * channels // 256) * 256
     steps = min(frames, 3)
     of_a = lambda t: partner_a(t, tiles)
@@ -354,7 +367,7 @@
 
     flat = latents.reshape(frames, channels * rows, width)
     edge_a, edge_b = edges(flat, rows)
-    rim_a, rim_b = (rim_pairs(tiles, sections, of) for of in (of_a, of_b))
+    rim_a, rim_b = (rim_pairs(shape, of) for of in (of_a, of_b))
     near_a = [send(edge_a, rim_a)] * frames
     near_b = [send(edge_b, rim_b)] * frames
     *weights, gains = prepare(conv_weight[0], gain, steps, depth, width)
@@ -362,9 +375,9 @@
 
     for layer in range(sections):
         if layer > 0:
-            straight = hop_pairs(layer - 1, tiles, sections, lambda t: t)
-            cross_a = hop_pairs(layer - 1, tiles, sections, of_a)
-            cross_b = hop_pairs(layer - 1, tiles, sections, of_b)
+            straight = hop_pairs(layer - 1, shape, lambda t: t)
+            cross_a = hop_pairs(layer - 1, shape, of_a)
+            cross_b = hop_pairs(layer - 1, shape, of_b)
             main = [send(main[f], straight) for f in range(frames)]
             near_a = [send(edge_a[f], cross_a) for f in range(frames)]
             near_b = [send(edge_b[f], cross_b) for f in range(frames)]
@@ -386,15 +399,37 @@
             edge_b.append(done[2])
         main = next_main
 
-    outs = []
+    parts = []
     for f in range(frames):
-        own = main[f][sections - 1]
         for target in range(sections - 1):
-            pairs = share_pairs(target, tiles, sections)
-            got = send(main[f][target], pairs)
-            own = jnp.where(section == target, got, own)
-        outs.append(own)
-    return jnp.stack(outs).reshape(frames, channels // sections, rows, width)
+            pairs = share_pairs(target, shape)
+            parts.append(send(main[f][target], pairs))
+        parts.append(main[f][sections - 1])
+    return assemble(parts, frames, sections).reshape(
+        frames, channels // sections, rows, width
+    )
+
+
+def assemble(parts, frames, sections):
+    lines, width = parts[0].shape
+
+    def kernel(*refs):
+        out = refs[-1]
+        for s in range(sections):
+
+            @pl.when(lax.axis_index("section") == s)
+            def _():
+                for f in range(frames):
+                    out[f] = refs[f * sections + s][...]
+
+    return pl.pallas_call(
+        kernel,
+        out_shape=jax.ShapeDtypeStruct((frames, lines, width), jnp.float32),
+        in_specs=[VMEM] * len(parts),
+        out_specs=VMEM,
+        compiler_params=GRANT,
+        name="assemble",
+    )(*parts)
 
 
 def solution(mesh):

time: 42.2 us -> 40.2 us (0.953)
  waiting for transfers between devices: 13 us -> 11.5 us
  other arithmetic: 0.71 us -> 0 us
    ppermute x26, waiting for transfers between devices: 13 us -> 11.5 us  [send(): return lax.ppermute(value, ('groups', 'tiles', 'section'), pairs)]
    another operation x1 -> x0, other arithmetic: 0.69 us -> none  [local(): return jnp.stack(outs).reshape(frames, channels // sections, rows, width)]
    pallas_call x1, Pallas kernels: 2.93 us -> 2.25 us  [prepare(): pl.pallas_call(kernel, out_shape=(held(shape, jnp.bfloat16), held(shape,...]
    pallas_call x0 -> x1, Pallas kernels: none -> 0.66 us  [assemble(): pl.pallas_call(kernel, out_shape=jax.ShapeDtypeStruct((frames, lines, wid...]
  transfers between devices with their start and end apart: 26 -> 26, of which waited for: 11 -> 8; matrix products, arithmetic and copies ran while one was open for 0% -> 0% of each run, Pallas kernels for 11% -> 10%
where the time goes in v2:
time: 40.2 us; the launch traced here: 40.1 us
  starting transfers between devices  21.6 us (54%)
  waiting for transfers between devices  11.5 us (29%)
  Pallas kernels  5.87 us (15%)
  local copies, waits for them, and re-layouts  1 us (2%)
    ppermute x26, starting transfers between devices, send(): return lax.ppermute(value, ('groups', 'tiles', 'section'), pairs)  21.6 us
    ppermute x26, waiting for transfers between devices, send(): return lax.ppermute(value, ('groups', 'tiles', 'section'), pairs)  11.5 us
    pallas_call x1, Pallas kernels, prepare(): pl.pallas_call(kernel, out_shape=(held(shape, jnp.bfloat16), held(shape,...  2.25 us
    pallas_call x8, Pallas kernels, frame_step(): pl.pallas_call(kernel, out_shape=tuple(out_shape), in_specs=[VMEM] * len(...  2.22 us
    unnamed x2, local copies, waits for them, and re-layouts  1 us
  transfers between devices with their start and end apart: 26, of which 8 were waited for; matrix products, arithmetic and copies ran while one was open for 0% of the time, Pallas kernels for 10%

profile of v2, /device:TPU:0, one launch (start us, length us, event | category | flops | bytes accessed | tf_op | source)
XLA Modules:
  0.0 40.1 jit_solution(14294176288095767721)
XLA Ops:
  0.0 1.0 %copy-done = f32[2,192,2,128]{3,2,1,0:T(2,128)S(1)} copy-done((f32[2,192,2,128]{3,2,1,0:T(2,128)S(1)}, f32[2,192,2,128]{3,2,1,0:T(2,128)}, u32[]{:S(2)}) %copy-start) | copy-done | bytes 393240
  1.0 3.1 %collective-permute-start = (f32[2,192,128]{2,1,0:T(8,128)S(1)}, f32[2,192,128]{2,1,0:T(8,128)S(1)}, u32[]{:S(2)}, u32[]{:S(2)}) collective-permute-start(f32[2,192,128]{2,1,0:T(8,128)S(1)} %get-tuple-element.44), channel_id=1, source_target_pairs={{0,4},{1,17},{2,3},{3,2},{4,0},{5,21},{6,7},{7,6},{8,12},{9,25},{1... | collective-permute-start | bytes 589832 | tf_op jit(solution)/shard_map/ppermute | solution.py:104
  4.2 2.3 %prepare.1 = (bf16[2,192,1792]{2,1,0:T(8,128)(2,1)S(1)}, bf16[2,192,1792]{2,1,0:T(8,128)(2,1)S(1)}, f32[192,128]{1,0:T(8,128)S(1)}) custom-call(f32[27,192,192]{2,1,0:T(8,128)} %bitcast.6, f32[1,192]{1,0:T(1,128)} %gain_ref.1), custom_call_target="tpu_custom_call" | custom-call | tf_op jit(solution)/shard_map/prepare/pallas_call | solution.py:156
  6.4 1.4 %collective-permute-done.refs_1_ = f32[2,192,128]{2,1,0:T(8,128)S(1)} collective-permute-done((f32[2,192,128]{2,1,0:T(8,128)S(1)}, f32[2,192,128]{2,1,0:T(8,128)S(1)}, u32[]{:S(2)}, u32[]{:S(2)}) %collective-permute-start) | collective-permute-done | bytes 196640 | tf_op jit(solution)/shard_map/ppermute | solution.py:104
  7.8 1.1 %frame_step.8 = (f32[384,128]{1,0:T(8,128)S(1)}, f32[192,128]{1,0:T(8,128)S(1)}, f32[192,128]{1,0:T(8,128)S(1)}, bf16[1792,256]{1,0:T(8,128)(2,1)S(1)}, bf16[1792,256]{1,0:T(8,128)(2,1)S(1)}) custom-call(f32[2,384,128]{2,1,0:T(8,128)S(1)} %bitcast.4, f32[2,192,128]{2,1,0:T(8,128)S(1)} %collective-permute-done.refs_1_, ...), custom_call_target="tpu_custom_call" | custom-call | flops 528482304 | bytes 1048576 | tf_op jit(solution)/shard_map/frame_step/pallas_call | solution.py:306
  8.9 0.1 collective-permute-start.2
  9.0 3.3 %collective-permute-start.3 = (f32[192,128]{1,0:T(8,128)S(1)}, f32[192,128]{1,0:T(8,128)S(1)}, u32[]{:S(2)}, u32[]{:S(2)}) collective-permute-start(f32[192,128]{1,0:T(8,128)S(1)} %get-tuple-element.50), channel_id=1, source_target_pairs={{0,5},{1,0},{2,3},{3,2},{4,1},{5,4},{6,7},{7,6},{8,13},{9,8},{10,1... | collective-permute-start | bytes 294920 | tf_op jit(solution)/shard_map/ppermute | solution.py:104
  12.2 0.7 %earlier_frames.4.refs_6_ = f32[192,256]{1,0:T(8,128)S(1)} custom-call(bf16[2,192,1792]{2,1,0:T(8,128)(2,1)S(1)} %get-tuple-element.47.refs_4_.high_ref, bf16[2,192,1792]{2,1,0:T(8,128)(2,1)S(1)} %get-tuple-element.48.refs_5_.low_ref, bf16[1792,256]{1,0:T(8,128)(2,1)S(1)} %get-tuple-element.62.refs_0_, bf16[1792,256]{1,0:T(8,128)(2,1)S(1)} %get-tuple-element.63.refs_1_), custom_call_target="tpu_custom_call" | custom-call | flops 528482304 | bytes 1048576 | tf_op jit(solution)/shard_map/earlier_frames/pallas_call | solution.py:344
  12.9 1.1 %frame_step.12 = (f32[384,128]{1,0:T(8,128)S(1)}, f32[192,128]{1,0:T(8,128)S(1)}, f32[192,128]{1,0:T(8,128)S(1)}) custom-call(f32[2,384,128]{2,1,0:T(8,128)S(1)} %bitcast.5, f32[2,192,128]{2,1,0:T(8,128)S(1)} %collective-permute-done.refs_1_, f32[2,192,128]{2,1,0:T(8,128)S(1)} %collective-permute-done.1.refs_2_, f32[192,128]{1,0:T(8,128)S(1)} %get-tuple-element.46.refs_3_, ...), custom_call_target="tpu_custom_call" | custom-call | flops 528482304 | bytes 1048576 | tf_op jit(solution)/shard_map/frame_step/pallas_call | solution.py:306
  14.1 0.1 collective-permute-start.14
  14.1 2.2 %collective-permute-start.15 = (f32[192,128]{1,0:T(8,128)S(1)}, f32[192,128]{1,0:T(8,128)S(1)}, u32[]{:S(2)}, u32[]{:S(2)}) collective-permute-start(f32[192,128]{1,0:T(8,128)S(1)} %get-tuple-element.65), channel_id=1, source_target_pairs={{0,5},{1,0},{2,3},{3,2},{4,1},{5,4},{6,7},{7,6},{8,13},{9,8},{10,1... | collective-permute-start | bytes 294920 | tf_op jit(solution)/shard_map/ppermute | solution.py:104
  16.4 1.6 %collective-permute-start.5 = (f32[384,128]{1,0:T(8,128)S(1)}, f32[384,128]{1,0:T(8,128)S(1)}, u32[]{:S(2)}, u32[]{:S(2)}) collective-permute-start(f32[384,128]{1,0:T(8,128)S(1)} %get-tuple-element.52), channel_id=1, source_target_pairs={{0,1},{1,2},{2,3},{3,0},{4,5},{5,6},{6,7},{7,4},{8,9},{9,10},{10,1... | collective-permute-start | bytes 589832 | tf_op jit(solution)/shard_map/ppermute | solution.py:104
  18.0 0.1 collective-permute-start.6
  18.0 0.5 %collective-permute-done.15.refs_1_ = f32[192,128]{1,0:T(8,128)S(1)} collective-permute-done((f32[192,128]{1,0:T(8,128)S(1)}, f32[192,128]{1,0:T(8,128)S(1)}, u32[]{:S(2)}, u32[]{:S(2)}) %collective-permute-start.15) | collective-permute-done | bytes 98336 | tf_op jit(solution)/shard_map/ppermute | solution.py:104
  18.5 0.3 collective-permute-start.7
  18.8 1.2 %collective-permute-start.17 = (f32[384,128]{1,0:T(8,128)S(1)}, f32[384,128]{1,0:T(8,128)S(1)}, u32[]{:S(2)}, u32[]{:S(2)}) collective-permute-start(f32[384,128]{1,0:T(8,128)S(1)} %get-tuple-element.69), channel_id=1, source_target_pairs={{0,1},{1,2},{2,3},{3,0},{4,5},{5,6},{6,7},{7,4},{8,9},{9,10},{10,1... | collective-permute-start | bytes 589832 | tf_op jit(solution)/shard_map/ppermute | solution.py:104
  20.0 0.2 collective-permute-start.18
  20.3 2.3 %collective-permute-done.6.refs_1_ = f32[192,128]{1,0:T(8,128)S(1)} collective-permute-done((f32[192,128]{1,0:T(8,128)S(1)}, f32[192,128]{1,0:T(8,128)S(1)}, u32[]{:S(2)}, u32[]{:S(2)}) %collective-permute-start.6) | collective-permute-done | bytes 98336 | tf_op jit(solution)/shard_map/ppermute | solution.py:104
  22.6 1.1 %collective-permute-done.7.refs_2_ = f32[192,128]{1,0:T(8,128)S(1)} collective-permute-done((f32[192,128]{1,0:T(8,128)S(1)}, f32[192,128]{1,0:T(8,128)S(1)}, u32[]{:S(2)}, u32[]{:S(2)}) %collective-permute-start.7) | collective-permute-done | bytes 98336 | tf_op jit(solution)/shard_map/ppermute | solution.py:104
  23.6 0.5 %collective-permute-start.9 = (f32[192,128]{1,0:T(8,128)S(1)}, f32[192,128]{1,0:T(8,128)S(1)}, u32[]{:S(2)}, u32[]{:S(2)}) collective-permute-start(f32[192,128]{1,0:T(8,128)S(1)} %get-tuple-element.56), channel_id=1, source_target_pairs={{0,1},{1,0},{2,7},{3,2},{4,5},{5,4},{6,3},{7,6},{8,9},{9,8},{10,15... | collective-permute-start | bytes 294920 | tf_op jit(solution)/shard_map/ppermute | solution.py:104
  24.1 2.6 %collective-permute-done.18.refs_1_ = f32[192,128]{1,0:T(8,128)S(1)} collective-permute-done((f32[192,128]{1,0:T(8,128)S(1)}, f32[192,128]{1,0:T(8,128)S(1)}, u32[]{:S(2)}, u32[]{:S(2)}) %collective-permute-start.18) | collective-permute-done | bytes 98336 | tf_op jit(solution)/shard_map/ppermute | solution.py:104
  26.8 1.0 %collective-permute-done.19.refs_2_ = f32[192,128]{1,0:T(8,128)S(1)} collective-permute-done((f32[192,128]{1,0:T(8,128)S(1)}, f32[192,128]{1,0:T(8,128)S(1)}, u32[]{:S(2)}, u32[]{:S(2)}) %collective-permute-start.19) | collective-permute-done | bytes 98336 | tf_op jit(solution)/shard_map/ppermute | solution.py:104
  27.8 0.5 %collective-permute-start.21 = (f32[192,128]{1,0:T(8,128)S(1)}, f32[192,128]{1,0:T(8,128)S(1)}, u32[]{:S(2)}, u32[]{:S(2)}) collective-permute-start(f32[192,128]{1,0:T(8,128)S(1)} %get-tuple-element.75), channel_id=1, source_target_pairs={{0,1},{1,0},{2,7},{3,2},{4,5},{5,4},{6,3},{7,6},{8,9},{9,8},{10,15... | collective-permute-start | bytes 294920 | tf_op jit(solution)/shard_map/ppermute | solution.py:104
  28.4 0.0 collective-permute-start.22
  28.4 4.4 %collective-permute-start.11 = (f32[96,128]{1,0:T(8,128)S(1)}, f32[96,128]{1,0:T(8,128)S(1)}, u32[]{:S(2)}, u32[]{:S(2)}) collective-permute-start(f32[96,128]{1,0:T(8,128)S(1)} %get-tuple-element.58), channel_id=1, source_target_pairs={{0,3},{1,17},{2,18},{3,0},{4,7},{5,21},{6,22},{7,4},{8,11},{9,25},... | collective-permute-start | bytes 147464 | tf_op jit(solution)/shard_map/ppermute | solution.py:104
  32.8 1.5 %collective-permute-start.12 = (f32[96,128]{1,0:T(8,128)S(1)}, f32[96,128]{1,0:T(8,128)S(1)}, u32[]{:S(2)}, u32[]{:S(2)}) collective-permute-start(f32[96,128]{1,0:T(8,128)S(1)} %get-tuple-element.59), channel_id=1, source_target_pairs={{0,16},{1,2},{2,3},{3,1},{4,20},{5,6},{6,7},{7,5},{8,24},{9,10},{1... | collective-permute-start | bytes 147464 | tf_op jit(solution)/shard_map/ppermute | solution.py:104
  34.3 1.0 %collective-permute-start.23 = (f32[96,128]{1,0:T(8,128)S(1)}, f32[96,128]{1,0:T(8,128)S(1)}, u32[]{:S(2)}, u32[]{:S(2)}) collective-permute-start(f32[96,128]{1,0:T(8,128)S(1)} %get-tuple-element.79), channel_id=1, source_target_pairs={{0,3},{1,17},{2,18},{3,0},{4,7},{5,21},{6,22},{7,4},{8,11},{9,25},... | collective-permute-start | bytes 147464 | tf_op jit(solution)/shard_map/ppermute | solution.py:104
  35.3 1.5 %collective-permute-start.24 = (f32[96,128]{1,0:T(8,128)S(1)}, f32[96,128]{1,0:T(8,128)S(1)}, u32[]{:S(2)}, u32[]{:S(2)}) collective-permute-start(f32[96,128]{1,0:T(8,128)S(1)} %get-tuple-element.80), channel_id=1, source_target_pairs={{0,16},{1,2},{2,3},{3,1},{4,20},{5,6},{6,7},{7,5},{8,24},{9,10},{1... | collective-permute-start | bytes 147464 | tf_op jit(solution)/shard_map/ppermute | solution.py:104
  36.8 0.0 collective-permute-done.12.refs_1_
  36.9 1.0 %collective-permute-done.23.refs_4_ = f32[96,128]{1,0:T(8,128)S(1)} collective-permute-done((f32[96,128]{1,0:T(8,128)S(1)}, f32[96,128]{1,0:T(8,128)S(1)}, u32[]{:S(2)}, u32[]{:S(2)}) %collective-permute-start.23) | collective-permute-done | bytes 49184 | tf_op jit(solution)/shard_map/ppermute | solution.py:104
  37.9 1.5 %collective-permute-done.24.refs_5_ = f32[96,128]{1,0:T(8,128)S(1)} collective-permute-done((f32[96,128]{1,0:T(8,128)S(1)}, f32[96,128]{1,0:T(8,128)S(1)}, u32[]{:S(2)}, u32[]{:S(2)}) %collective-permute-start.24) | collective-permute-done | bytes 49184 | tf_op jit(solution)/shard_map/ppermute | solution.py:104
  39.4 0.7 %assemble.1 = f32[2,96,128]{2,1,0:T(8,128)} custom-call(f32[96,128]{1,0:T(8,128)S(1)} %collective-permute-done.11.refs_0_, f32[96,128]{1,0:T(8,128)S(1)} %collective-permute-done.12.refs_1_, f32[96,128]{1,0:T(8,128)S(1)} %collective-permute-done.13.refs_2_, f32[96,128]{1,0:T(8,128)S(1)} %get-tuple-element.61.refs_3_, ...), custom_call_target="tpu_custom_call" | custom-call | tf_op jit(solution)/shard_map/assemble/pallas_call | solution.py:425
  (37 shorter events, 0.1 us)
Async XLA Ops:
  0.0 1.0 %copy-start = (f32[2,192,2,128]{3,2,1,0:T(2,128)S(1)}, f32[2,192,2,128]{3,2,1,0:T(2,128)}, u32[]{:S(2)}) copy-start(f32[2,192,2,128]{3,2,1,0:T(2,128)} %param.3) | copy-start | bytes 1179652
  1.0 6.8 %collective-permute-start = (f32[2,192,128]{2,1,0:T(8,128)S(1)}, f32[2,192,128]{2,1,0:T(8,128)S(1)}, u32[]{:S(2)}, u32[]{:S(2)}) collective-permute-start(f32[2,192,128]{2,1,0:T(8,128)S(1)} %get-tuple-element.44), channel_id=1, source_target_pairs={{0,4},{1,17},{2,3},{3,2},{4,0},{5,21},{6,7},{7,6},{8,12},{9,25},{1... | collective-permute-start | bytes 589832 | tf_op jit(solution)/shard_map/ppermute | solution.py:104
  4.2 3.7 %collective-permute-start.1 = (f32[2,192,128]{2,1,0:T(8,128)S(1)}, f32[2,192,128]{2,1,0:T(8,128)S(1)}, u32[]{:S(2)}, u32[]{:S(2)}) collective-permute-start(f32[2,192,128]{2,1,0:T(8,128)S(1)} %get-tuple-element.45), channel_id=1, source_target_pairs={{0,1},{1,0},{2,3},{3,2},{4,8},{5,21},{6,7},{7,6},{8,4},{9,25},{10,... | collective-permute-start | bytes 589832 | tf_op jit(solution)/shard_map/ppermute | solution.py:104
  8.9 7.4 %collective-permute-start.2 = (f32[384,128]{1,0:T(8,128)S(1)}, f32[384,128]{1,0:T(8,128)S(1)}, u32[]{:S(2)}, u32[]{:S(2)}) collective-permute-start(f32[384,128]{1,0:T(8,128)S(1)} %get-tuple-element.49), channel_id=1, source_target_pairs={{0,1},{1,0},{2,3},{3,2},{4,5},{5,4},{6,7},{7,6},{8,9},{9,8},{10,11... | collective-permute-start | bytes 589832 | tf_op jit(solution)/shard_map/ppermute | solution.py:104
  9.0 7.3 %collective-permute-start.3 = (f32[192,128]{1,0:T(8,128)S(1)}, f32[192,128]{1,0:T(8,128)S(1)}, u32[]{:S(2)}, u32[]{:S(2)}) collective-permute-start(f32[192,128]{1,0:T(8,128)S(1)} %get-tuple-element.50), channel_id=1, source_target_pairs={{0,5},{1,0},{2,3},{3,2},{4,1},{5,4},{6,7},{7,6},{8,13},{9,8},{10,1... | collective-permute-start | bytes 294920 | tf_op jit(solution)/shard_map/ppermute | solution.py:104
  12.2 4.1 %collective-permute-start.4 = (f32[192,128]{1,0:T(8,128)S(1)}, f32[192,128]{1,0:T(8,128)S(1)}, u32[]{:S(2)}, u32[]{:S(2)}) collective-permute-start(f32[192,128]{1,0:T(8,128)S(1)} %get-tuple-element.51), channel_id=1, source_target_pairs={{0,1},{1,0},{2,3},{3,2},{4,9},{5,4},{6,7},{7,6},{8,5},{9,8},{10,11... | collective-permute-start | bytes 294920 | tf_op jit(solution)/shard_map/ppermute | solution.py:104
  14.1 4.8 %collective-permute-start.14 = (f32[384,128]{1,0:T(8,128)S(1)}, f32[384,128]{1,0:T(8,128)S(1)}, u32[]{:S(2)}, u32[]{:S(2)}) collective-permute-start(f32[384,128]{1,0:T(8,128)S(1)} %get-tuple-element.64), channel_id=1, source_target_pairs={{0,1},{1,0},{2,3},{3,2},{4,5},{5,4},{6,7},{7,6},{8,9},{9,8},{10,11... | collective-permute-start | bytes 589832 | tf_op jit(solution)/shard_map/ppermute | solution.py:104
  14.1 4.4 %collective-permute-start.15 = (f32[192,128]{1,0:T(8,128)S(1)}, f32[192,128]{1,0:T(8,128)S(1)}, u32[]{:S(2)}, u32[]{:S(2)}) collective-permute-start(f32[192,128]{1,0:T(8,128)S(1)} %get-tuple-element.65), channel_id=1, source_target_pairs={{0,5},{1,0},{2,3},{3,2},{4,1},{5,4},{6,7},{7,6},{8,13},{9,8},{10,1... | collective-permute-start | bytes 294920 | tf_op jit(solution)/shard_map/ppermute | solution.py:104
  16.3 2.5 %collective-permute-start.16 = (f32[192,128]{1,0:T(8,128)S(1)}, f32[192,128]{1,0:T(8,128)S(1)}, u32[]{:S(2)}, u32[]{:S(2)}) collective-permute-start(f32[192,128]{1,0:T(8,128)S(1)} %get-tuple-element.66), channel_id=1, source_target_pairs={{0,1},{1,0},{2,3},{3,2},{4,9},{5,4},{6,7},{7,6},{8,5},{9,8},{10,11... | collective-permute-start | bytes 294920 | tf_op jit(solution)/shard_map/ppermute | solution.py:104
  16.4 7.3 %collective-permute-start.5 = (f32[384,128]{1,0:T(8,128)S(1)}, f32[384,128]{1,0:T(8,128)S(1)}, u32[]{:S(2)}, u32[]{:S(2)}) collective-permute-start(f32[384,128]{1,0:T(8,128)S(1)} %get-tuple-element.52), channel_id=1, source_target_pairs={{0,1},{1,2},{2,3},{3,0},{4,5},{5,6},{6,7},{7,4},{8,9},{9,10},{10,1... | collective-permute-start | bytes 589832 | tf_op jit(solution)/shard_map/ppermute | solution.py:104
  18.0 4.6 %collective-permute-start.6 = (f32[192,128]{1,0:T(8,128)S(1)}, f32[192,128]{1,0:T(8,128)S(1)}, u32[]{:S(2)}, u32[]{:S(2)}) collective-permute-start(f32[192,128]{1,0:T(8,128)S(1)} %get-tuple-element.53), channel_id=1, source_target_pairs={{0,1},{1,6},{2,3},{3,0},{4,5},{5,2},{6,7},{7,4},{8,9},{9,14},{10,1... | collective-permute-start | bytes 294920 | tf_op jit(solution)/shard_map/ppermute | solution.py:104
  18.5 5.1 %collective-permute-start.7 = (f32[192,128]{1,0:T(8,128)S(1)}, f32[192,128]{1,0:T(8,128)S(1)}, u32[]{:S(2)}, u32[]{:S(2)}) collective-permute-start(f32[192,128]{1,0:T(8,128)S(1)} %get-tuple-element.54), channel_id=1, source_target_pairs={{0,1},{1,2},{2,3},{3,0},{4,5},{5,10},{6,7},{7,4},{8,9},{9,6},{10,1... | collective-permute-start | bytes 294920 | tf_op jit(solution)/shard_map/ppermute | solution.py:104
  18.8 9.0 %collective-permute-start.17 = (f32[384,128]{1,0:T(8,128)S(1)}, f32[384,128]{1,0:T(8,128)S(1)}, u32[]{:S(2)}, u32[]{:S(2)}) collective-permute-start(f32[384,128]{1,0:T(8,128)S(1)} %get-tuple-element.69), channel_id=1, source_target_pairs={{0,1},{1,2},{2,3},{3,0},{4,5},{5,6},{6,7},{7,4},{8,9},{9,10},{10,1... | collective-permute-start | bytes 589832 | tf_op jit(solution)/shard_map/ppermute | solution.py:104
  20.0 6.7 %collective-permute-start.18 = (f32[192,128]{1,0:T(8,128)S(1)}, f32[192,128]{1,0:T(8,128)S(1)}, u32[]{:S(2)}, u32[]{:S(2)}) collective-permute-start(f32[192,128]{1,0:T(8,128)S(1)} %get-tuple-element.70), channel_id=1, source_target_pairs={{0,1},{1,6},{2,3},{3,0},{4,5},{5,2},{6,7},{7,4},{8,9},{9,14},{10,1... | collective-permute-start | bytes 294920 | tf_op jit(solution)/shard_map/ppermute | solution.py:104
  22.6 5.3 %collective-permute-start.19 = (f32[192,128]{1,0:T(8,128)S(1)}, f32[192,128]{1,0:T(8,128)S(1)}, u32[]{:S(2)}, u32[]{:S(2)}) collective-permute-start(f32[192,128]{1,0:T(8,128)S(1)} %get-tuple-element.71), channel_id=1, source_target_pairs={{0,1},{1,2},{2,3},{3,0},{4,5},{5,10},{6,7},{7,4},{8,9},{9,6},{10,1... | collective-permute-start | bytes 294920 | tf_op jit(solution)/shard_map/ppermute | solution.py:104
  23.6 4.8 %collective-permute-start.8 = (f32[384,128]{1,0:T(8,128)S(1)}, f32[384,128]{1,0:T(8,128)S(1)}, u32[]{:S(2)}, u32[]{:S(2)}) collective-permute-start(f32[384,128]{1,0:T(8,128)S(1)} %get-tuple-element.55), channel_id=1, source_target_pairs={{0,1},{1,0},{2,3},{3,2},{4,5},{5,4},{6,7},{7,6},{8,9},{9,8},{10,11... | collective-permute-start | bytes 589832 | tf_op jit(solution)/shard_map/ppermute | solution.py:104
  23.6 4.7 %collective-permute-start.9 = (f32[192,128]{1,0:T(8,128)S(1)}, f32[192,128]{1,0:T(8,128)S(1)}, u32[]{:S(2)}, u32[]{:S(2)}) collective-permute-start(f32[192,128]{1,0:T(8,128)S(1)} %get-tuple-element.56), channel_id=1, source_target_pairs={{0,1},{1,0},{2,7},{3,2},{4,5},{5,4},{6,3},{7,6},{8,9},{9,8},{10,15... | collective-permute-start | bytes 294920 | tf_op jit(solution)/shard_map/ppermute | solution.py:104
  26.8 1.6 %collective-permute-start.10 = (f32[192,128]{1,0:T(8,128)S(1)}, f32[192,128]{1,0:T(8,128)S(1)}, u32[]{:S(2)}, u32[]{:S(2)}) collective-permute-start(f32[192,128]{1,0:T(8,128)S(1)} %get-tuple-element.57), channel_id=1, source_target_pairs={{0,1},{1,0},{2,3},{3,2},{4,5},{5,4},{6,11},{7,6},{8,9},{9,8},{10,7... | collective-permute-start | bytes 294920 | tf_op jit(solution)/shard_map/ppermute | solution.py:104
  27.8 6.5 %collective-permute-start.20 = (f32[384,128]{1,0:T(8,128)S(1)}, f32[384,128]{1,0:T(8,128)S(1)}, u32[]{:S(2)}, u32[]{:S(2)}) collective-permute-start(f32[384,128]{1,0:T(8,128)S(1)} %get-tuple-element.74), channel_id=1, source_target_pairs={{0,1},{1,0},{2,3},{3,2},{4,5},{5,4},{6,7},{7,6},{8,9},{9,8},{10,11... | collective-permute-start | bytes 589832 | tf_op jit(solution)/shard_map/ppermute | solution.py:104
  27.8 6.5 %collective-permute-start.21 = (f32[192,128]{1,0:T(8,128)S(1)}, f32[192,128]{1,0:T(8,128)S(1)}, u32[]{:S(2)}, u32[]{:S(2)}) collective-permute-start(f32[192,128]{1,0:T(8,128)S(1)} %get-tuple-element.75), channel_id=1, source_target_pairs={{0,1},{1,0},{2,7},{3,2},{4,5},{5,4},{6,3},{7,6},{8,9},{9,8},{10,15... | collective-permute-start | bytes 294920 | tf_op jit(solution)/shard_map/ppermute | solution.py:104
  28.4 5.9 %collective-permute-start.22 = (f32[192,128]{1,0:T(8,128)S(1)}, f32[192,128]{1,0:T(8,128)S(1)}, u32[]{:S(2)}, u32[]{:S(2)}) collective-permute-start(f32[192,128]{1,0:T(8,128)S(1)} %get-tuple-element.76), channel_id=1, source_target_pairs={{0,1},{1,0},{2,3},{3,2},{4,5},{5,4},{6,11},{7,6},{8,9},{9,8},{10,7... | collective-permute-start | bytes 294920 | tf_op jit(solution)/shard_map/ppermute | solution.py:104
  28.4 8.4 %collective-permute-start.11 = (f32[96,128]{1,0:T(8,128)S(1)}, f32[96,128]{1,0:T(8,128)S(1)}, u32[]{:S(2)}, u32[]{:S(2)}) collective-permute-start(f32[96,128]{1,0:T(8,128)S(1)} %get-tuple-element.58), channel_id=1, source_target_pairs={{0,3},{1,17},{2,18},{3,0},{4,7},{5,21},{6,22},{7,4},{8,11},{9,25},... | collective-permute-start | bytes 147464 | tf_op jit(solution)/shard_map/ppermute | solution.py:104
  32.8 4.1 %collective-permute-start.12 = (f32[96,128]{1,0:T(8,128)S(1)}, f32[96,128]{1,0:T(8,128)S(1)}, u32[]{:S(2)}, u32[]{:S(2)}) collective-permute-start(f32[96,128]{1,0:T(8,128)S(1)} %get-tuple-element.59), channel_id=1, source_target_pairs={{0,16},{1,2},{2,3},{3,1},{4,20},{5,6},{6,7},{7,5},{8,24},{9,10},{1... | collective-permute-start | bytes 147464 | tf_op jit(solution)/shard_map/ppermute | solution.py:104
  34.3 2.6 %collective-permute-start.13 = (f32[96,128]{1,0:T(8,128)S(1)}, f32[96,128]{1,0:T(8,128)S(1)}, u32[]{:S(2)}, u32[]{:S(2)}) collective-permute-start(f32[96,128]{1,0:T(8,128)S(1)} %get-tuple-element.60), channel_id=1, source_target_pairs={{0,1},{1,0},{2,3},{3,2},{4,5},{5,4},{6,7},{7,6},{8,9},{9,8},{10,11... | collective-permute-start | bytes 147464 | tf_op jit(solution)/shard_map/ppermute | solution.py:104
  34.3 3.6 %collective-permute-start.23 = (f32[96,128]{1,0:T(8,128)S(1)}, f32[96,128]{1,0:T(8,128)S(1)}, u32[]{:S(2)}, u32[]{:S(2)}) collective-permute-start(f32[96,128]{1,0:T(8,128)S(1)} %get-tuple-element.79), channel_id=1, source_target_pairs={{0,3},{1,17},{2,18},{3,0},{4,7},{5,21},{6,22},{7,4},{8,11},{9,25},... | collective-permute-start | bytes 147464 | tf_op jit(solution)/shard_map/ppermute | solution.py:104
  35.3 4.1 %collective-permute-start.24 = (f32[96,128]{1,0:T(8,128)S(1)}, f32[96,128]{1,0:T(8,128)S(1)}, u32[]{:S(2)}, u32[]{:S(2)}) collective-permute-start(f32[96,128]{1,0:T(8,128)S(1)} %get-tuple-element.80), channel_id=1, source_target_pairs={{0,16},{1,2},{2,3},{3,1},{4,20},{5,6},{6,7},{7,5},{8,24},{9,10},{1... | collective-permute-start | bytes 147464 | tf_op jit(solution)/shard_map/ppermute | solution.py:104
  36.8 2.6 %collective-permute-start.25 = (f32[96,128]{1,0:T(8,128)S(1)}, f32[96,128]{1,0:T(8,128)S(1)}, u32[]{:S(2)}, u32[]{:S(2)}) collective-permute-start(f32[96,128]{1,0:T(8,128)S(1)} %get-tuple-element.81), channel_id=1, source_target_pairs={{0,1},{1,0},{2,3},{3,2},{4,5},{5,4},{6,7},{7,6},{8,9},{9,8},{10,11... | collective-permute-start | bytes 147464 | tf_op jit(solution)/shard_map/ppermute | solution.py:104

commit v3 on v2

--- a/solution.py
+++ b/solution.py
@@ -85,15 +85,17 @@
     groups, _, sections = shape
     last = sections - 1
     where = {}
-    if target == last - 1 or target == 0:
+    if target == last - 1:
         idle_cycle(where, [last, target])
+    elif target == 0:
+        idle_cycle(where, [last, 0, 1, last - 1])
     else:
-        idle_cycle(where, [last, target, last - 1])
+        idle_cycle(where, [last, target, target ^ 1])
 
     def goal(g, t, s):
         if s in where:
             return g, t, where[s]
-        if target == last - 1 and s ^ 1 < last - 1:
+        if s ^ 1 not in where and s ^ 1 < sections:
             return g, t, s ^ 1
         return other_group(g, groups), t, s
 
@@ -180,19 +182,19 @@
     frames, lines, width = latents.shape
     channels = lines // rows
 
-    def kernel(ref, out_a, out_b):
+    def kernel(ref, *outs):
         even = lax.rem(lax.axis_index("tiles"), 2) == 0
         for f in range(frames):
             top = ref[f, pl.ds(0, channels, stride=rows), :]
             bottom = ref[f, pl.ds(rows - 1, channels, stride=rows), :]
-            out_a[f] = jnp.where(even, bottom, top)
-            out_b[f] = jnp.where(even, top, bottom)
+            outs[2 * f][...] = jnp.where(even, bottom, top)
+            outs[2 * f + 1][...] = jnp.where(even, top, bottom)
 
     return pl.pallas_call(
         kernel,
-        out_shape=tuple([held((frames, channels, width))] * 2),
+        out_shape=tuple([held((channels, width))] * (2 * frames)),
         in_specs=[VMEM],
-        out_specs=(VMEM, VMEM),
+        out_specs=tuple([VMEM] * (2 * frames)),
         compiler_params=GRANT,
         name="edges",
     )(latents)
@@ -242,9 +244,7 @@
         @pl.when(lax.axis_index("section") == layer)
         def _():
             gains = gain_ref[...]
-            near_one, near_two = (
-                ref[...] if frame is None else ref[frame] for ref in (a_ref, b_ref)
-            )
+            near_one, near_two = a_ref[...], b_ref[...]
             above = jnp.where(even, near_two, near_one)
             below = jnp.where(even, near_one, near_two)
             above = jnp.where(tile == 0, 0.0, above)
@@ -366,10 +366,11 @@
     of_b = lambda t: partner_b(t, tiles)
 
     flat = latents.reshape(frames, channels * rows, width)
-    edge_a, edge_b = edges(flat, rows)
+    edge = edges(flat, rows)
+    edge_a, edge_b = edge[0::2], edge[1::2]
     rim_a, rim_b = (rim_pairs(shape, of) for of in (of_a, of_b))
-    near_a = [send(edge_a, rim_a)] * frames
-    near_b = [send(edge_b, rim_b)] * frames
+    near_a = [send(edge_a[f], rim_a) for f in range(frames)]
+    near_b = [send(edge_b[f], rim_b) for f in range(frames)]
     *weights, gains = prepare(conv_weight[0], gain, steps, depth, width)
     main = [flat] * frames
 

time: 40.2 us -> 37.6 us (0.935)
  waiting for transfers between devices: 11.5 us -> 8.59 us
    ppermute x26 -> x28, waiting for transfers between devices: 11.5 us -> 8.59 us  [send(): return lax.ppermute(value, ('groups', 'tiles', 'section'), pairs)]
    ppermute x26 -> x28, starting transfers between devices: 21.6 us -> 21.8 us  [send(): return lax.ppermute(value, ('groups', 'tiles', 'section'), pairs)]
  transfers between devices with their start and end apart: 26 -> 28, of which waited for: 8 -> 6; matrix products, arithmetic and copies ran while one was open for 0% -> 0% of each run, Pallas kernels for 10% -> 14%
where the time goes in v3:
time: 37.6 us; the launch traced here: 37.4 us
  starting transfers between devices  21.8 us (58%)
  waiting for transfers between devices  8.59 us (23%)
  Pallas kernels  5.88 us (16%)
  local copies, waits for them, and re-layouts  1 us (3%)
    ppermute x28, starting transfers between devices, send(): return lax.ppermute(value, ('groups', 'tiles', 'section'), pairs)  21.8 us
    ppermute x28, waiting for transfers between devices, send(): return lax.ppermute(value, ('groups', 'tiles', 'section'), pairs)  8.59 us
    pallas_call x1, Pallas kernels, prepare(): pl.pallas_call(kernel, out_shape=(held(shape, jnp.bfloat16), held(shape,...  2.25 us
    pallas_call x8, Pallas kernels, frame_step(): pl.pallas_call(kernel, out_shape=tuple(out_shape), in_specs=[VMEM] * len(...  2.22 us
    unnamed x2, local copies, waits for them, and re-layouts  1 us
  transfers between devices with their start and end apart: 28, of which 6 were waited for; matrix products, arithmetic and copies ran while one was open for 0% of the time, Pallas kernels for 14%

profile of v3, /device:TPU:0, one launch (start us, length us, event | category | flops | bytes accessed | tf_op | source)
XLA Modules:
  0.0 37.4 jit_solution(14087350649746642840)
XLA Ops:
  0.0 1.0 %copy-done = f32[2,192,2,128]{3,2,1,0:T(2,128)S(1)} copy-done((f32[2,192,2,128]{3,2,1,0:T(2,128)S(1)}, f32[2,192,2,128]{3,2,1,0:T(2,128)}, u32[]{:S(2)}) %copy-start) | copy-done | bytes 393240
  1.0 3.1 %collective-permute-start = (f32[192,128]{1,0:T(8,128)S(1)}, f32[192,128]{1,0:T(8,128)S(1)}, u32[]{:S(2)}, u32[]{:S(2)}) collective-permute-start(f32[192,128]{1,0:T(8,128)S(1)} %get-tuple-element.46), channel_id=1, source_target_pairs={{0,4},{1,17},{2,3},{3,2},{4,0},{5,21},{6,7},{7,6},{8,12},{9,25},{1... | collective-permute-start | bytes 294920 | tf_op jit(solution)/shard_map/ppermute | solution.py:106
  4.2 3.1 %collective-permute-start.14 = (f32[192,128]{1,0:T(8,128)S(1)}, f32[192,128]{1,0:T(8,128)S(1)}, u32[]{:S(2)}, u32[]{:S(2)}) collective-permute-start(f32[192,128]{1,0:T(8,128)S(1)} %get-tuple-element.64), channel_id=1, source_target_pairs={{0,4},{1,17},{2,3},{3,2},{4,0},{5,21},{6,7},{7,6},{8,12},{9,25},{1... | collective-permute-start | bytes 294920 | tf_op jit(solution)/shard_map/ppermute | solution.py:106
  7.3 2.3 %prepare.1 = (bf16[2,192,1792]{2,1,0:T(8,128)(2,1)S(1)}, bf16[2,192,1792]{2,1,0:T(8,128)(2,1)S(1)}, f32[192,128]{1,0:T(8,128)S(1)}) custom-call(f32[27,192,192]{2,1,0:T(8,128)} %bitcast.6, f32[1,192]{1,0:T(1,128)} %gain_ref.1), custom_call_target="tpu_custom_call" | custom-call | tf_op jit(solution)/shard_map/prepare/pallas_call | solution.py:158
  9.6 1.1 %frame_step.8 = (f32[384,128]{1,0:T(8,128)S(1)}, f32[192,128]{1,0:T(8,128)S(1)}, f32[192,128]{1,0:T(8,128)S(1)}, bf16[1792,256]{1,0:T(8,128)(2,1)S(1)}, bf16[1792,256]{1,0:T(8,128)(2,1)S(1)}) custom-call(f32[2,384,128]{2,1,0:T(8,128)S(1)} %bitcast.4, f32[192,128]{1,0:T(8,128)S(1)} %collective-permute-done.refs_1_, ...), custom_call_target="tpu_custom_call" | custom-call | flops 528482304 | bytes 1048576 | tf_op jit(solution)/shard_map/frame_step/pallas_call | solution.py:306
  10.7 0.1 collective-permute-start.2
  10.8 1.2 %collective-permute-start.3 = (f32[192,128]{1,0:T(8,128)S(1)}, f32[192,128]{1,0:T(8,128)S(1)}, u32[]{:S(2)}, u32[]{:S(2)}) collective-permute-start(f32[192,128]{1,0:T(8,128)S(1)} %get-tuple-element.52), channel_id=1, source_target_pairs={{0,5},{1,0},{2,3},{3,2},{4,1},{5,4},{6,7},{7,6},{8,13},{9,8},{10,1... | collective-permute-start | bytes 294920 | tf_op jit(solution)/shard_map/ppermute | solution.py:106
  12.0 0.7 %earlier_frames.4.refs_6_ = f32[192,256]{1,0:T(8,128)S(1)} custom-call(bf16[2,192,1792]{2,1,0:T(8,128)(2,1)S(1)} %get-tuple-element.49.refs_4_.high_ref, bf16[2,192,1792]{2,1,0:T(8,128)(2,1)S(1)} %get-tuple-element.50.refs_5_.low_ref, bf16[1792,256]{1,0:T(8,128)(2,1)S(1)} %get-tuple-element.66.refs_0_, bf16[1792,256]{1,0:T(8,128)(2,1)S(1)} %get-tuple-element.67.refs_1_), custom_call_target="tpu_custom_call" | custom-call | flops 528482304 | bytes 1048576 | tf_op jit(solution)/shard_map/earlier_frames/pallas_call | solution.py:344
  12.7 1.1 %frame_step.12 = (f32[384,128]{1,0:T(8,128)S(1)}, f32[192,128]{1,0:T(8,128)S(1)}, f32[192,128]{1,0:T(8,128)S(1)}) custom-call(f32[2,384,128]{2,1,0:T(8,128)S(1)} %bitcast.5, f32[192,128]{1,0:T(8,128)S(1)} %collective-permute-done.14.refs_1_, f32[192,128]{1,0:T(8,128)S(1)} %collective-permute-done.15.refs_2_, f32[192,128]{1,0:T(8,128)S(1)} %get-tuple-element.48.refs_3_, ...), custom_call_target="tpu_custom_call" | custom-call | flops 528482304 | bytes 1048576 | tf_op jit(solution)/shard_map/frame_step/pallas_call | solution.py:306
  13.8 0.1 collective-permute-start.16
  13.9 1.4 %collective-permute-start.17 = (f32[192,128]{1,0:T(8,128)S(1)}, f32[192,128]{1,0:T(8,128)S(1)}, u32[]{:S(2)}, u32[]{:S(2)}) collective-permute-start(f32[192,128]{1,0:T(8,128)S(1)} %get-tuple-element.69), channel_id=1, source_target_pairs={{0,5},{1,0},{2,3},{3,2},{4,1},{5,4},{6,7},{7,6},{8,13},{9,8},{10,1... | collective-permute-start | bytes 294920 | tf_op jit(solution)/shard_map/ppermute | solution.py:106
  15.3 0.0 collective-permute-start.18
  15.3 1.6 %collective-permute-start.5 = (f32[384,128]{1,0:T(8,128)S(1)}, f32[384,128]{1,0:T(8,128)S(1)}, u32[]{:S(2)}, u32[]{:S(2)}) collective-permute-start(f32[384,128]{1,0:T(8,128)S(1)} %get-tuple-element.54), channel_id=1, source_target_pairs={{0,1},{1,2},{2,3},{3,0},{4,5},{5,6},{6,7},{7,4},{8,9},{9,10},{10,1... | collective-permute-start | bytes 589832 | tf_op jit(solution)/shard_map/ppermute | solution.py:106
  16.9 0.1 collective-permute-start.6
  17.0 0.5 %collective-permute-done.17.refs_1_ = f32[192,128]{1,0:T(8,128)S(1)} collective-permute-done((f32[192,128]{1,0:T(8,128)S(1)}, f32[192,128]{1,0:T(8,128)S(1)}, u32[]{:S(2)}, u32[]{:S(2)}) %collective-permute-start.17) | collective-permute-done | bytes 98336 | tf_op jit(solution)/shard_map/ppermute | solution.py:106
  17.5 1.2 %collective-permute-start.7 = (f32[192,128]{1,0:T(8,128)S(1)}, f32[192,128]{1,0:T(8,128)S(1)}, u32[]{:S(2)}, u32[]{:S(2)}) collective-permute-start(f32[192,128]{1,0:T(8,128)S(1)} %get-tuple-element.56), channel_id=1, source_target_pairs={{0,1},{1,2},{2,3},{3,0},{4,5},{5,10},{6,7},{7,4},{8,9},{9,6},{10,1... | collective-permute-start | bytes 294920 | tf_op jit(solution)/shard_map/ppermute | solution.py:106
  18.7 1.2 %collective-permute-start.19 = (f32[384,128]{1,0:T(8,128)S(1)}, f32[384,128]{1,0:T(8,128)S(1)}, u32[]{:S(2)}, u32[]{:S(2)}) collective-permute-start(f32[384,128]{1,0:T(8,128)S(1)} %get-tuple-element.73), channel_id=1, source_target_pairs={{0,1},{1,2},{2,3},{3,0},{4,5},{5,6},{6,7},{7,4},{8,9},{9,10},{10,1... | collective-permute-start | bytes 589832 | tf_op jit(solution)/shard_map/ppermute | solution.py:106
  19.9 0.1 collective-permute-start.20
  20.0 1.6 %collective-permute-done.6.refs_1_ = f32[192,128]{1,0:T(8,128)S(1)} collective-permute-done((f32[192,128]{1,0:T(8,128)S(1)}, f32[192,128]{1,0:T(8,128)S(1)}, u32[]{:S(2)}, u32[]{:S(2)}) %collective-permute-start.6) | collective-permute-done | bytes 98336 | tf_op jit(solution)/shard_map/ppermute | solution.py:106
  21.5 1.1 %collective-permute-done.7.refs_2_ = f32[192,128]{1,0:T(8,128)S(1)} collective-permute-done((f32[192,128]{1,0:T(8,128)S(1)}, f32[192,128]{1,0:T(8,128)S(1)}, u32[]{:S(2)}, u32[]{:S(2)}) %collective-permute-start.7) | collective-permute-done | bytes 98336 | tf_op jit(solution)/shard_map/ppermute | solution.py:106
  22.6 0.5 %collective-permute-start.9 = (f32[192,128]{1,0:T(8,128)S(1)}, f32[192,128]{1,0:T(8,128)S(1)}, u32[]{:S(2)}, u32[]{:S(2)}) collective-permute-start(f32[192,128]{1,0:T(8,128)S(1)} %get-tuple-element.58), channel_id=1, source_target_pairs={{0,1},{1,0},{2,7},{3,2},{4,5},{5,4},{6,3},{7,6},{8,9},{9,8},{10,15... | collective-permute-start | bytes 294920 | tf_op jit(solution)/shard_map/ppermute | solution.py:106
  23.1 2.6 %collective-permute-done.20.refs_1_ = f32[192,128]{1,0:T(8,128)S(1)} collective-permute-done((f32[192,128]{1,0:T(8,128)S(1)}, f32[192,128]{1,0:T(8,128)S(1)}, u32[]{:S(2)}, u32[]{:S(2)}) %collective-permute-start.20) | collective-permute-done | bytes 98336 | tf_op jit(solution)/shard_map/ppermute | solution.py:106
  25.8 1.0 %collective-permute-done.21.refs_2_ = f32[192,128]{1,0:T(8,128)S(1)} collective-permute-done((f32[192,128]{1,0:T(8,128)S(1)}, f32[192,128]{1,0:T(8,128)S(1)}, u32[]{:S(2)}, u32[]{:S(2)}) %collective-permute-start.21) | collective-permute-done | bytes 98336 | tf_op jit(solution)/shard_map/ppermute | solution.py:106
  26.8 0.5 %collective-permute-start.23 = (f32[192,128]{1,0:T(8,128)S(1)}, f32[192,128]{1,0:T(8,128)S(1)}, u32[]{:S(2)}, u32[]{:S(2)}) collective-permute-start(f32[192,128]{1,0:T(8,128)S(1)} %get-tuple-element.79), channel_id=1, source_target_pairs={{0,1},{1,0},{2,7},{3,2},{4,5},{5,4},{6,3},{7,6},{8,9},{9,8},{10,15... | collective-permute-start | bytes 294920 | tf_op jit(solution)/shard_map/ppermute | solution.py:106
  27.3 0.0 collective-permute-start.24
  27.4 0.5 %collective-permute-start.11 = (f32[96,128]{1,0:T(8,128)S(1)}, f32[96,128]{1,0:T(8,128)S(1)}, u32[]{:S(2)}, u32[]{:S(2)}) collective-permute-start(f32[96,128]{1,0:T(8,128)S(1)} %get-tuple-element.60), channel_id=1, source_target_pairs={{0,1},{1,2},{2,3},{3,0},{4,5},{5,6},{6,7},{7,4},{8,9},{9,10},{10,1... | collective-permute-start | bytes 147464 | tf_op jit(solution)/shard_map/ppermute | solution.py:106
  27.8 3.7 %collective-permute-start.12 = (f32[96,128]{1,0:T(8,128)S(1)}, f32[96,128]{1,0:T(8,128)S(1)}, u32[]{:S(2)}, u32[]{:S(2)}) collective-permute-start(f32[96,128]{1,0:T(8,128)S(1)} %get-tuple-element.61), channel_id=1, source_target_pairs={{0,3},{1,0},{2,18},{3,1},{4,7},{5,4},{6,22},{7,5},{8,11},{9,8},{10... | collective-permute-start | bytes 147464 | tf_op jit(solution)/shard_map/ppermute | solution.py:106
  31.6 0.5 %collective-permute-start.25 = (f32[96,128]{1,0:T(8,128)S(1)}, f32[96,128]{1,0:T(8,128)S(1)}, u32[]{:S(2)}, u32[]{:S(2)}) collective-permute-start(f32[96,128]{1,0:T(8,128)S(1)} %get-tuple-element.83), channel_id=1, source_target_pairs={{0,1},{1,2},{2,3},{3,0},{4,5},{5,6},{6,7},{7,4},{8,9},{9,10},{10,1... | collective-permute-start | bytes 147464 | tf_op jit(solution)/shard_map/ppermute | solution.py:106
  32.1 2.9 %collective-permute-start.26 = (f32[96,128]{1,0:T(8,128)S(1)}, f32[96,128]{1,0:T(8,128)S(1)}, u32[]{:S(2)}, u32[]{:S(2)}) collective-permute-start(f32[96,128]{1,0:T(8,128)S(1)} %get-tuple-element.84), channel_id=1, source_target_pairs={{0,3},{1,0},{2,18},{3,1},{4,7},{5,4},{6,22},{7,5},{8,11},{9,8},{10... | collective-permute-start | bytes 147464 | tf_op jit(solution)/shard_map/ppermute | solution.py:106
  35.0 1.7 %collective-permute-done.25.refs_4_ = f32[96,128]{1,0:T(8,128)S(1)} collective-permute-done((f32[96,128]{1,0:T(8,128)S(1)}, f32[96,128]{1,0:T(8,128)S(1)}, u32[]{:S(2)}, u32[]{:S(2)}) %collective-permute-start.25) | collective-permute-done | bytes 49184 | tf_op jit(solution)/shard_map/ppermute | solution.py:106
  36.7 0.0 collective-permute-done.26.refs_5_
  36.7 0.7 %assemble.1 = f32[2,96,128]{2,1,0:T(8,128)} custom-call(f32[96,128]{1,0:T(8,128)S(1)} %collective-permute-done.11.refs_0_, f32[96,128]{1,0:T(8,128)S(1)} %collective-permute-done.12.refs_1_, f32[96,128]{1,0:T(8,128)S(1)} %collective-permute-done.13.refs_2_, f32[96,128]{1,0:T(8,128)S(1)} %get-tuple-element.63.refs_3_, ...), custom_call_target="tpu_custom_call" | custom-call | tf_op jit(solution)/shard_map/assemble/pallas_call | solution.py:426
  (41 shorter events, 0.1 us)
Async XLA Ops:
  0.0 1.0 %copy-start = (f32[2,192,2,128]{3,2,1,0:T(2,128)S(1)}, f32[2,192,2,128]{3,2,1,0:T(2,128)}, u32[]{:S(2)}) copy-start(f32[2,192,2,128]{3,2,1,0:T(2,128)} %param.3) | copy-start | bytes 1179652
  1.0 8.5 %collective-permute-start = (f32[192,128]{1,0:T(8,128)S(1)}, f32[192,128]{1,0:T(8,128)S(1)}, u32[]{:S(2)}, u32[]{:S(2)}) collective-permute-start(f32[192,128]{1,0:T(8,128)S(1)} %get-tuple-element.46), channel_id=1, source_target_pairs={{0,4},{1,17},{2,3},{3,2},{4,0},{5,21},{6,7},{7,6},{8,12},{9,25},{1... | collective-permute-start | bytes 294920 | tf_op jit(solution)/shard_map/ppermute | solution.py:106
  4.2 5.4 %collective-permute-start.1 = (f32[192,128]{1,0:T(8,128)S(1)}, f32[192,128]{1,0:T(8,128)S(1)}, u32[]{:S(2)}, u32[]{:S(2)}) collective-permute-start(f32[192,128]{1,0:T(8,128)S(1)} %get-tuple-element.47), channel_id=1, source_target_pairs={{0,1},{1,0},{2,3},{3,2},{4,8},{5,21},{6,7},{7,6},{8,4},{9,25},{10,... | collective-permute-start | bytes 294920 | tf_op jit(solution)/shard_map/ppermute | solution.py:106
  4.2 8.5 %collective-permute-start.14 = (f32[192,128]{1,0:T(8,128)S(1)}, f32[192,128]{1,0:T(8,128)S(1)}, u32[]{:S(2)}, u32[]{:S(2)}) collective-permute-start(f32[192,128]{1,0:T(8,128)S(1)} %get-tuple-element.64), channel_id=1, source_target_pairs={{0,4},{1,17},{2,3},{3,2},{4,0},{5,21},{6,7},{7,6},{8,12},{9,25},{1... | collective-permute-start | bytes 294920 | tf_op jit(solution)/shard_map/ppermute | solution.py:106
  7.3 5.4 %collective-permute-start.15 = (f32[192,128]{1,0:T(8,128)S(1)}, f32[192,128]{1,0:T(8,128)S(1)}, u32[]{:S(2)}, u32[]{:S(2)}) collective-permute-start(f32[192,128]{1,0:T(8,128)S(1)} %get-tuple-element.65), channel_id=1, source_target_pairs={{0,1},{1,0},{2,3},{3,2},{4,8},{5,21},{6,7},{7,6},{8,4},{9,25},{10,... | collective-permute-start | bytes 294920 | tf_op jit(solution)/shard_map/ppermute | solution.py:106
  10.7 4.6 %collective-permute-start.2 = (f32[384,128]{1,0:T(8,128)S(1)}, f32[384,128]{1,0:T(8,128)S(1)}, u32[]{:S(2)}, u32[]{:S(2)}) collective-permute-start(f32[384,128]{1,0:T(8,128)S(1)} %get-tuple-element.51), channel_id=1, source_target_pairs={{0,1},{1,0},{2,3},{3,2},{4,5},{5,4},{6,7},{7,6},{8,9},{9,8},{10,11... | collective-permute-start | bytes 589832 | tf_op jit(solution)/shard_map/ppermute | solution.py:106
  10.8 4.5 %collective-permute-start.3 = (f32[192,128]{1,0:T(8,128)S(1)}, f32[192,128]{1,0:T(8,128)S(1)}, u32[]{:S(2)}, u32[]{:S(2)}) collective-permute-start(f32[192,128]{1,0:T(8,128)S(1)} %get-tuple-element.52), channel_id=1, source_target_pairs={{0,5},{1,0},{2,3},{3,2},{4,1},{5,4},{6,7},{7,6},{8,13},{9,8},{10,1... | collective-permute-start | bytes 294920 | tf_op jit(solution)/shard_map/ppermute | solution.py:106
  12.0 3.4 %collective-permute-start.4 = (f32[192,128]{1,0:T(8,128)S(1)}, f32[192,128]{1,0:T(8,128)S(1)}, u32[]{:S(2)}, u32[]{:S(2)}) collective-permute-start(f32[192,128]{1,0:T(8,128)S(1)} %get-tuple-element.53), channel_id=1, source_target_pairs={{0,1},{1,0},{2,3},{3,2},{4,9},{5,4},{6,7},{7,6},{8,5},{9,8},{10,11... | collective-permute-start | bytes 294920 | tf_op jit(solution)/shard_map/ppermute | solution.py:106
  13.8 4.9 %collective-permute-start.16 = (f32[384,128]{1,0:T(8,128)S(1)}, f32[384,128]{1,0:T(8,128)S(1)}, u32[]{:S(2)}, u32[]{:S(2)}) collective-permute-start(f32[384,128]{1,0:T(8,128)S(1)} %get-tuple-element.68), channel_id=1, source_target_pairs={{0,1},{1,0},{2,3},{3,2},{4,5},{5,4},{6,7},{7,6},{8,9},{9,8},{10,11... | collective-permute-start | bytes 589832 | tf_op jit(solution)/shard_map/ppermute | solution.py:106
  13.9 3.6 %collective-permute-start.17 = (f32[192,128]{1,0:T(8,128)S(1)}, f32[192,128]{1,0:T(8,128)S(1)}, u32[]{:S(2)}, u32[]{:S(2)}) collective-permute-start(f32[192,128]{1,0:T(8,128)S(1)} %get-tuple-element.69), channel_id=1, source_target_pairs={{0,5},{1,0},{2,3},{3,2},{4,1},{5,4},{6,7},{7,6},{8,13},{9,8},{10,1... | collective-permute-start | bytes 294920 | tf_op jit(solution)/shard_map/ppermute | solution.py:106
  15.3 3.4 %collective-permute-start.18 = (f32[192,128]{1,0:T(8,128)S(1)}, f32[192,128]{1,0:T(8,128)S(1)}, u32[]{:S(2)}, u32[]{:S(2)}) collective-permute-start(f32[192,128]{1,0:T(8,128)S(1)} %get-tuple-element.70), channel_id=1, source_target_pairs={{0,1},{1,0},{2,3},{3,2},{4,9},{5,4},{6,7},{7,6},{8,5},{9,8},{10,11... | collective-permute-start | bytes 294920 | tf_op jit(solution)/shard_map/ppermute | solution.py:106
  15.3 7.3 %collective-permute-start.5 = (f32[384,128]{1,0:T(8,128)S(1)}, f32[384,128]{1,0:T(8,128)S(1)}, u32[]{:S(2)}, u32[]{:S(2)}) collective-permute-start(f32[384,128]{1,0:T(8,128)S(1)} %get-tuple-element.54), channel_id=1, source_target_pairs={{0,1},{1,2},{2,3},{3,0},{4,5},{5,6},{6,7},{7,4},{8,9},{9,10},{10,1... | collective-permute-start | bytes 589832 | tf_op jit(solution)/shard_map/ppermute | solution.py:106
  16.9 4.6 %collective-permute-start.6 = (f32[192,128]{1,0:T(8,128)S(1)}, f32[192,128]{1,0:T(8,128)S(1)}, u32[]{:S(2)}, u32[]{:S(2)}) collective-permute-start(f32[192,128]{1,0:T(8,128)S(1)} %get-tuple-element.55), channel_id=1, source_target_pairs={{0,1},{1,6},{2,3},{3,0},{4,5},{5,2},{6,7},{7,4},{8,9},{9,14},{10,1... | collective-permute-start | bytes 294920 | tf_op jit(solution)/shard_map/ppermute | solution.py:106
  17.5 5.1 %collective-permute-start.7 = (f32[192,128]{1,0:T(8,128)S(1)}, f32[192,128]{1,0:T(8,128)S(1)}, u32[]{:S(2)}, u32[]{:S(2)}) collective-permute-start(f32[192,128]{1,0:T(8,128)S(1)} %get-tuple-element.56), channel_id=1, source_target_pairs={{0,1},{1,2},{2,3},{3,0},{4,5},{5,10},{6,7},{7,4},{8,9},{9,6},{10,1... | collective-permute-start | bytes 294920 | tf_op jit(solution)/shard_map/ppermute | solution.py:106
  18.7 8.1 %collective-permute-start.19 = (f32[384,128]{1,0:T(8,128)S(1)}, f32[384,128]{1,0:T(8,128)S(1)}, u32[]{:S(2)}, u32[]{:S(2)}) collective-permute-start(f32[384,128]{1,0:T(8,128)S(1)} %get-tuple-element.73), channel_id=1, source_target_pairs={{0,1},{1,2},{2,3},{3,0},{4,5},{5,6},{6,7},{7,4},{8,9},{9,10},{10,1... | collective-permute-start | bytes 589832 | tf_op jit(solution)/shard_map/ppermute | solution.py:106
  19.9 5.9 %collective-permute-start.20 = (f32[192,128]{1,0:T(8,128)S(1)}, f32[192,128]{1,0:T(8,128)S(1)}, u32[]{:S(2)}, u32[]{:S(2)}) collective-permute-start(f32[192,128]{1,0:T(8,128)S(1)} %get-tuple-element.74), channel_id=1, source_target_pairs={{0,1},{1,6},{2,3},{3,0},{4,5},{5,2},{6,7},{7,4},{8,9},{9,14},{10,1... | collective-permute-start | bytes 294920 | tf_op jit(solution)/shard_map/ppermute | solution.py:106
  21.5 5.3 %collective-permute-start.21 = (f32[192,128]{1,0:T(8,128)S(1)}, f32[192,128]{1,0:T(8,128)S(1)}, u32[]{:S(2)}, u32[]{:S(2)}) collective-permute-start(f32[192,128]{1,0:T(8,128)S(1)} %get-tuple-element.75), channel_id=1, source_target_pairs={{0,1},{1,2},{2,3},{3,0},{4,5},{5,10},{6,7},{7,4},{8,9},{9,6},{10,1... | collective-permute-start | bytes 294920 | tf_op jit(solution)/shard_map/ppermute | solution.py:106
  22.6 4.8 %collective-permute-start.8 = (f32[384,128]{1,0:T(8,128)S(1)}, f32[384,128]{1,0:T(8,128)S(1)}, u32[]{:S(2)}, u32[]{:S(2)}) collective-permute-start(f32[384,128]{1,0:T(8,128)S(1)} %get-tuple-element.57), channel_id=1, source_target_pairs={{0,1},{1,0},{2,3},{3,2},{4,5},{5,4},{6,7},{7,6},{8,9},{9,8},{10,11... | collective-permute-start | bytes 589832 | tf_op jit(solution)/shard_map/ppermute | solution.py:106
  22.6 4.7 %collective-permute-start.9 = (f32[192,128]{1,0:T(8,128)S(1)}, f32[192,128]{1,0:T(8,128)S(1)}, u32[]{:S(2)}, u32[]{:S(2)}) collective-permute-start(f32[192,128]{1,0:T(8,128)S(1)} %get-tuple-element.58), channel_id=1, source_target_pairs={{0,1},{1,0},{2,7},{3,2},{4,5},{5,4},{6,3},{7,6},{8,9},{9,8},{10,15... | collective-permute-start | bytes 294920 | tf_op jit(solution)/shard_map/ppermute | solution.py:106
  25.8 1.6 %collective-permute-start.10 = (f32[192,128]{1,0:T(8,128)S(1)}, f32[192,128]{1,0:T(8,128)S(1)}, u32[]{:S(2)}, u32[]{:S(2)}) collective-permute-start(f32[192,128]{1,0:T(8,128)S(1)} %get-tuple-element.59), channel_id=1, source_target_pairs={{0,1},{1,0},{2,3},{3,2},{4,5},{5,4},{6,11},{7,6},{8,9},{9,8},{10,7... | collective-permute-start | bytes 294920 | tf_op jit(solution)/shard_map/ppermute | solution.py:106
  26.8 4.8 %collective-permute-start.22 = (f32[384,128]{1,0:T(8,128)S(1)}, f32[384,128]{1,0:T(8,128)S(1)}, u32[]{:S(2)}, u32[]{:S(2)}) collective-permute-start(f32[384,128]{1,0:T(8,128)S(1)} %get-tuple-element.78), channel_id=1, source_target_pairs={{0,1},{1,0},{2,3},{3,2},{4,5},{5,4},{6,7},{7,6},{8,9},{9,8},{10,11... | collective-permute-start | bytes 589832 | tf_op jit(solution)/shard_map/ppermute | solution.py:106
  26.8 4.8 %collective-permute-start.23 = (f32[192,128]{1,0:T(8,128)S(1)}, f32[192,128]{1,0:T(8,128)S(1)}, u32[]{:S(2)}, u32[]{:S(2)}) collective-permute-start(f32[192,128]{1,0:T(8,128)S(1)} %get-tuple-element.79), channel_id=1, source_target_pairs={{0,1},{1,0},{2,7},{3,2},{4,5},{5,4},{6,3},{7,6},{8,9},{9,8},{10,15... | collective-permute-start | bytes 294920 | tf_op jit(solution)/shard_map/ppermute | solution.py:106
  27.3 4.3 %collective-permute-start.24 = (f32[192,128]{1,0:T(8,128)S(1)}, f32[192,128]{1,0:T(8,128)S(1)}, u32[]{:S(2)}, u32[]{:S(2)}) collective-permute-start(f32[192,128]{1,0:T(8,128)S(1)} %get-tuple-element.80), channel_id=1, source_target_pairs={{0,1},{1,0},{2,3},{3,2},{4,5},{5,4},{6,11},{7,6},{8,9},{9,8},{10,7... | collective-permute-start | bytes 294920 | tf_op jit(solution)/shard_map/ppermute | solution.py:106
  27.4 7.6 %collective-permute-start.11 = (f32[96,128]{1,0:T(8,128)S(1)}, f32[96,128]{1,0:T(8,128)S(1)}, u32[]{:S(2)}, u32[]{:S(2)}) collective-permute-start(f32[96,128]{1,0:T(8,128)S(1)} %get-tuple-element.60), channel_id=1, source_target_pairs={{0,1},{1,2},{2,3},{3,0},{4,5},{5,6},{6,7},{7,4},{8,9},{9,10},{10,1... | collective-permute-start | bytes 147464 | tf_op jit(solution)/shard_map/ppermute | solution.py:106
  27.8 7.2 %collective-permute-start.12 = (f32[96,128]{1,0:T(8,128)S(1)}, f32[96,128]{1,0:T(8,128)S(1)}, u32[]{:S(2)}, u32[]{:S(2)}) collective-permute-start(f32[96,128]{1,0:T(8,128)S(1)} %get-tuple-element.61), channel_id=1, source_target_pairs={{0,3},{1,0},{2,18},{3,1},{4,7},{5,4},{6,22},{7,5},{8,11},{9,8},{10... | collective-permute-start | bytes 147464 | tf_op jit(solution)/shard_map/ppermute | solution.py:106
  31.6 3.4 %collective-permute-start.13 = (f32[96,128]{1,0:T(8,128)S(1)}, f32[96,128]{1,0:T(8,128)S(1)}, u32[]{:S(2)}, u32[]{:S(2)}) collective-permute-start(f32[96,128]{1,0:T(8,128)S(1)} %get-tuple-element.62), channel_id=1, source_target_pairs={{0,1},{1,0},{2,3},{3,2},{4,5},{5,4},{6,7},{7,6},{8,9},{9,8},{10,11... | collective-permute-start | bytes 147464 | tf_op jit(solution)/shard_map/ppermute | solution.py:106
  31.6 5.0 %collective-permute-start.25 = (f32[96,128]{1,0:T(8,128)S(1)}, f32[96,128]{1,0:T(8,128)S(1)}, u32[]{:S(2)}, u32[]{:S(2)}) collective-permute-start(f32[96,128]{1,0:T(8,128)S(1)} %get-tuple-element.83), channel_id=1, source_target_pairs={{0,1},{1,2},{2,3},{3,0},{4,5},{5,6},{6,7},{7,4},{8,9},{9,10},{10,1... | collective-permute-start | bytes 147464 | tf_op jit(solution)/shard_map/ppermute | solution.py:106
  32.1 4.6 %collective-permute-start.26 = (f32[96,128]{1,0:T(8,128)S(1)}, f32[96,128]{1,0:T(8,128)S(1)}, u32[]{:S(2)}, u32[]{:S(2)}) collective-permute-start(f32[96,128]{1,0:T(8,128)S(1)} %get-tuple-element.84), channel_id=1, source_target_pairs={{0,3},{1,0},{2,18},{3,1},{4,7},{5,4},{6,22},{7,5},{8,11},{9,8},{10... | collective-permute-start | bytes 147464 | tf_op jit(solution)/shard_map/ppermute | solution.py:106
  35.0 1.8 %collective-permute-start.27 = (f32[96,128]{1,0:T(8,128)S(1)}, f32[96,128]{1,0:T(8,128)S(1)}, u32[]{:S(2)}, u32[]{:S(2)}) collective-permute-start(f32[96,128]{1,0:T(8,128)S(1)} %get-tuple-element.85), channel_id=1, source_target_pairs={{0,1},{1,0},{2,3},{3,2},{4,5},{5,4},{6,7},{7,6},{8,9},{9,8},{10,11... | collective-permute-start | bytes 147464 | tf_op jit(solution)/shard_map/ppermute | solution.py:106

commit v4 on v3

--- a/solution.py
+++ b/solution.py
@@ -121,7 +121,7 @@
     first = 9 * (3 - steps)
     groups = [(k, min(2, 9 - k)) for k in range(0, 9, 2)]
 
-    def kernel(weight_ref, gain_ref, high, low, gains, staged, row, sems, gain_sem):
+    def kernel(weight_ref, gain_ref, both, gains, staged, row, sems, gain_sem):
         gain_copy = pltpu.make_async_copy(gain_ref, row, gain_sem)
         gain_copy.start()
         copies = {}
@@ -144,8 +144,9 @@
                     parts.append(jnp.zeros((channels, extra), jnp.float32))
                     span += extra
                 upper, lower = split(jnp.concatenate(parts, axis=1))
-                high[a, :, k * channels : k * channels + span] = upper
-                low[a, :, k * channels : k * channels + span] = lower
+                cols = slice(k * channels, k * channels + span)
+                both[a, :channels, cols] = upper
+                both[a, channels:, cols] = lower
         gain_copy.wait()
         square = (channels, channels)
         lane = lax.broadcasted_iota(jnp.int32, square, 1)
@@ -154,16 +155,15 @@
         column = jnp.sum(jnp.where(lane == sublane, spread, 0.0), axis=1, keepdims=True)
         gains[...] = jnp.broadcast_to(column, (channels, width))
 
-    shape = (steps, channels, depth)
+    shape = (steps, 2 * channels, depth)
     return pl.pallas_call(
         kernel,
         out_shape=(
             held(shape, jnp.bfloat16),
-            held(shape, jnp.bfloat16),
             held((channels, width)),
         ),
         in_specs=[HBM, HBM],
-        out_specs=(VMEM, VMEM, VMEM),
+        out_specs=(VMEM, VMEM),
         scratch_shapes=[
             pltpu.VMEM((9 * steps, channels, channels), jnp.float32),
             pltpu.VMEM(gain.shape, jnp.float32),
@@ -216,25 +216,27 @@
     return jnp.where(lane == width - 1, 0.0, pltpu.roll(values, width - 1, 1))
 
 
-def product(high, low, patch_high, patch_low):
+def product(both, patch_high, patch_low):
     def dot(a, b):
         return jnp.dot(a, b, preferred_element_type=jnp.float32)
 
-    return dot(high, patch_high) + dot(low, patch_high) + dot(high, patch_low)
+    channels = both.shape[0] // 2
+    first = dot(both, patch_high)
+    return first[:channels] + first[channels:] + dot(both[:channels], patch_low)
 
 
 def frame_step(layer, tiles, sections, main, frame, near_a, near_b, gain, weights, partial, keep):
     channels, width = near_a.shape[-2:]
     lines = main.shape[-2]
     rows = lines // channels
-    steps, _, depth = weights[0].shape
+    steps, _, depth = weights.shape
     last = layer == sections - 1
     share = lines // sections
     count = sections if last else 3
 
     def kernel(*refs):
-        main_ref, a_ref, b_ref, gain_ref, high_ref, low_ref = refs[:6]
-        refs = refs[6:]
+        main_ref, a_ref, b_ref, gain_ref, both_ref = refs[:5]
+        refs = refs[5:]
         if partial is not None:
             partial_ref, refs = refs[0], refs[1:]
         outs, (patch_high, patch_low) = refs[:count], refs[count:]
@@ -268,9 +270,7 @@
                             cols = slice(r * width, (r + 1) * width)
                             patch_high[k : k + channels, cols] = upper
                             patch_low[k : k + channels, cols] = lower
-            total = product(
-                high_ref[steps - 1], low_ref[steps - 1], patch_high[...], patch_low[...]
-            )
+            total = product(both_ref[steps - 1], patch_high[...], patch_low[...])
             if partial is not None:
                 total = total + partial_ref[...]
             results = [
@@ -289,7 +289,7 @@
                 outs[1][...] = jnp.where(even, results[-1], results[0])
                 outs[2][...] = jnp.where(even, results[0], results[-1])
 
-    operands = [main, near_a, near_b, gain, *weights]
+    operands = [main, near_a, near_b, gain, weights]
     if partial is not None:
         operands.append(partial)
     if last:
@@ -320,11 +320,11 @@
 
 
 def earlier_frames(layer, weights, patches):
-    steps, channels, depth = weights[0].shape
+    steps, channels, depth = weights.shape[0], weights.shape[1] // 2, weights.shape[2]
     count = len(patches)
     columns = patches[0][0].shape[1]
 
-    def kernel(high_ref, low_ref, *refs):
+    def kernel(both_ref, *refs):
         out_ref = refs[-1]
 
         @pl.when(lax.axis_index("section") == layer)
@@ -332,13 +332,11 @@
             total = None
             for n in range(count):
                 a = steps - 1 - (count - n)
-                term = product(
-                    high_ref[a], low_ref[a], refs[2 * n][...], refs[2 * n + 1][...]
-                )
+                term = product(both_ref[a], refs[2 * n][...], refs[2 * n + 1][...])
                 total = term if total is None else total + term
             out_ref[...] = total
 
-    operands = [*weights]
+    operands = [weights]
     for pair in patches:
         operands += list(pair)
     return pl.pallas_call(
@@ -371,7 +369,7 @@
     rim_a, rim_b = (rim_pairs(shape, of) for of in (of_a, of_b))
     near_a = [send(edge_a[f], rim_a) for f in range(frames)]
     near_b = [send(edge_b[f], rim_b) for f in range(frames)]
-    *weights, gains = prepare(conv_weight[0], gain, steps, depth, width)
+    weights, gains = prepare(conv_weight[0], gain, steps, depth, width)
     main = [flat] * frames
 
     for layer in range(sections):

time: 37.6 us -> 37.2 us (0.989)
  starting transfers between devices: 21.8 us -> 21.3 us
    ppermute x28, starting transfers between devices: 21.8 us -> 21.3 us  [send(): return lax.ppermute(value, ('groups', 'tiles', 'section'), pairs)]
where the time goes in v4:
time: 37.2 us; the launch traced here: 36.9 us
  starting transfers between devices  21.3 us (57%)
  waiting for transfers between devices  8.74 us (23%)
  Pallas kernels  5.71 us (15%)
  local copies, waits for them, and re-layouts  1 us (3%)
    ppermute x28, starting transfers between devices, send(): return lax.ppermute(value, ('groups', 'tiles', 'section'), pairs)  21.3 us
    ppermute x28, waiting for transfers between devices, send(): return lax.ppermute(value, ('groups', 'tiles', 'section'), pairs)  8.74 us
    pallas_call x1, Pallas kernels, prepare(): pl.pallas_call(kernel, out_shape=(held(shape, jnp.bfloat16), held((channe...  2.25 us
    pallas_call x8, Pallas kernels, frame_step(): pl.pallas_call(kernel, out_shape=tuple(out_shape), in_specs=[VMEM] * len(...  2.06 us
    unnamed x2, local copies, waits for them, and re-layouts  1 us
  transfers between devices with their start and end apart: 28, of which 6 were waited for; matrix products, arithmetic and copies ran while one was open for 0% of the time, Pallas kernels for 14%

profile of v4, /device:TPU:0, one launch (start us, length us, event | category | flops | bytes accessed | tf_op | source)
XLA Modules:
  0.0 36.9 jit_solution(15804921625756283126)
XLA Ops:
  0.0 1.0 %copy-done = f32[2,192,2,128]{3,2,1,0:T(2,128)S(1)} copy-done((f32[2,192,2,128]{3,2,1,0:T(2,128)S(1)}, f32[2,192,2,128]{3,2,1,0:T(2,128)}, u32[]{:S(2)}) %copy-start) | copy-done | bytes 393240
  1.0 3.1 %collective-permute-start = (f32[192,128]{1,0:T(8,128)S(1)}, f32[192,128]{1,0:T(8,128)S(1)}, u32[]{:S(2)}, u32[]{:S(2)}) collective-permute-start(f32[192,128]{1,0:T(8,128)S(1)} %get-tuple-element.45), channel_id=1, source_target_pairs={{0,4},{1,17},{2,3},{3,2},{4,0},{5,21},{6,7},{7,6},{8,12},{9,25},{1... | collective-permute-start | bytes 294920 | tf_op jit(solution)/shard_map/ppermute | solution.py:106
  4.2 3.1 %collective-permute-start.14 = (f32[192,128]{1,0:T(8,128)S(1)}, f32[192,128]{1,0:T(8,128)S(1)}, u32[]{:S(2)}, u32[]{:S(2)}) collective-permute-start(f32[192,128]{1,0:T(8,128)S(1)} %get-tuple-element.62), channel_id=1, source_target_pairs={{0,4},{1,17},{2,3},{3,2},{4,0},{5,21},{6,7},{7,6},{8,12},{9,25},{1... | collective-permute-start | bytes 294920 | tf_op jit(solution)/shard_map/ppermute | solution.py:106
  7.3 2.3 %prepare.1 = (bf16[2,384,1792]{2,1,0:T(8,128)(2,1)S(1)}, f32[192,128]{1,0:T(8,128)S(1)}) custom-call(f32[27,192,192]{2,1,0:T(8,128)} %bitcast.6, f32[1,192]{1,0:T(1,128)} %gain_ref.1), custom_call_target="tpu_custom_call" | custom-call | tf_op jit(solution)/shard_map/prepare/pallas_call | solution.py:159
  9.6 1.0 %frame_step.8 = (f32[384,128]{1,0:T(8,128)S(1)}, f32[192,128]{1,0:T(8,128)S(1)}, f32[192,128]{1,0:T(8,128)S(1)}, bf16[1792,256]{1,0:T(8,128)(2,1)S(1)}, bf16[1792,256]{1,0:T(8,128)(2,1)S(1)}) custom-call(f32[2,384,128]{2,1,0:T(8,128)S(1)} %bitcast.4, f32[192,128]{1,0:T(8,128)S(1)} %collective-permute-done.refs_1_, ...), custom_call_target="tpu_custom_call" | custom-call | flops 528482304 | bytes 1048576 | tf_op jit(solution)/shard_map/frame_step/pallas_call | solution.py:306
  10.6 0.1 collective-permute-start.2
  10.7 1.2 %collective-permute-start.3 = (f32[192,128]{1,0:T(8,128)S(1)}, f32[192,128]{1,0:T(8,128)S(1)}, u32[]{:S(2)}, u32[]{:S(2)}) collective-permute-start(f32[192,128]{1,0:T(8,128)S(1)} %get-tuple-element.50), channel_id=1, source_target_pairs={{0,5},{1,0},{2,3},{3,2},{4,1},{5,4},{6,7},{7,6},{8,13},{9,8},{10,1... | collective-permute-start | bytes 294920 | tf_op jit(solution)/shard_map/ppermute | solution.py:106
  11.9 0.7 %earlier_frames.4.refs_5_ = f32[192,256]{1,0:T(8,128)S(1)} custom-call(bf16[2,384,1792]{2,1,0:T(8,128)(2,1)S(1)} %get-tuple-element.48.refs_4_.both_ref, bf16[1792,256]{1,0:T(8,128)(2,1)S(1)} %get-tuple-element.64.refs_0_, bf16[1792,256]{1,0:T(8,128)(2,1)S(1)} %get-tuple-element.65.refs_1_), custom_call_target="tpu_custom_call" | custom-call | flops 528482304 | bytes 1048576 | tf_op jit(solution)/shard_map/earlier_frames/pallas_call | solution.py:342
  12.6 1.0 %frame_step.12 = (f32[384,128]{1,0:T(8,128)S(1)}, f32[192,128]{1,0:T(8,128)S(1)}, f32[192,128]{1,0:T(8,128)S(1)}) custom-call(f32[2,384,128]{2,1,0:T(8,128)S(1)} %bitcast.5, f32[192,128]{1,0:T(8,128)S(1)} %collective-permute-done.14.refs_1_, f32[192,128]{1,0:T(8,128)S(1)} %collective-permute-done.15.refs_2_, f32[192,128]{1,0:T(8,128)S(1)} %get-tuple-element.47.refs_3_, ...), custom_call_target="tpu_custom_call" | custom-call | flops 528482304 | bytes 1048576 | tf_op jit(solution)/shard_map/frame_step/pallas_call | solution.py:306
  13.6 0.1 collective-permute-start.16
  13.7 1.4 %collective-permute-start.17 = (f32[192,128]{1,0:T(8,128)S(1)}, f32[192,128]{1,0:T(8,128)S(1)}, u32[]{:S(2)}, u32[]{:S(2)}) collective-permute-start(f32[192,128]{1,0:T(8,128)S(1)} %get-tuple-element.67), channel_id=1, source_target_pairs={{0,5},{1,0},{2,3},{3,2},{4,1},{5,4},{6,7},{7,6},{8,13},{9,8},{10,1... | collective-permute-start | bytes 294920 | tf_op jit(solution)/shard_map/ppermute | solution.py:106
  15.1 0.1 collective-permute-start.18
  15.2 1.5 %collective-permute-start.5 = (f32[384,128]{1,0:T(8,128)S(1)}, f32[384,128]{1,0:T(8,128)S(1)}, u32[]{:S(2)}, u32[]{:S(2)}) collective-permute-start(f32[384,128]{1,0:T(8,128)S(1)} %get-tuple-element.52), channel_id=1, source_target_pairs={{0,1},{1,2},{2,3},{3,0},{4,5},{5,6},{6,7},{7,4},{8,9},{9,10},{10,1... | collective-permute-start | bytes 589832 | tf_op jit(solution)/shard_map/ppermute | solution.py:106
  16.7 0.1 collective-permute-start.6
  16.8 0.6 %collective-permute-done.17.refs_1_ = f32[192,128]{1,0:T(8,128)S(1)} collective-permute-done((f32[192,128]{1,0:T(8,128)S(1)}, f32[192,128]{1,0:T(8,128)S(1)}, u32[]{:S(2)}, u32[]{:S(2)}) %collective-permute-start.17) | collective-permute-done | bytes 98336 | tf_op jit(solution)/shard_map/ppermute | solution.py:106
  17.3 1.3 %collective-permute-start.7 = (f32[192,128]{1,0:T(8,128)S(1)}, f32[192,128]{1,0:T(8,128)S(1)}, u32[]{:S(2)}, u32[]{:S(2)}) collective-permute-start(f32[192,128]{1,0:T(8,128)S(1)} %get-tuple-element.54), channel_id=1, source_target_pairs={{0,1},{1,2},{2,3},{3,0},{4,5},{5,10},{6,7},{7,4},{8,9},{9,6},{10,1... | collective-permute-start | bytes 294920 | tf_op jit(solution)/shard_map/ppermute | solution.py:106
  18.6 1.1 %collective-permute-start.19 = (f32[384,128]{1,0:T(8,128)S(1)}, f32[384,128]{1,0:T(8,128)S(1)}, u32[]{:S(2)}, u32[]{:S(2)}) collective-permute-start(f32[384,128]{1,0:T(8,128)S(1)} %get-tuple-element.71), channel_id=1, source_target_pairs={{0,1},{1,2},{2,3},{3,0},{4,5},{5,6},{6,7},{7,4},{8,9},{9,10},{10,1... | collective-permute-start | bytes 589832 | tf_op jit(solution)/shard_map/ppermute | solution.py:106
  19.7 0.1 collective-permute-start.20
  19.8 1.6 %collective-permute-done.6.refs_1_ = f32[192,128]{1,0:T(8,128)S(1)} collective-permute-done((f32[192,128]{1,0:T(8,128)S(1)}, f32[192,128]{1,0:T(8,128)S(1)}, u32[]{:S(2)}, u32[]{:S(2)}) %collective-permute-start.6) | collective-permute-done | bytes 98336 | tf_op jit(solution)/shard_map/ppermute | solution.py:106
  21.4 1.1 %collective-permute-done.7.refs_2_ = f32[192,128]{1,0:T(8,128)S(1)} collective-permute-done((f32[192,128]{1,0:T(8,128)S(1)}, f32[192,128]{1,0:T(8,128)S(1)}, u32[]{:S(2)}, u32[]{:S(2)}) %collective-permute-start.7) | collective-permute-done | bytes 98336 | tf_op jit(solution)/shard_map/ppermute | solution.py:106
  22.5 0.5 %collective-permute-start.9 = (f32[192,128]{1,0:T(8,128)S(1)}, f32[192,128]{1,0:T(8,128)S(1)}, u32[]{:S(2)}, u32[]{:S(2)}) collective-permute-start(f32[192,128]{1,0:T(8,128)S(1)} %get-tuple-element.56), channel_id=1, source_target_pairs={{0,1},{1,0},{2,7},{3,2},{4,5},{5,4},{6,3},{7,6},{8,9},{9,8},{10,15... | collective-permute-start | bytes 294920 | tf_op jit(solution)/shard_map/ppermute | solution.py:106
  23.0 2.6 %collective-permute-done.20.refs_1_ = f32[192,128]{1,0:T(8,128)S(1)} collective-permute-done((f32[192,128]{1,0:T(8,128)S(1)}, f32[192,128]{1,0:T(8,128)S(1)}, u32[]{:S(2)}, u32[]{:S(2)}) %collective-permute-start.20) | collective-permute-done | bytes 98336 | tf_op jit(solution)/shard_map/ppermute | solution.py:106
  25.6 1.0 %collective-permute-done.21.refs_2_ = f32[192,128]{1,0:T(8,128)S(1)} collective-permute-done((f32[192,128]{1,0:T(8,128)S(1)}, f32[192,128]{1,0:T(8,128)S(1)}, u32[]{:S(2)}, u32[]{:S(2)}) %collective-permute-start.21) | collective-permute-done | bytes 98336 | tf_op jit(solution)/shard_map/ppermute | solution.py:106
  26.7 0.5 %collective-permute-start.23 = (f32[192,128]{1,0:T(8,128)S(1)}, f32[192,128]{1,0:T(8,128)S(1)}, u32[]{:S(2)}, u32[]{:S(2)}) collective-permute-start(f32[192,128]{1,0:T(8,128)S(1)} %get-tuple-element.77), channel_id=1, source_target_pairs={{0,1},{1,0},{2,7},{3,2},{4,5},{5,4},{6,3},{7,6},{8,9},{9,8},{10,15... | collective-permute-start | bytes 294920 | tf_op jit(solution)/shard_map/ppermute | solution.py:106
  27.2 0.0 collective-permute-start.24
  27.3 0.5 %collective-permute-start.11 = (f32[96,128]{1,0:T(8,128)S(1)}, f32[96,128]{1,0:T(8,128)S(1)}, u32[]{:S(2)}, u32[]{:S(2)}) collective-permute-start(f32[96,128]{1,0:T(8,128)S(1)} %get-tuple-element.58), channel_id=1, source_target_pairs={{0,1},{1,2},{2,3},{3,0},{4,5},{5,6},{6,7},{7,4},{8,9},{9,10},{10,1... | collective-permute-start | bytes 147464 | tf_op jit(solution)/shard_map/ppermute | solution.py:106
  27.7 3.5 %collective-permute-start.12 = (f32[96,128]{1,0:T(8,128)S(1)}, f32[96,128]{1,0:T(8,128)S(1)}, u32[]{:S(2)}, u32[]{:S(2)}) collective-permute-start(f32[96,128]{1,0:T(8,128)S(1)} %get-tuple-element.59), channel_id=1, source_target_pairs={{0,3},{1,0},{2,18},{3,1},{4,7},{5,4},{6,22},{7,5},{8,11},{9,8},{10... | collective-permute-start | bytes 147464 | tf_op jit(solution)/shard_map/ppermute | solution.py:106
  31.2 0.5 %collective-permute-start.25 = (f32[96,128]{1,0:T(8,128)S(1)}, f32[96,128]{1,0:T(8,128)S(1)}, u32[]{:S(2)}, u32[]{:S(2)}) collective-permute-start(f32[96,128]{1,0:T(8,128)S(1)} %get-tuple-element.81), channel_id=1, source_target_pairs={{0,1},{1,2},{2,3},{3,0},{4,5},{5,6},{6,7},{7,4},{8,9},{9,10},{10,1... | collective-permute-start | bytes 147464 | tf_op jit(solution)/shard_map/ppermute | solution.py:106
  31.7 2.8 %collective-permute-start.26 = (f32[96,128]{1,0:T(8,128)S(1)}, f32[96,128]{1,0:T(8,128)S(1)}, u32[]{:S(2)}, u32[]{:S(2)}) collective-permute-start(f32[96,128]{1,0:T(8,128)S(1)} %get-tuple-element.82), channel_id=1, source_target_pairs={{0,3},{1,0},{2,18},{3,1},{4,7},{5,4},{6,22},{7,5},{8,11},{9,8},{10... | collective-permute-start | bytes 147464 | tf_op jit(solution)/shard_map/ppermute | solution.py:106
  34.5 1.7 %collective-permute-done.25.refs_4_ = f32[96,128]{1,0:T(8,128)S(1)} collective-permute-done((f32[96,128]{1,0:T(8,128)S(1)}, f32[96,128]{1,0:T(8,128)S(1)}, u32[]{:S(2)}, u32[]{:S(2)}) %collective-permute-start.25) | collective-permute-done | bytes 49184 | tf_op jit(solution)/shard_map/ppermute | solution.py:106
  36.2 0.0 collective-permute-done.26.refs_5_
  36.3 0.7 %assemble.1 = f32[2,96,128]{2,1,0:T(8,128)} custom-call(f32[96,128]{1,0:T(8,128)S(1)} %collective-permute-done.11.refs_0_, f32[96,128]{1,0:T(8,128)S(1)} %collective-permute-done.12.refs_1_, f32[96,128]{1,0:T(8,128)S(1)} %collective-permute-done.13.refs_2_, f32[96,128]{1,0:T(8,128)S(1)} %get-tuple-element.61.refs_3_, ...), custom_call_target="tpu_custom_call" | custom-call | tf_op jit(solution)/shard_map/assemble/pallas_call | solution.py:424
  (41 shorter events, 0.1 us)
Async XLA Ops:
  0.0 1.0 %copy-start = (f32[2,192,2,128]{3,2,1,0:T(2,128)S(1)}, f32[2,192,2,128]{3,2,1,0:T(2,128)}, u32[]{:S(2)}) copy-start(f32[2,192,2,128]{3,2,1,0:T(2,128)} %param.3) | copy-start | bytes 1179652
  1.0 8.5 %collective-permute-start = (f32[192,128]{1,0:T(8,128)S(1)}, f32[192,128]{1,0:T(8,128)S(1)}, u32[]{:S(2)}, u32[]{:S(2)}) collective-permute-start(f32[192,128]{1,0:T(8,128)S(1)} %get-tuple-element.45), channel_id=1, source_target_pairs={{0,4},{1,17},{2,3},{3,2},{4,0},{5,21},{6,7},{7,6},{8,12},{9,25},{1... | collective-permute-start | bytes 294920 | tf_op jit(solution)/shard_map/ppermute | solution.py:106
  4.2 5.4 %collective-permute-start.1 = (f32[192,128]{1,0:T(8,128)S(1)}, f32[192,128]{1,0:T(8,128)S(1)}, u32[]{:S(2)}, u32[]{:S(2)}) collective-permute-start(f32[192,128]{1,0:T(8,128)S(1)} %get-tuple-element.46), channel_id=1, source_target_pairs={{0,1},{1,0},{2,3},{3,2},{4,8},{5,21},{6,7},{7,6},{8,4},{9,25},{10,... | collective-permute-start | bytes 294920 | tf_op jit(solution)/shard_map/ppermute | solution.py:106
  4.2 8.4 %collective-permute-start.14 = (f32[192,128]{1,0:T(8,128)S(1)}, f32[192,128]{1,0:T(8,128)S(1)}, u32[]{:S(2)}, u32[]{:S(2)}) collective-permute-start(f32[192,128]{1,0:T(8,128)S(1)} %get-tuple-element.62), channel_id=1, source_target_pairs={{0,4},{1,17},{2,3},{3,2},{4,0},{5,21},{6,7},{7,6},{8,12},{9,25},{1... | collective-permute-start | bytes 294920 | tf_op jit(solution)/shard_map/ppermute | solution.py:106
  7.3 5.3 %collective-permute-start.15 = (f32[192,128]{1,0:T(8,128)S(1)}, f32[192,128]{1,0:T(8,128)S(1)}, u32[]{:S(2)}, u32[]{:S(2)}) collective-permute-start(f32[192,128]{1,0:T(8,128)S(1)} %get-tuple-element.63), channel_id=1, source_target_pairs={{0,1},{1,0},{2,3},{3,2},{4,8},{5,21},{6,7},{7,6},{8,4},{9,25},{10,... | collective-permute-start | bytes 294920 | tf_op jit(solution)/shard_map/ppermute | solution.py:106
  10.6 4.6 %collective-permute-start.2 = (f32[384,128]{1,0:T(8,128)S(1)}, f32[384,128]{1,0:T(8,128)S(1)}, u32[]{:S(2)}, u32[]{:S(2)}) collective-permute-start(f32[384,128]{1,0:T(8,128)S(1)} %get-tuple-element.49), channel_id=1, source_target_pairs={{0,1},{1,0},{2,3},{3,2},{4,5},{5,4},{6,7},{7,6},{8,9},{9,8},{10,11... | collective-permute-start | bytes 589832 | tf_op jit(solution)/shard_map/ppermute | solution.py:106
  10.7 4.4 %collective-permute-start.3 = (f32[192,128]{1,0:T(8,128)S(1)}, f32[192,128]{1,0:T(8,128)S(1)}, u32[]{:S(2)}, u32[]{:S(2)}) collective-permute-start(f32[192,128]{1,0:T(8,128)S(1)} %get-tuple-element.50), channel_id=1, source_target_pairs={{0,5},{1,0},{2,3},{3,2},{4,1},{5,4},{6,7},{7,6},{8,13},{9,8},{10,1... | collective-permute-start | bytes 294920 | tf_op jit(solution)/shard_map/ppermute | solution.py:106
  11.9 3.4 %collective-permute-start.4 = (f32[192,128]{1,0:T(8,128)S(1)}, f32[192,128]{1,0:T(8,128)S(1)}, u32[]{:S(2)}, u32[]{:S(2)}) collective-permute-start(f32[192,128]{1,0:T(8,128)S(1)} %get-tuple-element.51), channel_id=1, source_target_pairs={{0,1},{1,0},{2,3},{3,2},{4,9},{5,4},{6,7},{7,6},{8,5},{9,8},{10,11... | collective-permute-start | bytes 294920 | tf_op jit(solution)/shard_map/ppermute | solution.py:106
  13.6 5.0 %collective-permute-start.16 = (f32[384,128]{1,0:T(8,128)S(1)}, f32[384,128]{1,0:T(8,128)S(1)}, u32[]{:S(2)}, u32[]{:S(2)}) collective-permute-start(f32[384,128]{1,0:T(8,128)S(1)} %get-tuple-element.66), channel_id=1, source_target_pairs={{0,1},{1,0},{2,3},{3,2},{4,5},{5,4},{6,7},{7,6},{8,9},{9,8},{10,11... | collective-permute-start | bytes 589832 | tf_op jit(solution)/shard_map/ppermute | solution.py:106
  13.7 3.6 %collective-permute-start.17 = (f32[192,128]{1,0:T(8,128)S(1)}, f32[192,128]{1,0:T(8,128)S(1)}, u32[]{:S(2)}, u32[]{:S(2)}) collective-permute-start(f32[192,128]{1,0:T(8,128)S(1)} %get-tuple-element.67), channel_id=1, source_target_pairs={{0,5},{1,0},{2,3},{3,2},{4,1},{5,4},{6,7},{7,6},{8,13},{9,8},{10,1... | collective-permute-start | bytes 294920 | tf_op jit(solution)/shard_map/ppermute | solution.py:106
  15.1 3.5 %collective-permute-start.18 = (f32[192,128]{1,0:T(8,128)S(1)}, f32[192,128]{1,0:T(8,128)S(1)}, u32[]{:S(2)}, u32[]{:S(2)}) collective-permute-start(f32[192,128]{1,0:T(8,128)S(1)} %get-tuple-element.68), channel_id=1, source_target_pairs={{0,1},{1,0},{2,3},{3,2},{4,9},{5,4},{6,7},{7,6},{8,5},{9,8},{10,11... | collective-permute-start | bytes 294920 | tf_op jit(solution)/shard_map/ppermute | solution.py:106
  15.2 7.2 %collective-permute-start.5 = (f32[384,128]{1,0:T(8,128)S(1)}, f32[384,128]{1,0:T(8,128)S(1)}, u32[]{:S(2)}, u32[]{:S(2)}) collective-permute-start(f32[384,128]{1,0:T(8,128)S(1)} %get-tuple-element.52), channel_id=1, source_target_pairs={{0,1},{1,2},{2,3},{3,0},{4,5},{5,6},{6,7},{7,4},{8,9},{9,10},{10,1... | collective-permute-start | bytes 589832 | tf_op jit(solution)/shard_map/ppermute | solution.py:106
  16.7 4.7 %collective-permute-start.6 = (f32[192,128]{1,0:T(8,128)S(1)}, f32[192,128]{1,0:T(8,128)S(1)}, u32[]{:S(2)}, u32[]{:S(2)}) collective-permute-start(f32[192,128]{1,0:T(8,128)S(1)} %get-tuple-element.53), channel_id=1, source_target_pairs={{0,1},{1,6},{2,3},{3,0},{4,5},{5,2},{6,7},{7,4},{8,9},{9,14},{10,1... | collective-permute-start | bytes 294920 | tf_op jit(solution)/shard_map/ppermute | solution.py:106
  17.3 5.1 %collective-permute-start.7 = (f32[192,128]{1,0:T(8,128)S(1)}, f32[192,128]{1,0:T(8,128)S(1)}, u32[]{:S(2)}, u32[]{:S(2)}) collective-permute-start(f32[192,128]{1,0:T(8,128)S(1)} %get-tuple-element.54), channel_id=1, source_target_pairs={{0,1},{1,2},{2,3},{3,0},{4,5},{5,10},{6,7},{7,4},{8,9},{9,6},{10,1... | collective-permute-start | bytes 294920 | tf_op jit(solution)/shard_map/ppermute | solution.py:106
  18.6 8.1 %collective-permute-start.19 = (f32[384,128]{1,0:T(8,128)S(1)}, f32[384,128]{1,0:T(8,128)S(1)}, u32[]{:S(2)}, u32[]{:S(2)}) collective-permute-start(f32[384,128]{1,0:T(8,128)S(1)} %get-tuple-element.71), channel_id=1, source_target_pairs={{0,1},{1,2},{2,3},{3,0},{4,5},{5,6},{6,7},{7,4},{8,9},{9,10},{10,1... | collective-permute-start | bytes 589832 | tf_op jit(solution)/shard_map/ppermute | solution.py:106
  19.7 5.9 %collective-permute-start.20 = (f32[192,128]{1,0:T(8,128)S(1)}, f32[192,128]{1,0:T(8,128)S(1)}, u32[]{:S(2)}, u32[]{:S(2)}) collective-permute-start(f32[192,128]{1,0:T(8,128)S(1)} %get-tuple-element.72), channel_id=1, source_target_pairs={{0,1},{1,6},{2,3},{3,0},{4,5},{5,2},{6,7},{7,4},{8,9},{9,14},{10,1... | collective-permute-start | bytes 294920 | tf_op jit(solution)/shard_map/ppermute | solution.py:106
  21.4 5.3 %collective-permute-start.21 = (f32[192,128]{1,0:T(8,128)S(1)}, f32[192,128]{1,0:T(8,128)S(1)}, u32[]{:S(2)}, u32[]{:S(2)}) collective-permute-start(f32[192,128]{1,0:T(8,128)S(1)} %get-tuple-element.73), channel_id=1, source_target_pairs={{0,1},{1,2},{2,3},{3,0},{4,5},{5,10},{6,7},{7,4},{8,9},{9,6},{10,1... | collective-permute-start | bytes 294920 | tf_op jit(solution)/shard_map/ppermute | solution.py:106
  22.5 4.8 %collective-permute-start.8 = (f32[384,128]{1,0:T(8,128)S(1)}, f32[384,128]{1,0:T(8,128)S(1)}, u32[]{:S(2)}, u32[]{:S(2)}) collective-permute-start(f32[384,128]{1,0:T(8,128)S(1)} %get-tuple-element.55), channel_id=1, source_target_pairs={{0,1},{1,0},{2,3},{3,2},{4,5},{5,4},{6,7},{7,6},{8,9},{9,8},{10,11... | collective-permute-start | bytes 589832 | tf_op jit(solution)/shard_map/ppermute | solution.py:106
  22.5 4.7 %collective-permute-start.9 = (f32[192,128]{1,0:T(8,128)S(1)}, f32[192,128]{1,0:T(8,128)S(1)}, u32[]{:S(2)}, u32[]{:S(2)}) collective-permute-start(f32[192,128]{1,0:T(8,128)S(1)} %get-tuple-element.56), channel_id=1, source_target_pairs={{0,1},{1,0},{2,7},{3,2},{4,5},{5,4},{6,3},{7,6},{8,9},{9,8},{10,15... | collective-permute-start | bytes 294920 | tf_op jit(solution)/shard_map/ppermute | solution.py:106
  25.6 1.6 %collective-permute-start.10 = (f32[192,128]{1,0:T(8,128)S(1)}, f32[192,128]{1,0:T(8,128)S(1)}, u32[]{:S(2)}, u32[]{:S(2)}) collective-permute-start(f32[192,128]{1,0:T(8,128)S(1)} %get-tuple-element.57), channel_id=1, source_target_pairs={{0,1},{1,0},{2,3},{3,2},{4,5},{5,4},{6,11},{7,6},{8,9},{9,8},{10,7... | collective-permute-start | bytes 294920 | tf_op jit(solution)/shard_map/ppermute | solution.py:106
  26.7 4.5 %collective-permute-start.22 = (f32[384,128]{1,0:T(8,128)S(1)}, f32[384,128]{1,0:T(8,128)S(1)}, u32[]{:S(2)}, u32[]{:S(2)}) collective-permute-start(f32[384,128]{1,0:T(8,128)S(1)} %get-tuple-element.76), channel_id=1, source_target_pairs={{0,1},{1,0},{2,3},{3,2},{4,5},{5,4},{6,7},{7,6},{8,9},{9,8},{10,11... | collective-permute-start | bytes 589832 | tf_op jit(solution)/shard_map/ppermute | solution.py:106
  26.7 4.5 %collective-permute-start.23 = (f32[192,128]{1,0:T(8,128)S(1)}, f32[192,128]{1,0:T(8,128)S(1)}, u32[]{:S(2)}, u32[]{:S(2)}) collective-permute-start(f32[192,128]{1,0:T(8,128)S(1)} %get-tuple-element.77), channel_id=1, source_target_pairs={{0,1},{1,0},{2,7},{3,2},{4,5},{5,4},{6,3},{7,6},{8,9},{9,8},{10,15... | collective-permute-start | bytes 294920 | tf_op jit(solution)/shard_map/ppermute | solution.py:106
  27.2 4.0 %collective-permute-start.24 = (f32[192,128]{1,0:T(8,128)S(1)}, f32[192,128]{1,0:T(8,128)S(1)}, u32[]{:S(2)}, u32[]{:S(2)}) collective-permute-start(f32[192,128]{1,0:T(8,128)S(1)} %get-tuple-element.78), channel_id=1, source_target_pairs={{0,1},{1,0},{2,3},{3,2},{4,5},{5,4},{6,11},{7,6},{8,9},{9,8},{10,7... | collective-permute-start | bytes 294920 | tf_op jit(solution)/shard_map/ppermute | solution.py:106
  27.3 7.2 %collective-permute-start.11 = (f32[96,128]{1,0:T(8,128)S(1)}, f32[96,128]{1,0:T(8,128)S(1)}, u32[]{:S(2)}, u32[]{:S(2)}) collective-permute-start(f32[96,128]{1,0:T(8,128)S(1)} %get-tuple-element.58), channel_id=1, source_target_pairs={{0,1},{1,2},{2,3},{3,0},{4,5},{5,6},{6,7},{7,4},{8,9},{9,10},{10,1... | collective-permute-start | bytes 147464 | tf_op jit(solution)/shard_map/ppermute | solution.py:106
  27.7 6.8 %collective-permute-start.12 = (f32[96,128]{1,0:T(8,128)S(1)}, f32[96,128]{1,0:T(8,128)S(1)}, u32[]{:S(2)}, u32[]{:S(2)}) collective-permute-start(f32[96,128]{1,0:T(8,128)S(1)} %get-tuple-element.59), channel_id=1, source_target_pairs={{0,3},{1,0},{2,18},{3,1},{4,7},{5,4},{6,22},{7,5},{8,11},{9,8},{10... | collective-permute-start | bytes 147464 | tf_op jit(solution)/shard_map/ppermute | solution.py:106
  31.2 3.3 %collective-permute-start.13 = (f32[96,128]{1,0:T(8,128)S(1)}, f32[96,128]{1,0:T(8,128)S(1)}, u32[]{:S(2)}, u32[]{:S(2)}) collective-permute-start(f32[96,128]{1,0:T(8,128)S(1)} %get-tuple-element.60), channel_id=1, source_target_pairs={{0,1},{1,0},{2,3},{3,2},{4,5},{5,4},{6,7},{7,6},{8,9},{9,8},{10,11... | collective-permute-start | bytes 147464 | tf_op jit(solution)/shard_map/ppermute | solution.py:106
  31.2 5.0 %collective-permute-start.25 = (f32[96,128]{1,0:T(8,128)S(1)}, f32[96,128]{1,0:T(8,128)S(1)}, u32[]{:S(2)}, u32[]{:S(2)}) collective-permute-start(f32[96,128]{1,0:T(8,128)S(1)} %get-tuple-element.81), channel_id=1, source_target_pairs={{0,1},{1,2},{2,3},{3,0},{4,5},{5,6},{6,7},{7,4},{8,9},{9,10},{10,1... | collective-permute-start | bytes 147464 | tf_op jit(solution)/shard_map/ppermute | solution.py:106
  31.7 4.5 %collective-permute-start.26 = (f32[96,128]{1,0:T(8,128)S(1)}, f32[96,128]{1,0:T(8,128)S(1)}, u32[]{:S(2)}, u32[]{:S(2)}) collective-permute-start(f32[96,128]{1,0:T(8,128)S(1)} %get-tuple-element.82), channel_id=1, source_target_pairs={{0,3},{1,0},{2,18},{3,1},{4,7},{5,4},{6,22},{7,5},{8,11},{9,8},{10... | collective-permute-start | bytes 147464 | tf_op jit(solution)/shard_map/ppermute | solution.py:106
  34.5 1.8 %collective-permute-start.27 = (f32[96,128]{1,0:T(8,128)S(1)}, f32[96,128]{1,0:T(8,128)S(1)}, u32[]{:S(2)}, u32[]{:S(2)}) collective-permute-start(f32[96,128]{1,0:T(8,128)S(1)} %get-tuple-element.83), channel_id=1, source_target_pairs={{0,1},{1,0},{2,3},{3,2},{4,5},{5,4},{6,7},{7,6},{8,9},{9,8},{10,11... | collective-permute-start | bytes 147464 | tf_op jit(solution)/shard_map/ppermute | solution.py:106

commit v5 on v4

--- a/solution.py
+++ b/solution.py
@@ -116,37 +116,72 @@
     return pltpu.VMEM(shape, dtype)
 
 
-def prepare(weight, gain, steps, depth, width):
-    channels = weight.shape[1]
-    first = 9 * (3 - steps)
-    groups = [(k, min(2, 9 - k)) for k in range(0, 9, 2)]
-
-    def kernel(weight_ref, gain_ref, both, gains, staged, row, sems, gain_sem):
+def tap_groups(channels, depth):
+    groups = []
+    for k in range(0, 9, 2):
+        size = min(2, 9 - k)
+        extra = depth - 9 * channels if k + size == 9 else 0
+        cols = slice(k * channels, (k + size) * channels + extra)
+        groups.append((k, size, cols, extra))
+    return groups
+
+
+def fetch_taps(weight_ref, first, staged, sems, groups):
+    copies = []
+    for n, (k, size, _, _) in enumerate(groups):
+        copies.append(
+            pltpu.make_async_copy(
+                weight_ref.at[pl.ds(first + k, size)],
+                staged.at[pl.ds(k, size)],
+                sems.at[n],
+            )
+        )
+        copies[-1].start()
+    return copies
+
+
+def split_taps(copies, staged, both, groups):
+    channels = staged.shape[1]
+    for copy, (k, size, cols, extra) in zip(copies, groups):
+        copy.wait()
+        parts = [staged[k + n] for n in range(size)]
+        if extra:
+            parts.append(jnp.zeros((channels, extra), jnp.float32))
+        upper, lower = split(jnp.concatenate(parts, axis=1))
+        both[:channels, cols] = upper
+        both[channels:, cols] = lower
+
+
+def in_hbm(value):
+    return pltpu.with_memory_space_constraint(value, pltpu.HBM)
+
+
+def opening(latents, weight, gain, rows, depth):
+    frames, lines, width = latents.shape
+    channels = lines // rows
+    groups = tap_groups(channels, depth)
+
+    def kernel(latent_ref, weight_ref, gain_ref, *refs):
+        held_ref, both, gains = refs[:3]
+        outs = refs[3 : 3 + 2 * frames]
+        staged, row, frame_sems, sems, gain_sem = refs[3 + 2 * frames :]
+        frame_copies = []
+        for f in range(frames):
+            frame_copies.append(
+                pltpu.make_async_copy(latent_ref.at[f], held_ref.at[f], frame_sems.at[f])
+            )
+            frame_copies[-1].start()
+        copies = fetch_taps(weight_ref, 18, staged, sems, groups)
         gain_copy = pltpu.make_async_copy(gain_ref, row, gain_sem)
         gain_copy.start()
-        copies = {}
-        for a in reversed(range(steps)):
-            for n, (k, size) in enumerate(groups):
-                at = 9 * a + k
-                copies[a, k] = pltpu.make_async_copy(
-                    weight_ref.at[pl.ds(first + at, size)],
-                    staged.at[pl.ds(at, size)],
-                    sems.at[a, n],
-                )
-                copies[a, k].start()
-        for a in reversed(range(steps)):
-            for k, size in groups:
-                copies[a, k].wait()
-                parts = [staged[9 * a + k + n] for n in range(size)]
-                span = size * channels
-                if k + size == 9 and depth > 9 * channels:
-                    extra = depth - 9 * channels
-                    parts.append(jnp.zeros((channels, extra), jnp.float32))
-                    span += extra
-                upper, lower = split(jnp.concatenate(parts, axis=1))
-                cols = slice(k * channels, k * channels + span)
-                both[a, :channels, cols] = upper
-                both[a, channels:, cols] = lower
+        even = lax.rem(lax.axis_index("tiles"), 2) == 0
+        for f in range(frames):
+            frame_copies[f].wait()
+            top = held_ref[f, pl.ds(0, channels, stride=rows), :]
+            bottom = held_ref[f, pl.ds(rows - 1, channels, stride=rows), :]
+            outs[2 * f][...] = jnp.where(even, bottom, top)
+            outs[2 * f + 1][...] = jnp.where(even, top, bottom)
+        split_taps(copies, staged, both, groups)
         gain_copy.wait()
         square = (channels, channels)
         lane = lax.broadcasted_iota(jnp.int32, square, 1)
@@ -155,49 +190,48 @@
         column = jnp.sum(jnp.where(lane == sublane, spread, 0.0), axis=1, keepdims=True)
         gains[...] = jnp.broadcast_to(column, (channels, width))
 
-    shape = (steps, 2 * channels, depth)
+    out_shape = [
+        held(latents.shape),
+        held((2 * channels, depth), jnp.bfloat16),
+        held((channels, width)),
+    ] + [held((channels, width))] * (2 * frames)
     return pl.pallas_call(
         kernel,
-        out_shape=(
-            held(shape, jnp.bfloat16),
-            held((channels, width)),
-        ),
-        in_specs=[HBM, HBM],
-        out_specs=(VMEM, VMEM),
+        out_shape=tuple(out_shape),
+        in_specs=[HBM, HBM, HBM],
+        out_specs=tuple([VMEM] * len(out_shape)),
         scratch_shapes=[
-            pltpu.VMEM((9 * steps, channels, channels), jnp.float32),
+            pltpu.VMEM((9, channels, channels), jnp.float32),
             pltpu.VMEM(gain.shape, jnp.float32),
-            pltpu.SemaphoreType.DMA((steps, len(groups))),
+            pltpu.SemaphoreType.DMA((frames,)),
+            pltpu.SemaphoreType.DMA((len(groups),)),
             pltpu.SemaphoreType.DMA,
         ],
         compiler_params=GRANT,
-        name="prepare",
-    )(
-        pltpu.with_memory_space_constraint(weight, pltpu.HBM),
-        pltpu.with_memory_space_constraint(gain, pltpu.HBM),
-    )
-
-
-def edges(latents, rows):
-    frames, lines, width = latents.shape
-    channels = lines // rows
-
-    def kernel(ref, *outs):
-        even = lax.rem(lax.axis_index("tiles"), 2) == 0
-        for f in range(frames):
-            top = ref[f, pl.ds(0, channels, stride=rows), :]
-            bottom = ref[f, pl.ds(rows - 1, channels, stride=rows), :]
-            outs[2 * f][...] = jnp.where(even, bottom, top)
-            outs[2 * f + 1][...] = jnp.where(even, top, bottom)
+        name="opening",
+    )(in_hbm(latents), in_hbm(weight), in_hbm(gain))
+
+
+def earlier_taps(weight, offset, depth):
+    channels = weight.shape[1]
+    groups = tap_groups(channels, depth)
+
+    def kernel(weight_ref, both, staged, sems):
+        copies = fetch_taps(weight_ref, 9 * offset, staged, sems, groups)
+        split_taps(copies, staged, both, groups)
 
     return pl.pallas_call(
         kernel,
-        out_shape=tuple([held((channels, width))] * (2 * frames)),
-        in_specs=[VMEM],
-        out_specs=tuple([VMEM] * (2 * frames)),
+        out_shape=held((2 * channels, depth), jnp.bfloat16),
+        in_specs=[HBM],
+        out_specs=VMEM,
+        scratch_shapes=[
+            pltpu.VMEM((9, channels, channels), jnp.float32),
+            pltpu.SemaphoreType.DMA((len(groups),)),
+        ],
         compiler_params=GRANT,
-        name="edges",
-    )(latents)
+        name="earlier_taps",
+    )(in_hbm(weight))
 
 
 def normalize(values, gain):
@@ -229,7 +263,7 @@
     channels, width = near_a.shape[-2:]
     lines = main.shape[-2]
     rows = lines // channels
-    steps, _, depth = weights.shape
+    depth = weights[-1].shape[1]
     last = layer == sections - 1
     share = lines // sections
     count = sections if last else 3
@@ -270,7 +304,7 @@
                             cols = slice(r * width, (r + 1) * width)
                             patch_high[k : k + channels, cols] = upper
                             patch_low[k : k + channels, cols] = lower
-            total = product(both_ref[steps - 1], patch_high[...], patch_low[...])
+            total = product(both_ref[...], patch_high[...], patch_low[...])
             if partial is not None:
                 total = total + partial_ref[...]
             results = [
@@ -289,7 +323,7 @@
                 outs[1][...] = jnp.where(even, results[-1], results[0])
                 outs[2][...] = jnp.where(even, results[0], results[-1])
 
-    operands = [main, near_a, near_b, gain, weights]
+    operands = [main, near_a, near_b, gain, weights[-1]]
     if partial is not None:
         operands.append(partial)
     if last:
@@ -320,23 +354,25 @@
 
 
 def earlier_frames(layer, weights, patches):
-    steps, channels, depth = weights.shape[0], weights.shape[1] // 2, weights.shape[2]
+    channels, depth = weights[-1].shape[0] // 2, weights[-1].shape[1]
     count = len(patches)
     columns = patches[0][0].shape[1]
 
-    def kernel(both_ref, *refs):
+    taps = weights[len(weights) - 1 - count : len(weights) - 1]
+
+    def kernel(*refs):
         out_ref = refs[-1]
 
         @pl.when(lax.axis_index("section") == layer)
         def _():
             total = None
             for n in range(count):
-                a = steps - 1 - (count - n)
-                term = product(both_ref[a], refs[2 * n][...], refs[2 * n + 1][...])
+                high, low = refs[count + 2 * n], refs[count + 2 * n + 1]
+                term = product(refs[n][...], high[...], low[...])
                 total = term if total is None else total + term
             out_ref[...] = total
 
-    operands = [weights]
+    operands = [*taps]
     for pair in patches:
         operands += list(pair)
     return pl.pallas_call(
@@ -364,12 +400,13 @@
     of_b = lambda t: partner_b(t, tiles)
 
     flat = latents.reshape(frames, channels * rows, width)
-    edge = edges(flat, rows)
+    flat, current, gains, *edge = opening(flat, conv_weight[0], gain, rows, depth)
     edge_a, edge_b = edge[0::2], edge[1::2]
     rim_a, rim_b = (rim_pairs(shape, of) for of in (of_a, of_b))
     near_a = [send(edge_a[f], rim_a) for f in range(frames)]
     near_b = [send(edge_b[f], rim_b) for f in range(frames)]
-    weights, gains = prepare(conv_weight[0], gain, steps, depth, width)
+    earlier = [earlier_taps(conv_weight[0], a, depth) for a in range(3 - steps, 2)]
+    weights = [*earlier, current]
     main = [flat] * frames
 
     for layer in range(sections):

time: 37.2 us -> 39.9 us (1.073)
  starting transfers between devices: 21.3 us -> 22.8 us
  Pallas kernels: 5.71 us -> 7.16 us
  local copies, waits for them, and re-layouts: 1 us -> 0 us
  waiting for transfers between devices: 8.74 us -> 9.5 us
    ppermute x28, starting transfers between devices: 21.3 us -> 22.8 us  [send(): return lax.ppermute(value, ('groups', 'tiles', 'section'), pairs)]
    pallas_call x2, Pallas kernels: 2.29 us -> 3.74 us  [the longest x1 2.17 us: opening(): pl.pallas_call(kernel, out_shape=tuple(out_shape), in_specs=[HBM, HBM, HB...]
    unnamed x2 -> x0, local copies, waits for them, and re-layouts: 1 us -> none
    ppermute x28, waiting for transfers between devices: 8.74 us -> 9.5 us  [send(): return lax.ppermute(value, ('groups', 'tiles', 'section'), pairs)]
  transfers between devices with their start and end apart: 28 -> 28, of which waited for: 6 -> 6; matrix products, arithmetic and copies ran while one was open for 0% -> 0% of each run, Pallas kernels for 14% -> 11%
where the time goes in v5:
time: 39.9 us; the launch traced here: 39.6 us
  starting transfers between devices  22.8 us (57%)
  waiting for transfers between devices  9.5 us (24%)
  Pallas kernels  7.16 us (18%)
    ppermute x28, starting transfers between devices, send(): return lax.ppermute(value, ('groups', 'tiles', 'section'), pairs)  22.8 us
    ppermute x28, waiting for transfers between devices, send(): return lax.ppermute(value, ('groups', 'tiles', 'section'), pairs)  9.5 us
    pallas_call x1, Pallas kernels, opening(): pl.pallas_call(kernel, out_shape=tuple(out_shape), in_specs=[HBM, HBM, HB...  2.17 us
    pallas_call x8, Pallas kernels, frame_step(): pl.pallas_call(kernel, out_shape=tuple(out_shape), in_specs=[VMEM] * len(...  2.07 us
    pallas_call x1, Pallas kernels, earlier_taps(): pl.pallas_call(kernel, out_shape=held((2 * channels, depth), jnp.bfloat16...  1.57 us
  transfers between devices with their start and end apart: 28, of which 6 were waited for; matrix products, arithmetic and copies ran while one was open for 0% of the time, Pallas kernels for 11%

profile of v5, /device:TPU:0, one launch (start us, length us, event | category | flops | bytes accessed | tf_op | source)
XLA Modules:
  0.0 39.6 jit_solution(15043549508457975339)
XLA Ops:
  0.0 2.2 %opening.1 = (f32[2,384,128]{2,1,0:T(8,128)S(1)}, bf16[384,1792]{1,0:T(8,128)(2,1)S(1)}, f32[192,128]{1,0:T(8,128)S(1)}, f32[192,128]{1,0:T(8,128)S(1)}, f32[192...) custom-call(f32[2,384,128]{2,1,0:T(8,128)} %bitcast.5, f32[27,192,192]{2,1,0:T(8,128)} %bitcast.3, ...), custom_call_target="tpu_custom_call" | custom-call | tf_op jit(solution)/shard_map/opening/pallas_call | solution.py:198
  2.2 3.1 %collective-permute-start = (f32[192,128]{1,0:T(8,128)S(1)}, f32[192,128]{1,0:T(8,128)S(1)}, u32[]{:S(2)}, u32[]{:S(2)}) collective-permute-start(f32[192,128]{1,0:T(8,128)S(1)} %get-tuple-element.47), channel_id=1, source_target_pairs={{0,4},{1,17},{2,3},{3,2},{4,0},{5,21},{6,7},{7,6},{8,12},{9,25},{1... | collective-permute-start | bytes 294920 | tf_op jit(solution)/shard_map/ppermute | solution.py:106
  5.3 3.1 %collective-permute-start.14 = (f32[192,128]{1,0:T(8,128)S(1)}, f32[192,128]{1,0:T(8,128)S(1)}, u32[]{:S(2)}, u32[]{:S(2)}) collective-permute-start(f32[192,128]{1,0:T(8,128)S(1)} %get-tuple-element.64), channel_id=1, source_target_pairs={{0,4},{1,17},{2,3},{3,2},{4,0},{5,21},{6,7},{7,6},{8,12},{9,25},{1... | collective-permute-start | bytes 294920 | tf_op jit(solution)/shard_map/ppermute | solution.py:106
  8.5 1.0 %frame_step.8 = (f32[384,128]{1,0:T(8,128)S(1)}, f32[192,128]{1,0:T(8,128)S(1)}, f32[192,128]{1,0:T(8,128)S(1)}, bf16[1792,256]{1,0:T(8,128)(2,1)S(1)}, bf16[1792,256]{1,0:T(8,128)(2,1)S(1)}) custom-call(f32[2,384,128]{2,1,0:T(8,128)S(1)} %get-tuple-element.46.refs_0_, f32[192,128]{1,0:T(8,128)S(1)} %collective-permute-done.refs_1_, ...), custom_call_target="tpu_custom_call" | custom-call | flops 528482304 | bytes 1048576 | tf_op jit(solution)/shard_map/frame_step/pallas_call | solution.py:340
  9.5 0.1 collective-permute-start.2
  9.6 1.6 %earlier_taps.1.refs_0_ = bf16[384,1792]{1,0:T(8,128)(2,1)S(1)} custom-call(f32[27,192,192]{2,1,0:T(8,128)} %bitcast.4), custom_call_target="tpu_custom_call" | custom-call | tf_op jit(solution)/shard_map/earlier_taps/pallas_call | solution.py:223
  11.1 2.7 %collective-permute-start.3 = (f32[192,128]{1,0:T(8,128)S(1)}, f32[192,128]{1,0:T(8,128)S(1)}, u32[]{:S(2)}, u32[]{:S(2)}) collective-permute-start(f32[192,128]{1,0:T(8,128)S(1)} %get-tuple-element.52), channel_id=1, source_target_pairs={{0,5},{1,0},{2,3},{3,2},{4,1},{5,4},{6,7},{7,6},{8,13},{9,8},{10,1... | collective-permute-start | bytes 294920 | tf_op jit(solution)/shard_map/ppermute | solution.py:106
  13.9 0.7 %earlier_frames.4.refs_5_ = f32[192,256]{1,0:T(8,128)S(1)} custom-call(bf16[384,1792]{1,0:T(8,128)(2,1)S(1)} %earlier_taps.1.refs_0_, bf16[1792,256]{1,0:T(8,128)(2,1)S(1)} %get-tuple-element.66.refs_1_, bf16[1792,256]{1,0:T(8,128)(2,1)S(1)} %get-tuple-element.67.refs_2_), custom_call_target="tpu_custom_call" | custom-call | flops 528482304 | bytes 1048576 | tf_op jit(solution)/shard_map/earlier_frames/pallas_call | solution.py:378
  14.6 0.0 collective-permute-done.15.refs_2_
  14.6 1.0 %frame_step.12 = (f32[384,128]{1,0:T(8,128)S(1)}, f32[192,128]{1,0:T(8,128)S(1)}, f32[192,128]{1,0:T(8,128)S(1)}) custom-call(f32[2,384,128]{2,1,0:T(8,128)S(1)} %get-tuple-element.46.refs_0_, f32[192,128]{1,0:T(8,128)S(1)} %collective-permute-done.14.refs_1_, f32[192,128]{1,0:T(8,128)S(1)} %collective-permute-done.15.refs_2_, ...), custom_call_target="tpu_custom_call" | custom-call | flops 528482304 | bytes 1048576 | tf_op jit(solution)/shard_map/frame_step/pallas_call | solution.py:340
  15.6 0.1 collective-permute-start.16
  15.7 2.2 %collective-permute-start.17 = (f32[192,128]{1,0:T(8,128)S(1)}, f32[192,128]{1,0:T(8,128)S(1)}, u32[]{:S(2)}, u32[]{:S(2)}) collective-permute-start(f32[192,128]{1,0:T(8,128)S(1)} %get-tuple-element.69), channel_id=1, source_target_pairs={{0,5},{1,0},{2,3},{3,2},{4,1},{5,4},{6,7},{7,6},{8,13},{9,8},{10,1... | collective-permute-start | bytes 294920 | tf_op jit(solution)/shard_map/ppermute | solution.py:106
  17.9 1.5 %collective-permute-start.5 = (f32[384,128]{1,0:T(8,128)S(1)}, f32[384,128]{1,0:T(8,128)S(1)}, u32[]{:S(2)}, u32[]{:S(2)}) collective-permute-start(f32[384,128]{1,0:T(8,128)S(1)} %get-tuple-element.54), channel_id=1, source_target_pairs={{0,1},{1,2},{2,3},{3,0},{4,5},{5,6},{6,7},{7,4},{8,9},{9,10},{10,1... | collective-permute-start | bytes 589832 | tf_op jit(solution)/shard_map/ppermute | solution.py:106
  19.5 0.1 collective-permute-start.6
  19.5 0.6 %collective-permute-done.17.refs_1_ = f32[192,128]{1,0:T(8,128)S(1)} collective-permute-done((f32[192,128]{1,0:T(8,128)S(1)}, f32[192,128]{1,0:T(8,128)S(1)}, u32[]{:S(2)}, u32[]{:S(2)}) %collective-permute-start.17) | collective-permute-done | bytes 98336 | tf_op jit(solution)/shard_map/ppermute | solution.py:106
  20.1 0.2 collective-permute-start.7
  20.3 1.1 %collective-permute-start.19 = (f32[384,128]{1,0:T(8,128)S(1)}, f32[384,128]{1,0:T(8,128)S(1)}, u32[]{:S(2)}, u32[]{:S(2)}) collective-permute-start(f32[384,128]{1,0:T(8,128)S(1)} %get-tuple-element.73), channel_id=1, source_target_pairs={{0,1},{1,2},{2,3},{3,0},{4,5},{5,6},{6,7},{7,4},{8,9},{9,10},{10,1... | collective-permute-start | bytes 589832 | tf_op jit(solution)/shard_map/ppermute | solution.py:106
  21.4 0.3 collective-permute-start.20
  21.7 2.4 %collective-permute-done.6.refs_1_ = f32[192,128]{1,0:T(8,128)S(1)} collective-permute-done((f32[192,128]{1,0:T(8,128)S(1)}, f32[192,128]{1,0:T(8,128)S(1)}, u32[]{:S(2)}, u32[]{:S(2)}) %collective-permute-start.6) | collective-permute-done | bytes 98336 | tf_op jit(solution)/shard_map/ppermute | solution.py:106
  24.1 1.1 %collective-permute-done.7.refs_2_ = f32[192,128]{1,0:T(8,128)S(1)} collective-permute-done((f32[192,128]{1,0:T(8,128)S(1)}, f32[192,128]{1,0:T(8,128)S(1)}, u32[]{:S(2)}, u32[]{:S(2)}) %collective-permute-start.7) | collective-permute-done | bytes 98336 | tf_op jit(solution)/shard_map/ppermute | solution.py:106
  25.2 0.5 %collective-permute-start.9 = (f32[192,128]{1,0:T(8,128)S(1)}, f32[192,128]{1,0:T(8,128)S(1)}, u32[]{:S(2)}, u32[]{:S(2)}) collective-permute-start(f32[192,128]{1,0:T(8,128)S(1)} %get-tuple-element.58), channel_id=1, source_target_pairs={{0,1},{1,0},{2,7},{3,2},{4,5},{5,4},{6,3},{7,6},{8,9},{9,8},{10,15... | collective-permute-start | bytes 294920 | tf_op jit(solution)/shard_map/ppermute | solution.py:106
  25.7 2.6 %collective-permute-done.20.refs_1_ = f32[192,128]{1,0:T(8,128)S(1)} collective-permute-done((f32[192,128]{1,0:T(8,128)S(1)}, f32[192,128]{1,0:T(8,128)S(1)}, u32[]{:S(2)}, u32[]{:S(2)}) %collective-permute-start.20) | collective-permute-done | bytes 98336 | tf_op jit(solution)/shard_map/ppermute | solution.py:106
  28.3 1.0 %collective-permute-done.21.refs_2_ = f32[192,128]{1,0:T(8,128)S(1)} collective-permute-done((f32[192,128]{1,0:T(8,128)S(1)}, f32[192,128]{1,0:T(8,128)S(1)}, u32[]{:S(2)}, u32[]{:S(2)}) %collective-permute-start.21) | collective-permute-done | bytes 98336 | tf_op jit(solution)/shard_map/ppermute | solution.py:106
  29.4 0.5 %collective-permute-start.23 = (f32[192,128]{1,0:T(8,128)S(1)}, f32[192,128]{1,0:T(8,128)S(1)}, u32[]{:S(2)}, u32[]{:S(2)}) collective-permute-start(f32[192,128]{1,0:T(8,128)S(1)} %get-tuple-element.79), channel_id=1, source_target_pairs={{0,1},{1,0},{2,7},{3,2},{4,5},{5,4},{6,3},{7,6},{8,9},{9,8},{10,15... | collective-permute-start | bytes 294920 | tf_op jit(solution)/shard_map/ppermute | solution.py:106
  29.9 0.0 collective-permute-start.24
  30.0 0.5 %collective-permute-start.11 = (f32[96,128]{1,0:T(8,128)S(1)}, f32[96,128]{1,0:T(8,128)S(1)}, u32[]{:S(2)}, u32[]{:S(2)}) collective-permute-start(f32[96,128]{1,0:T(8,128)S(1)} %get-tuple-element.60), channel_id=1, source_target_pairs={{0,1},{1,2},{2,3},{3,0},{4,5},{5,6},{6,7},{7,4},{8,9},{9,10},{10,1... | collective-permute-start | bytes 147464 | tf_op jit(solution)/shard_map/ppermute | solution.py:106
  30.4 3.7 %collective-permute-start.12 = (f32[96,128]{1,0:T(8,128)S(1)}, f32[96,128]{1,0:T(8,128)S(1)}, u32[]{:S(2)}, u32[]{:S(2)}) collective-permute-start(f32[96,128]{1,0:T(8,128)S(1)} %get-tuple-element.61), channel_id=1, source_target_pairs={{0,3},{1,0},{2,18},{3,1},{4,7},{5,4},{6,22},{7,5},{8,11},{9,8},{10... | collective-permute-start | bytes 147464 | tf_op jit(solution)/shard_map/ppermute | solution.py:106
  34.2 0.5 %collective-permute-start.25 = (f32[96,128]{1,0:T(8,128)S(1)}, f32[96,128]{1,0:T(8,128)S(1)}, u32[]{:S(2)}, u32[]{:S(2)}) collective-permute-start(f32[96,128]{1,0:T(8,128)S(1)} %get-tuple-element.83), channel_id=1, source_target_pairs={{0,1},{1,2},{2,3},{3,0},{4,5},{5,6},{6,7},{7,4},{8,9},{9,10},{10,1... | collective-permute-start | bytes 147464 | tf_op jit(solution)/shard_map/ppermute | solution.py:106
  34.6 2.6 %collective-permute-start.26 = (f32[96,128]{1,0:T(8,128)S(1)}, f32[96,128]{1,0:T(8,128)S(1)}, u32[]{:S(2)}, u32[]{:S(2)}) collective-permute-start(f32[96,128]{1,0:T(8,128)S(1)} %get-tuple-element.84), channel_id=1, source_target_pairs={{0,3},{1,0},{2,18},{3,1},{4,7},{5,4},{6,22},{7,5},{8,11},{9,8},{10... | collective-permute-start | bytes 147464 | tf_op jit(solution)/shard_map/ppermute | solution.py:106
  37.2 1.7 %collective-permute-done.25.refs_4_ = f32[96,128]{1,0:T(8,128)S(1)} collective-permute-done((f32[96,128]{1,0:T(8,128)S(1)}, f32[96,128]{1,0:T(8,128)S(1)}, u32[]{:S(2)}, u32[]{:S(2)}) %collective-permute-start.25) | collective-permute-done | bytes 49184 | tf_op jit(solution)/shard_map/ppermute | solution.py:106
  38.9 0.0 collective-permute-done.26.refs_5_
  39.0 0.7 %assemble.1 = f32[2,96,128]{2,1,0:T(8,128)} custom-call(f32[96,128]{1,0:T(8,128)S(1)} %collective-permute-done.11.refs_0_, f32[96,128]{1,0:T(8,128)S(1)} %collective-permute-done.12.refs_1_, f32[96,128]{1,0:T(8,128)S(1)} %collective-permute-done.13.refs_2_, f32[96,128]{1,0:T(8,128)S(1)} %get-tuple-element.63.refs_3_, ...), custom_call_target="tpu_custom_call" | custom-call | tf_op jit(solution)/shard_map/assemble/pallas_call | solution.py:461
  (39 shorter events, 0.1 us)
Async XLA Ops:
  2.2 6.3 %collective-permute-start = (f32[192,128]{1,0:T(8,128)S(1)}, f32[192,128]{1,0:T(8,128)S(1)}, u32[]{:S(2)}, u32[]{:S(2)}) collective-permute-start(f32[192,128]{1,0:T(8,128)S(1)} %get-tuple-element.47), channel_id=1, source_target_pairs={{0,4},{1,17},{2,3},{3,2},{4,0},{5,21},{6,7},{7,6},{8,12},{9,25},{1... | collective-permute-start | bytes 294920 | tf_op jit(solution)/shard_map/ppermute | solution.py:106
  5.3 3.2 %collective-permute-start.1 = (f32[192,128]{1,0:T(8,128)S(1)}, f32[192,128]{1,0:T(8,128)S(1)}, u32[]{:S(2)}, u32[]{:S(2)}) collective-permute-start(f32[192,128]{1,0:T(8,128)S(1)} %get-tuple-element.48), channel_id=1, source_target_pairs={{0,1},{1,0},{2,3},{3,2},{4,8},{5,21},{6,7},{7,6},{8,4},{9,25},{10,... | collective-permute-start | bytes 294920 | tf_op jit(solution)/shard_map/ppermute | solution.py:106
  5.3 9.3 %collective-permute-start.14 = (f32[192,128]{1,0:T(8,128)S(1)}, f32[192,128]{1,0:T(8,128)S(1)}, u32[]{:S(2)}, u32[]{:S(2)}) collective-permute-start(f32[192,128]{1,0:T(8,128)S(1)} %get-tuple-element.64), channel_id=1, source_target_pairs={{0,4},{1,17},{2,3},{3,2},{4,0},{5,21},{6,7},{7,6},{8,12},{9,25},{1... | collective-permute-start | bytes 294920 | tf_op jit(solution)/shard_map/ppermute | solution.py:106
  8.4 6.1 %collective-permute-start.15 = (f32[192,128]{1,0:T(8,128)S(1)}, f32[192,128]{1,0:T(8,128)S(1)}, u32[]{:S(2)}, u32[]{:S(2)}) collective-permute-start(f32[192,128]{1,0:T(8,128)S(1)} %get-tuple-element.65), channel_id=1, source_target_pairs={{0,1},{1,0},{2,3},{3,2},{4,8},{5,21},{6,7},{7,6},{8,4},{9,25},{10,... | collective-permute-start | bytes 294920 | tf_op jit(solution)/shard_map/ppermute | solution.py:106
  9.5 8.4 %collective-permute-start.2 = (f32[384,128]{1,0:T(8,128)S(1)}, f32[384,128]{1,0:T(8,128)S(1)}, u32[]{:S(2)}, u32[]{:S(2)}) collective-permute-start(f32[384,128]{1,0:T(8,128)S(1)} %get-tuple-element.51), channel_id=1, source_target_pairs={{0,1},{1,0},{2,3},{3,2},{4,5},{5,4},{6,7},{7,6},{8,9},{9,8},{10,11... | collective-permute-start | bytes 589832 | tf_op jit(solution)/shard_map/ppermute | solution.py:106
  11.1 6.7 %collective-permute-start.3 = (f32[192,128]{1,0:T(8,128)S(1)}, f32[192,128]{1,0:T(8,128)S(1)}, u32[]{:S(2)}, u32[]{:S(2)}) collective-permute-start(f32[192,128]{1,0:T(8,128)S(1)} %get-tuple-element.52), channel_id=1, source_target_pairs={{0,5},{1,0},{2,3},{3,2},{4,1},{5,4},{6,7},{7,6},{8,13},{9,8},{10,1... | collective-permute-start | bytes 294920 | tf_op jit(solution)/shard_map/ppermute | solution.py:106
  13.9 4.0 %collective-permute-start.4 = (f32[192,128]{1,0:T(8,128)S(1)}, f32[192,128]{1,0:T(8,128)S(1)}, u32[]{:S(2)}, u32[]{:S(2)}) collective-permute-start(f32[192,128]{1,0:T(8,128)S(1)} %get-tuple-element.53), channel_id=1, source_target_pairs={{0,1},{1,0},{2,3},{3,2},{4,9},{5,4},{6,7},{7,6},{8,5},{9,8},{10,11... | collective-permute-start | bytes 294920 | tf_op jit(solution)/shard_map/ppermute | solution.py:106
  15.6 4.7 %collective-permute-start.16 = (f32[384,128]{1,0:T(8,128)S(1)}, f32[384,128]{1,0:T(8,128)S(1)}, u32[]{:S(2)}, u32[]{:S(2)}) collective-permute-start(f32[384,128]{1,0:T(8,128)S(1)} %get-tuple-element.68), channel_id=1, source_target_pairs={{0,1},{1,0},{2,3},{3,2},{4,5},{5,4},{6,7},{7,6},{8,9},{9,8},{10,11... | collective-permute-start | bytes 589832 | tf_op jit(solution)/shard_map/ppermute | solution.py:106
  15.7 4.4 %collective-permute-start.17 = (f32[192,128]{1,0:T(8,128)S(1)}, f32[192,128]{1,0:T(8,128)S(1)}, u32[]{:S(2)}, u32[]{:S(2)}) collective-permute-start(f32[192,128]{1,0:T(8,128)S(1)} %get-tuple-element.69), channel_id=1, source_target_pairs={{0,5},{1,0},{2,3},{3,2},{4,1},{5,4},{6,7},{7,6},{8,13},{9,8},{10,1... | collective-permute-start | bytes 294920 | tf_op jit(solution)/shard_map/ppermute | solution.py:106
  17.9 2.4 %collective-permute-start.18 = (f32[192,128]{1,0:T(8,128)S(1)}, f32[192,128]{1,0:T(8,128)S(1)}, u32[]{:S(2)}, u32[]{:S(2)}) collective-permute-start(f32[192,128]{1,0:T(8,128)S(1)} %get-tuple-element.70), channel_id=1, source_target_pairs={{0,1},{1,0},{2,3},{3,2},{4,9},{5,4},{6,7},{7,6},{8,5},{9,8},{10,11... | collective-permute-start | bytes 294920 | tf_op jit(solution)/shard_map/ppermute | solution.py:106
  17.9 7.3 %collective-permute-start.5 = (f32[384,128]{1,0:T(8,128)S(1)}, f32[384,128]{1,0:T(8,128)S(1)}, u32[]{:S(2)}, u32[]{:S(2)}) collective-permute-start(f32[384,128]{1,0:T(8,128)S(1)} %get-tuple-element.54), channel_id=1, source_target_pairs={{0,1},{1,2},{2,3},{3,0},{4,5},{5,6},{6,7},{7,4},{8,9},{9,10},{10,1... | collective-permute-start | bytes 589832 | tf_op jit(solution)/shard_map/ppermute | solution.py:106
  19.5 4.7 %collective-permute-start.6 = (f32[192,128]{1,0:T(8,128)S(1)}, f32[192,128]{1,0:T(8,128)S(1)}, u32[]{:S(2)}, u32[]{:S(2)}) collective-permute-start(f32[192,128]{1,0:T(8,128)S(1)} %get-tuple-element.55), channel_id=1, source_target_pairs={{0,1},{1,6},{2,3},{3,0},{4,5},{5,2},{6,7},{7,4},{8,9},{9,14},{10,1... | collective-permute-start | bytes 294920 | tf_op jit(solution)/shard_map/ppermute | solution.py:106
  20.1 5.1 %collective-permute-start.7 = (f32[192,128]{1,0:T(8,128)S(1)}, f32[192,128]{1,0:T(8,128)S(1)}, u32[]{:S(2)}, u32[]{:S(2)}) collective-permute-start(f32[192,128]{1,0:T(8,128)S(1)} %get-tuple-element.56), channel_id=1, source_target_pairs={{0,1},{1,2},{2,3},{3,0},{4,5},{5,10},{6,7},{7,4},{8,9},{9,6},{10,1... | collective-permute-start | bytes 294920 | tf_op jit(solution)/shard_map/ppermute | solution.py:106
  20.3 9.1 %collective-permute-start.19 = (f32[384,128]{1,0:T(8,128)S(1)}, f32[384,128]{1,0:T(8,128)S(1)}, u32[]{:S(2)}, u32[]{:S(2)}) collective-permute-start(f32[384,128]{1,0:T(8,128)S(1)} %get-tuple-element.73), channel_id=1, source_target_pairs={{0,1},{1,2},{2,3},{3,0},{4,5},{5,6},{6,7},{7,4},{8,9},{9,10},{10,1... | collective-permute-start | bytes 589832 | tf_op jit(solution)/shard_map/ppermute | solution.py:106
  21.4 6.9 %collective-permute-start.20 = (f32[192,128]{1,0:T(8,128)S(1)}, f32[192,128]{1,0:T(8,128)S(1)}, u32[]{:S(2)}, u32[]{:S(2)}) collective-permute-start(f32[192,128]{1,0:T(8,128)S(1)} %get-tuple-element.74), channel_id=1, source_target_pairs={{0,1},{1,6},{2,3},{3,0},{4,5},{5,2},{6,7},{7,4},{8,9},{9,14},{10,1... | collective-permute-start | bytes 294920 | tf_op jit(solution)/shard_map/ppermute | solution.py:106
  24.1 5.3 %collective-permute-start.21 = (f32[192,128]{1,0:T(8,128)S(1)}, f32[192,128]{1,0:T(8,128)S(1)}, u32[]{:S(2)}, u32[]{:S(2)}) collective-permute-start(f32[192,128]{1,0:T(8,128)S(1)} %get-tuple-element.75), channel_id=1, source_target_pairs={{0,1},{1,2},{2,3},{3,0},{4,5},{5,10},{6,7},{7,4},{8,9},{9,6},{10,1... | collective-permute-start | bytes 294920 | tf_op jit(solution)/shard_map/ppermute | solution.py:106
  25.2 4.8 %collective-permute-start.8 = (f32[384,128]{1,0:T(8,128)S(1)}, f32[384,128]{1,0:T(8,128)S(1)}, u32[]{:S(2)}, u32[]{:S(2)}) collective-permute-start(f32[384,128]{1,0:T(8,128)S(1)} %get-tuple-element.57), channel_id=1, source_target_pairs={{0,1},{1,0},{2,3},{3,2},{4,5},{5,4},{6,7},{7,6},{8,9},{9,8},{10,11... | collective-permute-start | bytes 589832 | tf_op jit(solution)/shard_map/ppermute | solution.py:106
  25.2 4.7 %collective-permute-start.9 = (f32[192,128]{1,0:T(8,128)S(1)}, f32[192,128]{1,0:T(8,128)S(1)}, u32[]{:S(2)}, u32[]{:S(2)}) collective-permute-start(f32[192,128]{1,0:T(8,128)S(1)} %get-tuple-element.58), channel_id=1, source_target_pairs={{0,1},{1,0},{2,7},{3,2},{4,5},{5,4},{6,3},{7,6},{8,9},{9,8},{10,15... | collective-permute-start | bytes 294920 | tf_op jit(solution)/shard_map/ppermute | solution.py:106
  28.3 1.6 %collective-permute-start.10 = (f32[192,128]{1,0:T(8,128)S(1)}, f32[192,128]{1,0:T(8,128)S(1)}, u32[]{:S(2)}, u32[]{:S(2)}) collective-permute-start(f32[192,128]{1,0:T(8,128)S(1)} %get-tuple-element.59), channel_id=1, source_target_pairs={{0,1},{1,0},{2,3},{3,2},{4,5},{5,4},{6,11},{7,6},{8,9},{9,8},{10,7... | collective-permute-start | bytes 294920 | tf_op jit(solution)/shard_map/ppermute | solution.py:106
  29.4 4.7 %collective-permute-start.22 = (f32[384,128]{1,0:T(8,128)S(1)}, f32[384,128]{1,0:T(8,128)S(1)}, u32[]{:S(2)}, u32[]{:S(2)}) collective-permute-start(f32[384,128]{1,0:T(8,128)S(1)} %get-tuple-element.78), channel_id=1, source_target_pairs={{0,1},{1,0},{2,3},{3,2},{4,5},{5,4},{6,7},{7,6},{8,9},{9,8},{10,11... | collective-permute-start | bytes 589832 | tf_op jit(solution)/shard_map/ppermute | solution.py:106
  29.4 4.7 %collective-permute-start.23 = (f32[192,128]{1,0:T(8,128)S(1)}, f32[192,128]{1,0:T(8,128)S(1)}, u32[]{:S(2)}, u32[]{:S(2)}) collective-permute-start(f32[192,128]{1,0:T(8,128)S(1)} %get-tuple-element.79), channel_id=1, source_target_pairs={{0,1},{1,0},{2,7},{3,2},{4,5},{5,4},{6,3},{7,6},{8,9},{9,8},{10,15... | collective-permute-start | bytes 294920 | tf_op jit(solution)/shard_map/ppermute | solution.py:106
  29.9 4.2 %collective-permute-start.24 = (f32[192,128]{1,0:T(8,128)S(1)}, f32[192,128]{1,0:T(8,128)S(1)}, u32[]{:S(2)}, u32[]{:S(2)}) collective-permute-start(f32[192,128]{1,0:T(8,128)S(1)} %get-tuple-element.80), channel_id=1, source_target_pairs={{0,1},{1,0},{2,3},{3,2},{4,5},{5,4},{6,11},{7,6},{8,9},{9,8},{10,7... | collective-permute-start | bytes 294920 | tf_op jit(solution)/shard_map/ppermute | solution.py:106
  30.0 7.3 %collective-permute-start.11 = (f32[96,128]{1,0:T(8,128)S(1)}, f32[96,128]{1,0:T(8,128)S(1)}, u32[]{:S(2)}, u32[]{:S(2)}) collective-permute-start(f32[96,128]{1,0:T(8,128)S(1)} %get-tuple-element.60), channel_id=1, source_target_pairs={{0,1},{1,2},{2,3},{3,0},{4,5},{5,6},{6,7},{7,4},{8,9},{9,10},{10,1... | collective-permute-start | bytes 147464 | tf_op jit(solution)/shard_map/ppermute | solution.py:106
  30.4 6.8 %collective-permute-start.12 = (f32[96,128]{1,0:T(8,128)S(1)}, f32[96,128]{1,0:T(8,128)S(1)}, u32[]{:S(2)}, u32[]{:S(2)}) collective-permute-start(f32[96,128]{1,0:T(8,128)S(1)} %get-tuple-element.61), channel_id=1, source_target_pairs={{0,3},{1,0},{2,18},{3,1},{4,7},{5,4},{6,22},{7,5},{8,11},{9,8},{10... | collective-permute-start | bytes 147464 | tf_op jit(solution)/shard_map/ppermute | solution.py:106
  34.1 3.1 %collective-permute-start.13 = (f32[96,128]{1,0:T(8,128)S(1)}, f32[96,128]{1,0:T(8,128)S(1)}, u32[]{:S(2)}, u32[]{:S(2)}) collective-permute-start(f32[96,128]{1,0:T(8,128)S(1)} %get-tuple-element.62), channel_id=1, source_target_pairs={{0,1},{1,0},{2,3},{3,2},{4,5},{5,4},{6,7},{7,6},{8,9},{9,8},{10,11... | collective-permute-start | bytes 147464 | tf_op jit(solution)/shard_map/ppermute | solution.py:106
  34.2 4.8 %collective-permute-start.25 = (f32[96,128]{1,0:T(8,128)S(1)}, f32[96,128]{1,0:T(8,128)S(1)}, u32[]{:S(2)}, u32[]{:S(2)}) collective-permute-start(f32[96,128]{1,0:T(8,128)S(1)} %get-tuple-element.83), channel_id=1, source_target_pairs={{0,1},{1,2},{2,3},{3,0},{4,5},{5,6},{6,7},{7,4},{8,9},{9,10},{10,1... | collective-permute-start | bytes 147464 | tf_op jit(solution)/shard_map/ppermute | solution.py:106
  34.6 4.3 %collective-permute-start.26 = (f32[96,128]{1,0:T(8,128)S(1)}, f32[96,128]{1,0:T(8,128)S(1)}, u32[]{:S(2)}, u32[]{:S(2)}) collective-permute-start(f32[96,128]{1,0:T(8,128)S(1)} %get-tuple-element.84), channel_id=1, source_target_pairs={{0,3},{1,0},{2,18},{3,1},{4,7},{5,4},{6,22},{7,5},{8,11},{9,8},{10... | collective-permute-start | bytes 147464 | tf_op jit(solution)/shard_map/ppermute | solution.py:106
  37.2 1.8 %collective-permute-start.27 = (f32[96,128]{1,0:T(8,128)S(1)}, f32[96,128]{1,0:T(8,128)S(1)}, u32[]{:S(2)}, u32[]{:S(2)}) collective-permute-start(f32[96,128]{1,0:T(8,128)S(1)} %get-tuple-element.85), channel_id=1, source_target_pairs={{0,1},{1,0},{2,3},{3,2},{4,5},{5,4},{6,7},{7,6},{8,9},{9,8},{10,11... | collective-permute-start | bytes 147464 | tf_op jit(solution)/shard_map/ppermute | solution.py:106

commit v6 on v5

--- a/solution.py
+++ b/solution.py
@@ -116,64 +116,61 @@
     return pltpu.VMEM(shape, dtype)
 
 
-def tap_groups(channels, depth):
-    groups = []
-    for k in range(0, 9, 2):
-        size = min(2, 9 - k)
-        extra = depth - 9 * channels if k + size == 9 else 0
-        cols = slice(k * channels, (k + size) * channels + extra)
-        groups.append((k, size, cols, extra))
-    return groups
-
-
-def fetch_taps(weight_ref, first, staged, sems, groups):
-    copies = []
-    for n, (k, size, _, _) in enumerate(groups):
-        copies.append(
-            pltpu.make_async_copy(
-                weight_ref.at[pl.ds(first + k, size)],
-                staged.at[pl.ds(k, size)],
-                sems.at[n],
-            )
-        )
-        copies[-1].start()
-    return copies
-
-
-def split_taps(copies, staged, both, groups):
-    channels = staged.shape[1]
-    for copy, (k, size, cols, extra) in zip(copies, groups):
-        copy.wait()
-        parts = [staged[k + n] for n in range(size)]
-        if extra:
-            parts.append(jnp.zeros((channels, extra), jnp.float32))
-        upper, lower = split(jnp.concatenate(parts, axis=1))
-        both[:channels, cols] = upper
-        both[channels:, cols] = lower
+def prepare(weight, steps, depth):
+    channels = weight.shape[1]
+
+    def kernel(weight_ref, *outs):
+        for both, a in zip(outs, range(3 - steps, 3)):
+            for k in range(0, 9, 2):
+                size = min(2, 9 - k)
+                parts = [weight_ref[9 * a + k + n] for n in range(size)]
+                cols = slice(k * channels, (k + size) * channels)
+                if k + size == 9 and depth > 9 * channels:
+                    extra = depth - 9 * channels
+                    parts.append(jnp.zeros((channels, extra), jnp.float32))
+                    cols = slice(k * channels, depth)
+                upper, lower = split(jnp.concatenate(parts, axis=1))
+                both[:channels, cols] = upper
+                both[channels:, cols] = lower
+
+    out_shape = [held((2 * channels, depth), jnp.bfloat16)] * steps
+    return pl.pallas_call(
+        kernel,
+        out_shape=tuple(out_shape),
+        in_specs=[VMEM],
+        out_specs=tuple([VMEM] * steps),
+        compiler_params=GRANT,
+        name="prepare",
+    )(weight)
 
 
 def in_hbm(value):
     return pltpu.with_memory_space_constraint(value, pltpu.HBM)
 
 
-def opening(latents, weight, gain, rows, depth):
+def opening(latents, gain, rows):
     frames, lines, width = latents.shape
     channels = lines // rows
-    groups = tap_groups(channels, depth)
-
-    def kernel(latent_ref, weight_ref, gain_ref, *refs):
-        held_ref, both, gains = refs[:3]
-        outs = refs[3 : 3 + 2 * frames]
-        staged, row, frame_sems, sems, gain_sem = refs[3 + 2 * frames :]
+
+    def kernel(latent_ref, gain_ref, *refs):
+        held_ref, gains = refs[:2]
+        outs = refs[2 : 2 + 2 * frames]
+        row, frame_sems, gain_sem = refs[2 + 2 * frames :]
+        gain_copy = pltpu.make_async_copy(gain_ref, row, gain_sem)
+        gain_copy.start()
         frame_copies = []
         for f in range(frames):
             frame_copies.append(
                 pltpu.make_async_copy(latent_ref.at[f], held_ref.at[f], frame_sems.at[f])
             )
             frame_copies[-1].start()
-        copies = fetch_taps(weight_ref, 18, staged, sems, groups)
-        gain_copy = pltpu.make_async_copy(gain_ref, row, gain_sem)
-        gain_copy.start()
+        gain_copy.wait()
+        square = (channels, channels)
+        lane = lax.broadcasted_iota(jnp.int32, square, 1)
+        sublane = lax.broadcasted_iota(jnp.int32, square, 0)
+        spread = jnp.broadcast_to(row[...], square)
+        column = jnp.sum(jnp.where(lane == sublane, spread, 0.0), axis=1, keepdims=True)
+        gains[...] = jnp.broadcast_to(column, (channels, width))
         even = lax.rem(lax.axis_index("tiles"), 2) == 0
         for f in range(frames):
             frame_copies[f].wait()
@@ -181,57 +178,25 @@
             bottom = held_ref[f, pl.ds(rows - 1, channels, stride=rows), :]
             outs[2 * f][...] = jnp.where(even, bottom, top)
             outs[2 * f + 1][...] = jnp.where(even, top, bottom)
-        split_taps(copies, staged, both, groups)
-        gain_copy.wait()
-        square = (channels, channels)
-        lane = lax.broadcasted_iota(jnp.int32, square, 1)
-        sublane = lax.broadcasted_iota(jnp.int32, square, 0)
-        spread = jnp.broadcast_to(row[...], square)
-        column = jnp.sum(jnp.where(lane == sublane, spread, 0.0), axis=1, keepdims=True)
-        gains[...] = jnp.broadcast_to(column, (channels, width))
-
-    out_shape = [
-        held(latents.shape),
-        held((2 * channels, depth), jnp.bfloat16),
-        held((channels, width)),
-    ] + [held((channels, width))] * (2 * frames)
+
+    out_shape = [held(latents.shape), held((channels, width))]
+    out_shape += [held((channels, width))] * (2 * frames)
     return pl.pallas_call(
         kernel,
         out_shape=tuple(out_shape),
-        in_specs=[HBM, HBM, HBM],
+        in_specs=[HBM, HBM],
         out_specs=tuple([VMEM] * len(out_shape)),
         scratch_shapes=[
-            pltpu.VMEM((9, channels, channels), jnp.float32),
             pltpu.VMEM(gain.shape, jnp.float32),
             pltpu.SemaphoreType.DMA((frames,)),
-            pltpu.SemaphoreType.DMA((len(groups),)),
             pltpu.SemaphoreType.DMA,
         ],
         compiler_params=GRANT,
+        cost_estimate=pl.CostEstimate(
+            flops=2 * 10**9, bytes_accessed=2**20, transcendentals=0
+        ),
         name="opening",
-    )(in_hbm(latents), in_hbm(weight), in_hbm(gain))
-
-
-def earlier_taps(weight, offset, depth):
-    channels = weight.shape[1]
-    groups = tap_groups(channels, depth)
-
-    def kernel(weight_ref, both, staged, sems):
-        copies = fetch_taps(weight_ref, 9 * offset, staged, sems, groups)
-        split_taps(copies, staged, both, groups)
-
-    return pl.pallas_call(
-        kernel,
-        out_shape=held((2 * channels, depth), jnp.bfloat16),
-        in_specs=[HBM],
-        out_specs=VMEM,
-        scratch_shapes=[
-            pltpu.VMEM((9, channels, channels), jnp.float32),
-            pltpu.SemaphoreType.DMA((len(groups),)),
-        ],
-        compiler_params=GRANT,
-        name="earlier_taps",
-    )(in_hbm(weight))
+    )(in_hbm(latents), in_hbm(gain))
 
 
 def normalize(values, gain):
@@ -400,13 +365,12 @@
     of_b = lambda t: partner_b(t, tiles)
 
     flat = latents.reshape(frames, channels * rows, width)
-    flat, current, gains, *edge = opening(flat, conv_weight[0], gain, rows, depth)
+    flat, gains, *edge = opening(flat, gain, rows)
     edge_a, edge_b = edge[0::2], edge[1::2]
     rim_a, rim_b = (rim_pairs(shape, of) for of in (of_a, of_b))
     near_a = [send(edge_a[f], rim_a) for f in range(frames)]
     near_b = [send(edge_b[f], rim_b) for f in range(frames)]
-    earlier = [earlier_taps(conv_weight[0], a, depth) for a in range(3 - steps, 2)]
-    weights = [*earlier, current]
+    weights = prepare(conv_weight[0], steps, depth)
     main = [flat] * frames
 
     for layer in range(sections):

time: 39.9 us -> 37.3 us (0.935)
  Pallas kernels: 7.16 us -> 5.19 us
  starting transfers between devices: 22.8 us -> 22.2 us
    pallas_call x2, Pallas kernels: 3.74 us -> 1.76 us  [the longest x1 1.23 us: opening(): pl.pallas_call(kernel, out_shape=tuple(out_shape), in_specs=[HBM, HBM], o...]
    ppermute x28, starting transfers between devices: 22.8 us -> 22.2 us  [send(): return lax.ppermute(value, ('groups', 'tiles', 'section'), pairs)]
  transfers between devices with their start and end apart: 28 -> 28, of which waited for: 6 -> 6; matrix products, arithmetic and copies ran while one was open for 0% -> 0% of each run, Pallas kernels for 11% -> 9%
where the time goes in v6:
time: 37.3 us; the launch traced here: 37.1 us
  starting transfers between devices  22.2 us (60%)
  waiting for transfers between devices  9.49 us (25%)
  Pallas kernels  5.19 us (14%)
    ppermute x28, starting transfers between devices, send(): return lax.ppermute(value, ('groups', 'tiles', 'section'), pairs)  22.2 us
    ppermute x28, waiting for transfers between devices, send(): return lax.ppermute(value, ('groups', 'tiles', 'section'), pairs)  9.49 us
    pallas_call x8, Pallas kernels, frame_step(): pl.pallas_call(kernel, out_shape=tuple(out_shape), in_specs=[VMEM] * len(...  2.07 us
    pallas_call x1, Pallas kernels, opening(): pl.pallas_call(kernel, out_shape=tuple(out_shape), in_specs=[HBM, HBM], o...  1.23 us
  transfers between devices with their start and end apart: 28, of which 6 were waited for; matrix products, arithmetic and copies ran while one was open for 0% of the time, Pallas kernels for 9%

profile of v6, /device:TPU:0, one launch (start us, length us, event | category | flops | bytes accessed | tf_op | source)
XLA Modules:
  0.0 37.1 jit_solution(3854283613588030533)
XLA Ops:
  0.0 1.2 %opening.1 = (f32[2,384,128]{2,1,0:T(8,128)S(1)}, f32[192,128]{1,0:T(8,128)S(1)}, f32[192,128]{1,0:T(8,128)S(1)}, f32[192,128]{1,0:T(8,128)S(1)}, f32[192,128]{1,0:T(8,128)S(1)}, /*index=5*/f32[192,128]{1,0:T(8,128)S(1)}) custom-call(f32[2,384,128]{2,1,0:T(8,128)} %bitcast.4, f32[1,192]{1,0:T(1,128)} %gain_ref.1), custom_call_target="tpu_custom_call" | custom-call | flops 2000000000 | bytes 1048576 | tf_op jit(solution)/shard_map/opening/pallas_call | solution.py:184
  1.2 3.1 %collective-permute-start = (f32[192,128]{1,0:T(8,128)S(1)}, f32[192,128]{1,0:T(8,128)S(1)}, u32[]{:S(2)}, u32[]{:S(2)}) collective-permute-start(f32[192,128]{1,0:T(8,128)S(1)} %get-tuple-element.48), channel_id=1, source_target_pairs={{0,4},{1,17},{2,3},{3,2},{4,0},{5,21},{6,7},{7,6},{8,12},{9,25},{1... | collective-permute-start | bytes 294920 | tf_op jit(solution)/shard_map/ppermute | solution.py:106
  4.4 0.0 collective-permute-start.1
  4.4 3.1 %collective-permute-start.14 = (f32[192,128]{1,0:T(8,128)S(1)}, f32[192,128]{1,0:T(8,128)S(1)}, u32[]{:S(2)}, u32[]{:S(2)}) collective-permute-start(f32[192,128]{1,0:T(8,128)S(1)} %get-tuple-element.65), channel_id=1, source_target_pairs={{0,4},{1,17},{2,3},{3,2},{4,0},{5,21},{6,7},{7,6},{8,12},{9,25},{1... | collective-permute-start | bytes 294920 | tf_op jit(solution)/shard_map/ppermute | solution.py:106
  7.5 0.5 %prepare.1 = (bf16[384,1792]{1,0:T(8,128)(2,1)S(1)}, bf16[384,1792]{1,0:T(8,128)(2,1)S(1)}) custom-call(f32[27,192,192]{2,1,0:T(8,128)S(1)} %bitcast.3), custom_call_target="tpu_custom_call" | custom-call | tf_op jit(solution)/shard_map/prepare/pallas_call | solution.py:137
  8.1 1.0 %frame_step.8 = (f32[384,128]{1,0:T(8,128)S(1)}, f32[192,128]{1,0:T(8,128)S(1)}, f32[192,128]{1,0:T(8,128)S(1)}, bf16[1792,256]{1,0:T(8,128)(2,1)S(1)}, bf16[1792,256]{1,0:T(8,128)(2,1)S(1)}) custom-call(f32[2,384,128]{2,1,0:T(8,128)S(1)} %get-tuple-element.47.refs_0_, f32[192,128]{1,0:T(8,128)S(1)} %collective-permute-done.refs_1_, ...), custom_call_target="tpu_custom_call" | custom-call | flops 528482304 | bytes 1048576 | tf_op jit(solution)/shard_map/frame_step/pallas_call | solution.py:305
  9.1 0.1 collective-permute-start.2
  9.2 2.1 %collective-permute-start.3 = (f32[192,128]{1,0:T(8,128)S(1)}, f32[192,128]{1,0:T(8,128)S(1)}, u32[]{:S(2)}, u32[]{:S(2)}) collective-permute-start(f32[192,128]{1,0:T(8,128)S(1)} %get-tuple-element.53), channel_id=1, source_target_pairs={{0,5},{1,0},{2,3},{3,2},{4,1},{5,4},{6,7},{7,6},{8,13},{9,8},{10,1... | collective-permute-start | bytes 294920 | tf_op jit(solution)/shard_map/ppermute | solution.py:106
  11.3 0.7 %earlier_frames.4.refs_5_ = f32[192,256]{1,0:T(8,128)S(1)} custom-call(bf16[384,1792]{1,0:T(8,128)(2,1)S(1)} %get-tuple-element.67.refs_0_, bf16[1792,256]{1,0:T(8,128)(2,1)S(1)} %get-tuple-element.68.refs_1_, bf16[1792,256]{1,0:T(8,128)(2,1)S(1)} %get-tuple-element.69.refs_2_), custom_call_target="tpu_custom_call" | custom-call | flops 528482304 | bytes 1048576 | tf_op jit(solution)/shard_map/earlier_frames/pallas_call | solution.py:343
  12.0 1.0 %frame_step.12 = (f32[384,128]{1,0:T(8,128)S(1)}, f32[192,128]{1,0:T(8,128)S(1)}, f32[192,128]{1,0:T(8,128)S(1)}) custom-call(f32[2,384,128]{2,1,0:T(8,128)S(1)} %get-tuple-element.47.refs_0_, f32[192,128]{1,0:T(8,128)S(1)} %collective-permute-done.14.refs_1_, f32[192,128]{1,0:T(8,128)S(1)} %collective-permute-done.15.refs_2_, ...), custom_call_target="tpu_custom_call" | custom-call | flops 528482304 | bytes 1048576 | tf_op jit(solution)/shard_map/frame_step/pallas_call | solution.py:305
  13.1 0.1 collective-permute-start.16
  13.1 2.2 %collective-permute-start.17 = (f32[192,128]{1,0:T(8,128)S(1)}, f32[192,128]{1,0:T(8,128)S(1)}, u32[]{:S(2)}, u32[]{:S(2)}) collective-permute-start(f32[192,128]{1,0:T(8,128)S(1)} %get-tuple-element.71), channel_id=1, source_target_pairs={{0,5},{1,0},{2,3},{3,2},{4,1},{5,4},{6,7},{7,6},{8,13},{9,8},{10,1... | collective-permute-start | bytes 294920 | tf_op jit(solution)/shard_map/ppermute | solution.py:106
  15.4 1.5 %collective-permute-start.5 = (f32[384,128]{1,0:T(8,128)S(1)}, f32[384,128]{1,0:T(8,128)S(1)}, u32[]{:S(2)}, u32[]{:S(2)}) collective-permute-start(f32[384,128]{1,0:T(8,128)S(1)} %get-tuple-element.55), channel_id=1, source_target_pairs={{0,1},{1,2},{2,3},{3,0},{4,5},{5,6},{6,7},{7,4},{8,9},{9,10},{10,1... | collective-permute-start | bytes 589832 | tf_op jit(solution)/shard_map/ppermute | solution.py:106
  16.9 0.1 collective-permute-start.6
  17.0 0.6 %collective-permute-done.17.refs_1_ = f32[192,128]{1,0:T(8,128)S(1)} collective-permute-done((f32[192,128]{1,0:T(8,128)S(1)}, f32[192,128]{1,0:T(8,128)S(1)}, u32[]{:S(2)}, u32[]{:S(2)}) %collective-permute-start.17) | collective-permute-done | bytes 98336 | tf_op jit(solution)/shard_map/ppermute | solution.py:106
  17.5 0.2 collective-permute-start.7
  17.8 1.1 %collective-permute-start.19 = (f32[384,128]{1,0:T(8,128)S(1)}, f32[384,128]{1,0:T(8,128)S(1)}, u32[]{:S(2)}, u32[]{:S(2)}) collective-permute-start(f32[384,128]{1,0:T(8,128)S(1)} %get-tuple-element.75), channel_id=1, source_target_pairs={{0,1},{1,2},{2,3},{3,0},{4,5},{5,6},{6,7},{7,4},{8,9},{9,10},{10,1... | collective-permute-start | bytes 589832 | tf_op jit(solution)/shard_map/ppermute | solution.py:106
  18.9 0.3 collective-permute-start.20
  19.2 2.4 %collective-permute-done.6.refs_1_ = f32[192,128]{1,0:T(8,128)S(1)} collective-permute-done((f32[192,128]{1,0:T(8,128)S(1)}, f32[192,128]{1,0:T(8,128)S(1)}, u32[]{:S(2)}, u32[]{:S(2)}) %collective-permute-start.6) | collective-permute-done | bytes 98336 | tf_op jit(solution)/shard_map/ppermute | solution.py:106
  21.6 1.1 %collective-permute-done.7.refs_2_ = f32[192,128]{1,0:T(8,128)S(1)} collective-permute-done((f32[192,128]{1,0:T(8,128)S(1)}, f32[192,128]{1,0:T(8,128)S(1)}, u32[]{:S(2)}, u32[]{:S(2)}) %collective-permute-start.7) | collective-permute-done | bytes 98336 | tf_op jit(solution)/shard_map/ppermute | solution.py:106
  22.6 0.5 %collective-permute-start.9 = (f32[192,128]{1,0:T(8,128)S(1)}, f32[192,128]{1,0:T(8,128)S(1)}, u32[]{:S(2)}, u32[]{:S(2)}) collective-permute-start(f32[192,128]{1,0:T(8,128)S(1)} %get-tuple-element.59), channel_id=1, source_target_pairs={{0,1},{1,0},{2,7},{3,2},{4,5},{5,4},{6,3},{7,6},{8,9},{9,8},{10,15... | collective-permute-start | bytes 294920 | tf_op jit(solution)/shard_map/ppermute | solution.py:106
  23.1 2.6 %collective-permute-done.20.refs_1_ = f32[192,128]{1,0:T(8,128)S(1)} collective-permute-done((f32[192,128]{1,0:T(8,128)S(1)}, f32[192,128]{1,0:T(8,128)S(1)}, u32[]{:S(2)}, u32[]{:S(2)}) %collective-permute-start.20) | collective-permute-done | bytes 98336 | tf_op jit(solution)/shard_map/ppermute | solution.py:106
  25.8 1.0 %collective-permute-done.21.refs_2_ = f32[192,128]{1,0:T(8,128)S(1)} collective-permute-done((f32[192,128]{1,0:T(8,128)S(1)}, f32[192,128]{1,0:T(8,128)S(1)}, u32[]{:S(2)}, u32[]{:S(2)}) %collective-permute-start.21) | collective-permute-done | bytes 98336 | tf_op jit(solution)/shard_map/ppermute | solution.py:106
  26.8 0.5 %collective-permute-start.23 = (f32[192,128]{1,0:T(8,128)S(1)}, f32[192,128]{1,0:T(8,128)S(1)}, u32[]{:S(2)}, u32[]{:S(2)}) collective-permute-start(f32[192,128]{1,0:T(8,128)S(1)} %get-tuple-element.81), channel_id=1, source_target_pairs={{0,1},{1,0},{2,7},{3,2},{4,5},{5,4},{6,3},{7,6},{8,9},{9,8},{10,15... | collective-permute-start | bytes 294920 | tf_op jit(solution)/shard_map/ppermute | solution.py:106
  27.3 0.0 collective-permute-start.24
  27.4 0.5 %collective-permute-start.11 = (f32[96,128]{1,0:T(8,128)S(1)}, f32[96,128]{1,0:T(8,128)S(1)}, u32[]{:S(2)}, u32[]{:S(2)}) collective-permute-start(f32[96,128]{1,0:T(8,128)S(1)} %get-tuple-element.61), channel_id=1, source_target_pairs={{0,1},{1,2},{2,3},{3,0},{4,5},{5,6},{6,7},{7,4},{8,9},{9,10},{10,1... | collective-permute-start | bytes 147464 | tf_op jit(solution)/shard_map/ppermute | solution.py:106
  27.9 3.7 %collective-permute-start.12 = (f32[96,128]{1,0:T(8,128)S(1)}, f32[96,128]{1,0:T(8,128)S(1)}, u32[]{:S(2)}, u32[]{:S(2)}) collective-permute-start(f32[96,128]{1,0:T(8,128)S(1)} %get-tuple-element.62), channel_id=1, source_target_pairs={{0,3},{1,0},{2,18},{3,1},{4,7},{5,4},{6,22},{7,5},{8,11},{9,8},{10... | collective-permute-start | bytes 147464 | tf_op jit(solution)/shard_map/ppermute | solution.py:106
  31.6 0.5 %collective-permute-start.25 = (f32[96,128]{1,0:T(8,128)S(1)}, f32[96,128]{1,0:T(8,128)S(1)}, u32[]{:S(2)}, u32[]{:S(2)}) collective-permute-start(f32[96,128]{1,0:T(8,128)S(1)} %get-tuple-element.85), channel_id=1, source_target_pairs={{0,1},{1,2},{2,3},{3,0},{4,5},{5,6},{6,7},{7,4},{8,9},{9,10},{10,1... | collective-permute-start | bytes 147464 | tf_op jit(solution)/shard_map/ppermute | solution.py:106
  32.1 2.6 %collective-permute-start.26 = (f32[96,128]{1,0:T(8,128)S(1)}, f32[96,128]{1,0:T(8,128)S(1)}, u32[]{:S(2)}, u32[]{:S(2)}) collective-permute-start(f32[96,128]{1,0:T(8,128)S(1)} %get-tuple-element.86), channel_id=1, source_target_pairs={{0,3},{1,0},{2,18},{3,1},{4,7},{5,4},{6,22},{7,5},{8,11},{9,8},{10... | collective-permute-start | bytes 147464 | tf_op jit(solution)/shard_map/ppermute | solution.py:106
  34.7 1.7 %collective-permute-done.25.refs_4_ = f32[96,128]{1,0:T(8,128)S(1)} collective-permute-done((f32[96,128]{1,0:T(8,128)S(1)}, f32[96,128]{1,0:T(8,128)S(1)}, u32[]{:S(2)}, u32[]{:S(2)}) %collective-permute-start.25) | collective-permute-done | bytes 49184 | tf_op jit(solution)/shard_map/ppermute | solution.py:106
  36.4 0.0 collective-permute-done.26.refs_5_
  36.4 0.7 %assemble.1 = f32[2,96,128]{2,1,0:T(8,128)} custom-call(f32[96,128]{1,0:T(8,128)S(1)} %collective-permute-done.11.refs_0_, f32[96,128]{1,0:T(8,128)S(1)} %collective-permute-done.12.refs_1_, f32[96,128]{1,0:T(8,128)S(1)} %collective-permute-done.13.refs_2_, f32[96,128]{1,0:T(8,128)S(1)} %get-tuple-element.64.refs_3_, ...), custom_call_target="tpu_custom_call" | custom-call | tf_op jit(solution)/shard_map/assemble/pallas_call | solution.py:425
  (41 shorter events, 0.1 us)
Async XLA Ops:
  0.0 7.5 %copy-start = (f32[1,27,192,192]{3,2,1,0:T(8,128)S(1)}, f32[1,27,192,192]{3,2,1,0:T(8,128)}, u32[]{:S(2)}) copy-start(f32[1,27,192,192]{3,2,1,0:T(8,128)} %param.4) | copy-start | bytes 11943940
  1.2 6.8 %collective-permute-start = (f32[192,128]{1,0:T(8,128)S(1)}, f32[192,128]{1,0:T(8,128)S(1)}, u32[]{:S(2)}, u32[]{:S(2)}) collective-permute-start(f32[192,128]{1,0:T(8,128)S(1)} %get-tuple-element.48), channel_id=1, source_target_pairs={{0,4},{1,17},{2,3},{3,2},{4,0},{5,21},{6,7},{7,6},{8,12},{9,25},{1... | collective-permute-start | bytes 294920 | tf_op jit(solution)/shard_map/ppermute | solution.py:106
  4.4 3.7 %collective-permute-start.1 = (f32[192,128]{1,0:T(8,128)S(1)}, f32[192,128]{1,0:T(8,128)S(1)}, u32[]{:S(2)}, u32[]{:S(2)}) collective-permute-start(f32[192,128]{1,0:T(8,128)S(1)} %get-tuple-element.49), channel_id=1, source_target_pairs={{0,1},{1,0},{2,3},{3,2},{4,8},{5,21},{6,7},{7,6},{8,4},{9,25},{10,... | collective-permute-start | bytes 294920 | tf_op jit(solution)/shard_map/ppermute | solution.py:106
  4.4 7.6 %collective-permute-start.14 = (f32[192,128]{1,0:T(8,128)S(1)}, f32[192,128]{1,0:T(8,128)S(1)}, u32[]{:S(2)}, u32[]{:S(2)}) collective-permute-start(f32[192,128]{1,0:T(8,128)S(1)} %get-tuple-element.65), channel_id=1, source_target_pairs={{0,4},{1,17},{2,3},{3,2},{4,0},{5,21},{6,7},{7,6},{8,12},{9,25},{1... | collective-permute-start | bytes 294920 | tf_op jit(solution)/shard_map/ppermute | solution.py:106
  7.5 4.5 %collective-permute-start.15 = (f32[192,128]{1,0:T(8,128)S(1)}, f32[192,128]{1,0:T(8,128)S(1)}, u32[]{:S(2)}, u32[]{:S(2)}) collective-permute-start(f32[192,128]{1,0:T(8,128)S(1)} %get-tuple-element.66), channel_id=1, source_target_pairs={{0,1},{1,0},{2,3},{3,2},{4,8},{5,21},{6,7},{7,6},{8,4},{9,25},{10,... | collective-permute-start | bytes 294920 | tf_op jit(solution)/shard_map/ppermute | solution.py:106
  9.1 6.2 %collective-permute-start.2 = (f32[384,128]{1,0:T(8,128)S(1)}, f32[384,128]{1,0:T(8,128)S(1)}, u32[]{:S(2)}, u32[]{:S(2)}) collective-permute-start(f32[384,128]{1,0:T(8,128)S(1)} %get-tuple-element.52), channel_id=1, source_target_pairs={{0,1},{1,0},{2,3},{3,2},{4,5},{5,4},{6,7},{7,6},{8,9},{9,8},{10,11... | collective-permute-start | bytes 589832 | tf_op jit(solution)/shard_map/ppermute | solution.py:106
  9.2 6.1 %collective-permute-start.3 = (f32[192,128]{1,0:T(8,128)S(1)}, f32[192,128]{1,0:T(8,128)S(1)}, u32[]{:S(2)}, u32[]{:S(2)}) collective-permute-start(f32[192,128]{1,0:T(8,128)S(1)} %get-tuple-element.53), channel_id=1, source_target_pairs={{0,5},{1,0},{2,3},{3,2},{4,1},{5,4},{6,7},{7,6},{8,13},{9,8},{10,1... | collective-permute-start | bytes 294920 | tf_op jit(solution)/shard_map/ppermute | solution.py:106
  11.3 4.0 %collective-permute-start.4 = (f32[192,128]{1,0:T(8,128)S(1)}, f32[192,128]{1,0:T(8,128)S(1)}, u32[]{:S(2)}, u32[]{:S(2)}) collective-permute-start(f32[192,128]{1,0:T(8,128)S(1)} %get-tuple-element.54), channel_id=1, source_target_pairs={{0,1},{1,0},{2,3},{3,2},{4,9},{5,4},{6,7},{7,6},{8,5},{9,8},{10,11... | collective-permute-start | bytes 294920 | tf_op jit(solution)/shard_map/ppermute | solution.py:106
  13.1 4.7 %collective-permute-start.16 = (f32[384,128]{1,0:T(8,128)S(1)}, f32[384,128]{1,0:T(8,128)S(1)}, u32[]{:S(2)}, u32[]{:S(2)}) collective-permute-start(f32[384,128]{1,0:T(8,128)S(1)} %get-tuple-element.70), channel_id=1, source_target_pairs={{0,1},{1,0},{2,3},{3,2},{4,5},{5,4},{6,7},{7,6},{8,9},{9,8},{10,11... | collective-permute-start | bytes 589832 | tf_op jit(solution)/shard_map/ppermute | solution.py:106
  13.1 4.4 %collective-permute-start.17 = (f32[192,128]{1,0:T(8,128)S(1)}, f32[192,128]{1,0:T(8,128)S(1)}, u32[]{:S(2)}, u32[]{:S(2)}) collective-permute-start(f32[192,128]{1,0:T(8,128)S(1)} %get-tuple-element.71), channel_id=1, source_target_pairs={{0,5},{1,0},{2,3},{3,2},{4,1},{5,4},{6,7},{7,6},{8,13},{9,8},{10,1... | collective-permute-start | bytes 294920 | tf_op jit(solution)/shard_map/ppermute | solution.py:106
  15.3 2.4 %collective-permute-start.18 = (f32[192,128]{1,0:T(8,128)S(1)}, f32[192,128]{1,0:T(8,128)S(1)}, u32[]{:S(2)}, u32[]{:S(2)}) collective-permute-start(f32[192,128]{1,0:T(8,128)S(1)} %get-tuple-element.72), channel_id=1, source_target_pairs={{0,1},{1,0},{2,3},{3,2},{4,9},{5,4},{6,7},{7,6},{8,5},{9,8},{10,11... | collective-permute-start | bytes 294920 | tf_op jit(solution)/shard_map/ppermute | solution.py:106
  15.4 7.3 %collective-permute-start.5 = (f32[384,128]{1,0:T(8,128)S(1)}, f32[384,128]{1,0:T(8,128)S(1)}, u32[]{:S(2)}, u32[]{:S(2)}) collective-permute-start(f32[384,128]{1,0:T(8,128)S(1)} %get-tuple-element.55), channel_id=1, source_target_pairs={{0,1},{1,2},{2,3},{3,0},{4,5},{5,6},{6,7},{7,4},{8,9},{9,10},{10,1... | collective-permute-start | bytes 589832 | tf_op jit(solution)/shard_map/ppermute | solution.py:106
  16.9 4.7 %collective-permute-start.6 = (f32[192,128]{1,0:T(8,128)S(1)}, f32[192,128]{1,0:T(8,128)S(1)}, u32[]{:S(2)}, u32[]{:S(2)}) collective-permute-start(f32[192,128]{1,0:T(8,128)S(1)} %get-tuple-element.56), channel_id=1, source_target_pairs={{0,1},{1,6},{2,3},{3,0},{4,5},{5,2},{6,7},{7,4},{8,9},{9,14},{10,1... | collective-permute-start | bytes 294920 | tf_op jit(solution)/shard_map/ppermute | solution.py:106
  17.5 5.1 %collective-permute-start.7 = (f32[192,128]{1,0:T(8,128)S(1)}, f32[192,128]{1,0:T(8,128)S(1)}, u32[]{:S(2)}, u32[]{:S(2)}) collective-permute-start(f32[192,128]{1,0:T(8,128)S(1)} %get-tuple-element.57), channel_id=1, source_target_pairs={{0,1},{1,2},{2,3},{3,0},{4,5},{5,10},{6,7},{7,4},{8,9},{9,6},{10,1... | collective-permute-start | bytes 294920 | tf_op jit(solution)/shard_map/ppermute | solution.py:106
  17.8 9.1 %collective-permute-start.19 = (f32[384,128]{1,0:T(8,128)S(1)}, f32[384,128]{1,0:T(8,128)S(1)}, u32[]{:S(2)}, u32[]{:S(2)}) collective-permute-start(f32[384,128]{1,0:T(8,128)S(1)} %get-tuple-element.75), channel_id=1, source_target_pairs={{0,1},{1,2},{2,3},{3,0},{4,5},{5,6},{6,7},{7,4},{8,9},{9,10},{10,1... | collective-permute-start | bytes 589832 | tf_op jit(solution)/shard_map/ppermute | solution.py:106
  18.9 6.9 %collective-permute-start.20 = (f32[192,128]{1,0:T(8,128)S(1)}, f32[192,128]{1,0:T(8,128)S(1)}, u32[]{:S(2)}, u32[]{:S(2)}) collective-permute-start(f32[192,128]{1,0:T(8,128)S(1)} %get-tuple-element.76), channel_id=1, source_target_pairs={{0,1},{1,6},{2,3},{3,0},{4,5},{5,2},{6,7},{7,4},{8,9},{9,14},{10,1... | collective-permute-start | bytes 294920 | tf_op jit(solution)/shard_map/ppermute | solution.py:106
  21.6 5.3 %collective-permute-start.21 = (f32[192,128]{1,0:T(8,128)S(1)}, f32[192,128]{1,0:T(8,128)S(1)}, u32[]{:S(2)}, u32[]{:S(2)}) collective-permute-start(f32[192,128]{1,0:T(8,128)S(1)} %get-tuple-element.77), channel_id=1, source_target_pairs={{0,1},{1,2},{2,3},{3,0},{4,5},{5,10},{6,7},{7,4},{8,9},{9,6},{10,1... | collective-permute-start | bytes 294920 | tf_op jit(solution)/shard_map/ppermute | solution.py:106
  22.6 4.8 %collective-permute-start.8 = (f32[384,128]{1,0:T(8,128)S(1)}, f32[384,128]{1,0:T(8,128)S(1)}, u32[]{:S(2)}, u32[]{:S(2)}) collective-permute-start(f32[384,128]{1,0:T(8,128)S(1)} %get-tuple-element.58), channel_id=1, source_target_pairs={{0,1},{1,0},{2,3},{3,2},{4,5},{5,4},{6,7},{7,6},{8,9},{9,8},{10,11... | collective-permute-start | bytes 589832 | tf_op jit(solution)/shard_map/ppermute | solution.py:106
  22.6 4.7 %collective-permute-start.9 = (f32[192,128]{1,0:T(8,128)S(1)}, f32[192,128]{1,0:T(8,128)S(1)}, u32[]{:S(2)}, u32[]{:S(2)}) collective-permute-start(f32[192,128]{1,0:T(8,128)S(1)} %get-tuple-element.59), channel_id=1, source_target_pairs={{0,1},{1,0},{2,7},{3,2},{4,5},{5,4},{6,3},{7,6},{8,9},{9,8},{10,15... | collective-permute-start | bytes 294920 | tf_op jit(solution)/shard_map/ppermute | solution.py:106
  25.8 1.6 %collective-permute-start.10 = (f32[192,128]{1,0:T(8,128)S(1)}, f32[192,128]{1,0:T(8,128)S(1)}, u32[]{:S(2)}, u32[]{:S(2)}) collective-permute-start(f32[192,128]{1,0:T(8,128)S(1)} %get-tuple-element.60), channel_id=1, source_target_pairs={{0,1},{1,0},{2,3},{3,2},{4,5},{5,4},{6,11},{7,6},{8,9},{9,8},{10,7... | collective-permute-start | bytes 294920 | tf_op jit(solution)/shard_map/ppermute | solution.py:106
  26.8 4.7 %collective-permute-start.22 = (f32[384,128]{1,0:T(8,128)S(1)}, f32[384,128]{1,0:T(8,128)S(1)}, u32[]{:S(2)}, u32[]{:S(2)}) collective-permute-start(f32[384,128]{1,0:T(8,128)S(1)} %get-tuple-element.80), channel_id=1, source_target_pairs={{0,1},{1,0},{2,3},{3,2},{4,5},{5,4},{6,7},{7,6},{8,9},{9,8},{10,11... | collective-permute-start | bytes 589832 | tf_op jit(solution)/shard_map/ppermute | solution.py:106
  26.8 4.7 %collective-permute-start.23 = (f32[192,128]{1,0:T(8,128)S(1)}, f32[192,128]{1,0:T(8,128)S(1)}, u32[]{:S(2)}, u32[]{:S(2)}) collective-permute-start(f32[192,128]{1,0:T(8,128)S(1)} %get-tuple-element.81), channel_id=1, source_target_pairs={{0,1},{1,0},{2,7},{3,2},{4,5},{5,4},{6,3},{7,6},{8,9},{9,8},{10,15... | collective-permute-start | bytes 294920 | tf_op jit(solution)/shard_map/ppermute | solution.py:106
  27.3 4.2 %collective-permute-start.24 = (f32[192,128]{1,0:T(8,128)S(1)}, f32[192,128]{1,0:T(8,128)S(1)}, u32[]{:S(2)}, u32[]{:S(2)}) collective-permute-start(f32[192,128]{1,0:T(8,128)S(1)} %get-tuple-element.82), channel_id=1, source_target_pairs={{0,1},{1,0},{2,3},{3,2},{4,5},{5,4},{6,11},{7,6},{8,9},{9,8},{10,7... | collective-permute-start | bytes 294920 | tf_op jit(solution)/shard_map/ppermute | solution.py:106
  27.4 7.3 %collective-permute-start.11 = (f32[96,128]{1,0:T(8,128)S(1)}, f32[96,128]{1,0:T(8,128)S(1)}, u32[]{:S(2)}, u32[]{:S(2)}) collective-permute-start(f32[96,128]{1,0:T(8,128)S(1)} %get-tuple-element.61), channel_id=1, source_target_pairs={{0,1},{1,2},{2,3},{3,0},{4,5},{5,6},{6,7},{7,4},{8,9},{9,10},{10,1... | collective-permute-start | bytes 147464 | tf_op jit(solution)/shard_map/ppermute | solution.py:106
  27.9 6.8 %collective-permute-start.12 = (f32[96,128]{1,0:T(8,128)S(1)}, f32[96,128]{1,0:T(8,128)S(1)}, u32[]{:S(2)}, u32[]{:S(2)}) collective-permute-start(f32[96,128]{1,0:T(8,128)S(1)} %get-tuple-element.62), channel_id=1, source_target_pairs={{0,3},{1,0},{2,18},{3,1},{4,7},{5,4},{6,22},{7,5},{8,11},{9,8},{10... | collective-permute-start | bytes 147464 | tf_op jit(solution)/shard_map/ppermute | solution.py:106
  31.5 3.1 %collective-permute-start.13 = (f32[96,128]{1,0:T(8,128)S(1)}, f32[96,128]{1,0:T(8,128)S(1)}, u32[]{:S(2)}, u32[]{:S(2)}) collective-permute-start(f32[96,128]{1,0:T(8,128)S(1)} %get-tuple-element.63), channel_id=1, source_target_pairs={{0,1},{1,0},{2,3},{3,2},{4,5},{5,4},{6,7},{7,6},{8,9},{9,8},{10,11... | collective-permute-start | bytes 147464 | tf_op jit(solution)/shard_map/ppermute | solution.py:106
  31.6 4.8 %collective-permute-start.25 = (f32[96,128]{1,0:T(8,128)S(1)}, f32[96,128]{1,0:T(8,128)S(1)}, u32[]{:S(2)}, u32[]{:S(2)}) collective-permute-start(f32[96,128]{1,0:T(8,128)S(1)} %get-tuple-element.85), channel_id=1, source_target_pairs={{0,1},{1,2},{2,3},{3,0},{4,5},{5,6},{6,7},{7,4},{8,9},{9,10},{10,1... | collective-permute-start | bytes 147464 | tf_op jit(solution)/shard_map/ppermute | solution.py:106
  32.1 4.3 %collective-permute-start.26 = (f32[96,128]{1,0:T(8,128)S(1)}, f32[96,128]{1,0:T(8,128)S(1)}, u32[]{:S(2)}, u32[]{:S(2)}) collective-permute-start(f32[96,128]{1,0:T(8,128)S(1)} %get-tuple-element.86), channel_id=1, source_target_pairs={{0,3},{1,0},{2,18},{3,1},{4,7},{5,4},{6,22},{7,5},{8,11},{9,8},{10... | collective-permute-start | bytes 147464 | tf_op jit(solution)/shard_map/ppermute | solution.py:106
  34.7 1.8 %collective-permute-start.27 = (f32[96,128]{1,0:T(8,128)S(1)}, f32[96,128]{1,0:T(8,128)S(1)}, u32[]{:S(2)}, u32[]{:S(2)}) collective-permute-start(f32[96,128]{1,0:T(8,128)S(1)} %get-tuple-element.87), channel_id=1, source_target_pairs={{0,1},{1,0},{2,3},{3,2},{4,5},{5,4},{6,7},{7,6},{8,9},{9,8},{10,11... | collective-permute-start | bytes 147464 | tf_op jit(solution)/shard_map/ppermute | solution.py:106

commit v7 on v6

--- a/solution.py
+++ b/solution.py
@@ -27,9 +27,11 @@
         where[name] = names[(k + 1) % len(names)]
 
 
-def section_hop(layer, sections):
+def section_hop(layer, sections, early=False):
     where = {}
-    if layer % 2 == 0:
+    if early and layer + 3 < sections:
+        idle_cycle(where, [layer, layer + 1, layer + 2, layer + 3])
+    elif layer % 2 == 0:
         idle_cycle(where, [layer, layer + 1])
     elif layer + 2 < sections:
         idle_cycle(where, [layer - 1, layer, layer + 1, layer + 2])
@@ -59,8 +61,8 @@
     return g ^ 1 if (g ^ 1) < groups else g
 
 
-def hop_pairs(layer, shape, tile_of):
-    hop = section_hop(layer, shape[2])
+def hop_pairs(layer, shape, tile_of, early=False):
+    hop = section_hop(layer, shape[2], early)
     return all_pairs(
         shape, lambda g, t, s: (g, tile_of(t) if s == layer else t, hop[s])
     )
@@ -375,8 +377,9 @@
 
     for layer in range(sections):
         if layer > 0:
+            early = layer == 1
             straight = hop_pairs(layer - 1, shape, lambda t: t)
-            cross_a = hop_pairs(layer - 1, shape, of_a)
+            cross_a = hop_pairs(layer - 1, shape, of_a, early)
             cross_b = hop_pairs(layer - 1, shape, of_b)
             main = [send(main[f], straight) for f in range(frames)]
             near_a = [send(edge_a[f], cross_a) for f in range(frames)]

time: 37.3 us -> 37.4 us (level)
  no operation moved by 1% of the time
where the time goes in v7:
time: 37.4 us; the launch traced here: 37.3 us
  starting transfers between devices  22.4 us (60%)
  waiting for transfers between devices  9.49 us (25%)
  Pallas kernels  5.19 us (14%)
    ppermute x28, starting transfers between devices, send(): return lax.ppermute(value, ('groups', 'tiles', 'section'), pairs)  22.4 us
    ppermute x28, waiting for transfers between devices, send(): return lax.ppermute(value, ('groups', 'tiles', 'section'), pairs)  9.49 us
    pallas_call x8, Pallas kernels, frame_step(): pl.pallas_call(kernel, out_shape=tuple(out_shape), in_specs=[VMEM] * len(...  2.07 us
    pallas_call x1, Pallas kernels, opening(): pl.pallas_call(kernel, out_shape=tuple(out_shape), in_specs=[HBM, HBM], o...  1.23 us
  transfers between devices with their start and end apart: 28, of which 6 were waited for; matrix products, arithmetic and copies ran while one was open for 0% of the time, Pallas kernels for 9%

profile of v7, /device:TPU:0, one launch (start us, length us, event | category | flops | bytes accessed | tf_op | source)
XLA Modules:
  0.0 37.3 jit_solution(6765415259095533334)
XLA Ops:
  0.0 1.2 %opening.1 = (f32[2,384,128]{2,1,0:T(8,128)S(1)}, f32[192,128]{1,0:T(8,128)S(1)}, f32[192,128]{1,0:T(8,128)S(1)}, f32[192,128]{1,0:T(8,128)S(1)}, f32[192,128]{1,0:T(8,128)S(1)}, /*index=5*/f32[192,128]{1,0:T(8,128)S(1)}) custom-call(f32[2,384,128]{2,1,0:T(8,128)} %bitcast.4, f32[1,192]{1,0:T(1,128)} %gain_ref.1), custom_call_target="tpu_custom_call" | custom-call | flops 2000000000 | bytes 1048576 | tf_op jit(solution)/shard_map/opening/pallas_call | solution.py:186
  1.2 3.1 %collective-permute-start = (f32[192,128]{1,0:T(8,128)S(1)}, f32[192,128]{1,0:T(8,128)S(1)}, u32[]{:S(2)}, u32[]{:S(2)}) collective-permute-start(f32[192,128]{1,0:T(8,128)S(1)} %get-tuple-element.48), channel_id=1, source_target_pairs={{0,4},{1,17},{2,3},{3,2},{4,0},{5,21},{6,7},{7,6},{8,12},{9,25},{1... | collective-permute-start | bytes 294920 | tf_op jit(solution)/shard_map/ppermute | solution.py:108
  4.4 3.1 %collective-permute-start.14 = (f32[192,128]{1,0:T(8,128)S(1)}, f32[192,128]{1,0:T(8,128)S(1)}, u32[]{:S(2)}, u32[]{:S(2)}) collective-permute-start(f32[192,128]{1,0:T(8,128)S(1)} %get-tuple-element.65), channel_id=1, source_target_pairs={{0,4},{1,17},{2,3},{3,2},{4,0},{5,21},{6,7},{7,6},{8,12},{9,25},{1... | collective-permute-start | bytes 294920 | tf_op jit(solution)/shard_map/ppermute | solution.py:108
  7.5 0.5 %prepare.1 = (bf16[384,1792]{1,0:T(8,128)(2,1)S(1)}, bf16[384,1792]{1,0:T(8,128)(2,1)S(1)}) custom-call(f32[27,192,192]{2,1,0:T(8,128)S(1)} %bitcast.3), custom_call_target="tpu_custom_call" | custom-call | tf_op jit(solution)/shard_map/prepare/pallas_call | solution.py:139
  8.1 1.0 %frame_step.8 = (f32[384,128]{1,0:T(8,128)S(1)}, f32[192,128]{1,0:T(8,128)S(1)}, f32[192,128]{1,0:T(8,128)S(1)}, bf16[1792,256]{1,0:T(8,128)(2,1)S(1)}, bf16[1792,256]{1,0:T(8,128)(2,1)S(1)}) custom-call(f32[2,384,128]{2,1,0:T(8,128)S(1)} %get-tuple-element.47.refs_0_, f32[192,128]{1,0:T(8,128)S(1)} %collective-permute-done.refs_1_, ...), custom_call_target="tpu_custom_call" | custom-call | flops 528482304 | bytes 1048576 | tf_op jit(solution)/shard_map/frame_step/pallas_call | solution.py:307
  9.1 0.1 collective-permute-start.2
  9.2 2.1 %collective-permute-start.3 = (f32[192,128]{1,0:T(8,128)S(1)}, f32[192,128]{1,0:T(8,128)S(1)}, u32[]{:S(2)}, u32[]{:S(2)}) collective-permute-start(f32[192,128]{1,0:T(8,128)S(1)} %get-tuple-element.53), channel_id=1, source_target_pairs={{0,5},{1,2},{2,3},{3,0},{4,1},{5,6},{6,7},{7,4},{8,13},{9,10},{10,... | collective-permute-start | bytes 294920 | tf_op jit(solution)/shard_map/ppermute | solution.py:108
  11.3 0.7 %earlier_frames.4.refs_5_ = f32[192,256]{1,0:T(8,128)S(1)} custom-call(bf16[384,1792]{1,0:T(8,128)(2,1)S(1)} %get-tuple-element.67.refs_0_, bf16[1792,256]{1,0:T(8,128)(2,1)S(1)} %get-tuple-element.68.refs_1_, bf16[1792,256]{1,0:T(8,128)(2,1)S(1)} %get-tuple-element.69.refs_2_), custom_call_target="tpu_custom_call" | custom-call | flops 528482304 | bytes 1048576 | tf_op jit(solution)/shard_map/earlier_frames/pallas_call | solution.py:345
  12.0 1.0 %frame_step.12 = (f32[384,128]{1,0:T(8,128)S(1)}, f32[192,128]{1,0:T(8,128)S(1)}, f32[192,128]{1,0:T(8,128)S(1)}) custom-call(f32[2,384,128]{2,1,0:T(8,128)S(1)} %get-tuple-element.47.refs_0_, f32[192,128]{1,0:T(8,128)S(1)} %collective-permute-done.14.refs_1_, f32[192,128]{1,0:T(8,128)S(1)} %collective-permute-done.15.refs_2_, ...), custom_call_target="tpu_custom_call" | custom-call | flops 528482304 | bytes 1048576 | tf_op jit(solution)/shard_map/frame_step/pallas_call | solution.py:307
  13.1 0.1 collective-permute-start.16
  13.1 2.1 %collective-permute-start.17 = (f32[192,128]{1,0:T(8,128)S(1)}, f32[192,128]{1,0:T(8,128)S(1)}, u32[]{:S(2)}, u32[]{:S(2)}) collective-permute-start(f32[192,128]{1,0:T(8,128)S(1)} %get-tuple-element.71), channel_id=1, source_target_pairs={{0,5},{1,2},{2,3},{3,0},{4,1},{5,6},{6,7},{7,4},{8,13},{9,10},{10,... | collective-permute-start | bytes 294920 | tf_op jit(solution)/shard_map/ppermute | solution.py:108
  15.3 1.5 %collective-permute-start.5 = (f32[384,128]{1,0:T(8,128)S(1)}, f32[384,128]{1,0:T(8,128)S(1)}, u32[]{:S(2)}, u32[]{:S(2)}) collective-permute-start(f32[384,128]{1,0:T(8,128)S(1)} %get-tuple-element.55), channel_id=1, source_target_pairs={{0,1},{1,2},{2,3},{3,0},{4,5},{5,6},{6,7},{7,4},{8,9},{9,10},{10,1... | collective-permute-start | bytes 589832 | tf_op jit(solution)/shard_map/ppermute | solution.py:108
  16.8 0.1 collective-permute-start.6
  16.9 0.6 %collective-permute-done.17.refs_1_ = f32[192,128]{1,0:T(8,128)S(1)} collective-permute-done((f32[192,128]{1,0:T(8,128)S(1)}, f32[192,128]{1,0:T(8,128)S(1)}, u32[]{:S(2)}, u32[]{:S(2)}) %collective-permute-start.17) | collective-permute-done | bytes 98336 | tf_op jit(solution)/shard_map/ppermute | solution.py:108
  17.5 0.3 collective-permute-start.7
  17.8 1.1 %collective-permute-start.19 = (f32[384,128]{1,0:T(8,128)S(1)}, f32[384,128]{1,0:T(8,128)S(1)}, u32[]{:S(2)}, u32[]{:S(2)}) collective-permute-start(f32[384,128]{1,0:T(8,128)S(1)} %get-tuple-element.75), channel_id=1, source_target_pairs={{0,1},{1,2},{2,3},{3,0},{4,5},{5,6},{6,7},{7,4},{8,9},{9,10},{10,1... | collective-permute-start | bytes 589832 | tf_op jit(solution)/shard_map/ppermute | solution.py:108
  18.9 0.2 collective-permute-start.20
  19.1 2.4 %collective-permute-done.6.refs_1_ = f32[192,128]{1,0:T(8,128)S(1)} collective-permute-done((f32[192,128]{1,0:T(8,128)S(1)}, f32[192,128]{1,0:T(8,128)S(1)}, u32[]{:S(2)}, u32[]{:S(2)}) %collective-permute-start.6) | collective-permute-done | bytes 98336 | tf_op jit(solution)/shard_map/ppermute | solution.py:108
  21.5 1.1 %collective-permute-done.7.refs_2_ = f32[192,128]{1,0:T(8,128)S(1)} collective-permute-done((f32[192,128]{1,0:T(8,128)S(1)}, f32[192,128]{1,0:T(8,128)S(1)}, u32[]{:S(2)}, u32[]{:S(2)}) %collective-permute-start.7) | collective-permute-done | bytes 98336 | tf_op jit(solution)/shard_map/ppermute | solution.py:108
  22.6 0.1 collective-permute-start.8
  22.6 0.4 %collective-permute-start.9 = (f32[192,128]{1,0:T(8,128)S(1)}, f32[192,128]{1,0:T(8,128)S(1)}, u32[]{:S(2)}, u32[]{:S(2)}) collective-permute-start(f32[192,128]{1,0:T(8,128)S(1)} %get-tuple-element.59), channel_id=1, source_target_pairs={{0,1},{1,0},{2,7},{3,2},{4,5},{5,4},{6,3},{7,6},{8,9},{9,8},{10,15... | collective-permute-start | bytes 294920 | tf_op jit(solution)/shard_map/ppermute | solution.py:108
  23.1 2.6 %collective-permute-done.20.refs_1_ = f32[192,128]{1,0:T(8,128)S(1)} collective-permute-done((f32[192,128]{1,0:T(8,128)S(1)}, f32[192,128]{1,0:T(8,128)S(1)}, u32[]{:S(2)}, u32[]{:S(2)}) %collective-permute-start.20) | collective-permute-done | bytes 98336 | tf_op jit(solution)/shard_map/ppermute | solution.py:108
  25.7 1.0 %collective-permute-done.21.refs_2_ = f32[192,128]{1,0:T(8,128)S(1)} collective-permute-done((f32[192,128]{1,0:T(8,128)S(1)}, f32[192,128]{1,0:T(8,128)S(1)}, u32[]{:S(2)}, u32[]{:S(2)}) %collective-permute-start.21) | collective-permute-done | bytes 98336 | tf_op jit(solution)/shard_map/ppermute | solution.py:108
  26.8 0.5 %collective-permute-start.23 = (f32[192,128]{1,0:T(8,128)S(1)}, f32[192,128]{1,0:T(8,128)S(1)}, u32[]{:S(2)}, u32[]{:S(2)}) collective-permute-start(f32[192,128]{1,0:T(8,128)S(1)} %get-tuple-element.81), channel_id=1, source_target_pairs={{0,1},{1,0},{2,7},{3,2},{4,5},{5,4},{6,3},{7,6},{8,9},{9,8},{10,15... | collective-permute-start | bytes 294920 | tf_op jit(solution)/shard_map/ppermute | solution.py:108
  27.3 0.0 collective-permute-start.24
  27.3 0.5 %collective-permute-start.11 = (f32[96,128]{1,0:T(8,128)S(1)}, f32[96,128]{1,0:T(8,128)S(1)}, u32[]{:S(2)}, u32[]{:S(2)}) collective-permute-start(f32[96,128]{1,0:T(8,128)S(1)} %get-tuple-element.61), channel_id=1, source_target_pairs={{0,1},{1,2},{2,3},{3,0},{4,5},{5,6},{6,7},{7,4},{8,9},{9,10},{10,1... | collective-permute-start | bytes 147464 | tf_op jit(solution)/shard_map/ppermute | solution.py:108
  27.8 3.7 %collective-permute-start.12 = (f32[96,128]{1,0:T(8,128)S(1)}, f32[96,128]{1,0:T(8,128)S(1)}, u32[]{:S(2)}, u32[]{:S(2)}) collective-permute-start(f32[96,128]{1,0:T(8,128)S(1)} %get-tuple-element.62), channel_id=1, source_target_pairs={{0,3},{1,0},{2,18},{3,1},{4,7},{5,4},{6,22},{7,5},{8,11},{9,8},{10... | collective-permute-start | bytes 147464 | tf_op jit(solution)/shard_map/ppermute | solution.py:108
  31.5 0.5 %collective-permute-start.25 = (f32[96,128]{1,0:T(8,128)S(1)}, f32[96,128]{1,0:T(8,128)S(1)}, u32[]{:S(2)}, u32[]{:S(2)}) collective-permute-start(f32[96,128]{1,0:T(8,128)S(1)} %get-tuple-element.85), channel_id=1, source_target_pairs={{0,1},{1,2},{2,3},{3,0},{4,5},{5,6},{6,7},{7,4},{8,9},{9,10},{10,1... | collective-permute-start | bytes 147464 | tf_op jit(solution)/shard_map/ppermute | solution.py:108
  32.0 2.9 %collective-permute-start.26 = (f32[96,128]{1,0:T(8,128)S(1)}, f32[96,128]{1,0:T(8,128)S(1)}, u32[]{:S(2)}, u32[]{:S(2)}) collective-permute-start(f32[96,128]{1,0:T(8,128)S(1)} %get-tuple-element.86), channel_id=1, source_target_pairs={{0,3},{1,0},{2,18},{3,1},{4,7},{5,4},{6,22},{7,5},{8,11},{9,8},{10... | collective-permute-start | bytes 147464 | tf_op jit(solution)/shard_map/ppermute | solution.py:108
  34.9 1.7 %collective-permute-done.25.refs_4_ = f32[96,128]{1,0:T(8,128)S(1)} collective-permute-done((f32[96,128]{1,0:T(8,128)S(1)}, f32[96,128]{1,0:T(8,128)S(1)}, u32[]{:S(2)}, u32[]{:S(2)}) %collective-permute-start.25) | collective-permute-done | bytes 49184 | tf_op jit(solution)/shard_map/ppermute | solution.py:108
  36.5 0.0 collective-permute-done.26.refs_5_
  36.6 0.7 %assemble.1 = f32[2,96,128]{2,1,0:T(8,128)} custom-call(f32[96,128]{1,0:T(8,128)S(1)} %collective-permute-done.11.refs_0_, f32[96,128]{1,0:T(8,128)S(1)} %collective-permute-done.12.refs_1_, f32[96,128]{1,0:T(8,128)S(1)} %collective-permute-done.13.refs_2_, f32[96,128]{1,0:T(8,128)S(1)} %get-tuple-element.64.refs_3_, ...), custom_call_target="tpu_custom_call" | custom-call | tf_op jit(solution)/shard_map/assemble/pallas_call | solution.py:428
  (41 shorter events, 0.1 us)
Async XLA Ops:
  0.0 7.5 %copy-start = (f32[1,27,192,192]{3,2,1,0:T(8,128)S(1)}, f32[1,27,192,192]{3,2,1,0:T(8,128)}, u32[]{:S(2)}) copy-start(f32[1,27,192,192]{3,2,1,0:T(8,128)} %param.4) | copy-start | bytes 11943940
  1.2 6.8 %collective-permute-start = (f32[192,128]{1,0:T(8,128)S(1)}, f32[192,128]{1,0:T(8,128)S(1)}, u32[]{:S(2)}, u32[]{:S(2)}) collective-permute-start(f32[192,128]{1,0:T(8,128)S(1)} %get-tuple-element.48), channel_id=1, source_target_pairs={{0,4},{1,17},{2,3},{3,2},{4,0},{5,21},{6,7},{7,6},{8,12},{9,25},{1... | collective-permute-start | bytes 294920 | tf_op jit(solution)/shard_map/ppermute | solution.py:108
  4.4 3.7 %collective-permute-start.1 = (f32[192,128]{1,0:T(8,128)S(1)}, f32[192,128]{1,0:T(8,128)S(1)}, u32[]{:S(2)}, u32[]{:S(2)}) collective-permute-start(f32[192,128]{1,0:T(8,128)S(1)} %get-tuple-element.49), channel_id=1, source_target_pairs={{0,1},{1,0},{2,3},{3,2},{4,8},{5,21},{6,7},{7,6},{8,4},{9,25},{10,... | collective-permute-start | bytes 294920 | tf_op jit(solution)/shard_map/ppermute | solution.py:108
  4.4 7.6 %collective-permute-start.14 = (f32[192,128]{1,0:T(8,128)S(1)}, f32[192,128]{1,0:T(8,128)S(1)}, u32[]{:S(2)}, u32[]{:S(2)}) collective-permute-start(f32[192,128]{1,0:T(8,128)S(1)} %get-tuple-element.65), channel_id=1, source_target_pairs={{0,4},{1,17},{2,3},{3,2},{4,0},{5,21},{6,7},{7,6},{8,12},{9,25},{1... | collective-permute-start | bytes 294920 | tf_op jit(solution)/shard_map/ppermute | solution.py:108
  7.5 4.5 %collective-permute-start.15 = (f32[192,128]{1,0:T(8,128)S(1)}, f32[192,128]{1,0:T(8,128)S(1)}, u32[]{:S(2)}, u32[]{:S(2)}) collective-permute-start(f32[192,128]{1,0:T(8,128)S(1)} %get-tuple-element.66), channel_id=1, source_target_pairs={{0,1},{1,0},{2,3},{3,2},{4,8},{5,21},{6,7},{7,6},{8,4},{9,25},{10,... | collective-permute-start | bytes 294920 | tf_op jit(solution)/shard_map/ppermute | solution.py:108
  9.1 6.2 %collective-permute-start.2 = (f32[384,128]{1,0:T(8,128)S(1)}, f32[384,128]{1,0:T(8,128)S(1)}, u32[]{:S(2)}, u32[]{:S(2)}) collective-permute-start(f32[384,128]{1,0:T(8,128)S(1)} %get-tuple-element.52), channel_id=1, source_target_pairs={{0,1},{1,0},{2,3},{3,2},{4,5},{5,4},{6,7},{7,6},{8,9},{9,8},{10,11... | collective-permute-start | bytes 589832 | tf_op jit(solution)/shard_map/ppermute | solution.py:108
  9.2 6.1 %collective-permute-start.3 = (f32[192,128]{1,0:T(8,128)S(1)}, f32[192,128]{1,0:T(8,128)S(1)}, u32[]{:S(2)}, u32[]{:S(2)}) collective-permute-start(f32[192,128]{1,0:T(8,128)S(1)} %get-tuple-element.53), channel_id=1, source_target_pairs={{0,5},{1,2},{2,3},{3,0},{4,1},{5,6},{6,7},{7,4},{8,13},{9,10},{10,... | collective-permute-start | bytes 294920 | tf_op jit(solution)/shard_map/ppermute | solution.py:108
  11.3 4.0 %collective-permute-start.4 = (f32[192,128]{1,0:T(8,128)S(1)}, f32[192,128]{1,0:T(8,128)S(1)}, u32[]{:S(2)}, u32[]{:S(2)}) collective-permute-start(f32[192,128]{1,0:T(8,128)S(1)} %get-tuple-element.54), channel_id=1, source_target_pairs={{0,1},{1,0},{2,3},{3,2},{4,9},{5,4},{6,7},{7,6},{8,5},{9,8},{10,11... | collective-permute-start | bytes 294920 | tf_op jit(solution)/shard_map/ppermute | solution.py:108
  13.1 4.7 %collective-permute-start.16 = (f32[384,128]{1,0:T(8,128)S(1)}, f32[384,128]{1,0:T(8,128)S(1)}, u32[]{:S(2)}, u32[]{:S(2)}) collective-permute-start(f32[384,128]{1,0:T(8,128)S(1)} %get-tuple-element.70), channel_id=1, source_target_pairs={{0,1},{1,0},{2,3},{3,2},{4,5},{5,4},{6,7},{7,6},{8,9},{9,8},{10,11... | collective-permute-start | bytes 589832 | tf_op jit(solution)/shard_map/ppermute | solution.py:108
  13.1 4.3 %collective-permute-start.17 = (f32[192,128]{1,0:T(8,128)S(1)}, f32[192,128]{1,0:T(8,128)S(1)}, u32[]{:S(2)}, u32[]{:S(2)}) collective-permute-start(f32[192,128]{1,0:T(8,128)S(1)} %get-tuple-element.71), channel_id=1, source_target_pairs={{0,5},{1,2},{2,3},{3,0},{4,1},{5,6},{6,7},{7,4},{8,13},{9,10},{10,... | collective-permute-start | bytes 294920 | tf_op jit(solution)/shard_map/ppermute | solution.py:108
  15.3 2.5 %collective-permute-start.18 = (f32[192,128]{1,0:T(8,128)S(1)}, f32[192,128]{1,0:T(8,128)S(1)}, u32[]{:S(2)}, u32[]{:S(2)}) collective-permute-start(f32[192,128]{1,0:T(8,128)S(1)} %get-tuple-element.72), channel_id=1, source_target_pairs={{0,1},{1,0},{2,3},{3,2},{4,9},{5,4},{6,7},{7,6},{8,5},{9,8},{10,11... | collective-permute-start | bytes 294920 | tf_op jit(solution)/shard_map/ppermute | solution.py:108
  15.3 7.3 %collective-permute-start.5 = (f32[384,128]{1,0:T(8,128)S(1)}, f32[384,128]{1,0:T(8,128)S(1)}, u32[]{:S(2)}, u32[]{:S(2)}) collective-permute-start(f32[384,128]{1,0:T(8,128)S(1)} %get-tuple-element.55), channel_id=1, source_target_pairs={{0,1},{1,2},{2,3},{3,0},{4,5},{5,6},{6,7},{7,4},{8,9},{9,10},{10,1... | collective-permute-start | bytes 589832 | tf_op jit(solution)/shard_map/ppermute | solution.py:108
  16.8 4.7 %collective-permute-start.6 = (f32[192,128]{1,0:T(8,128)S(1)}, f32[192,128]{1,0:T(8,128)S(1)}, u32[]{:S(2)}, u32[]{:S(2)}) collective-permute-start(f32[192,128]{1,0:T(8,128)S(1)} %get-tuple-element.56), channel_id=1, source_target_pairs={{0,1},{1,6},{2,3},{3,0},{4,5},{5,2},{6,7},{7,4},{8,9},{9,14},{10,1... | collective-permute-start | bytes 294920 | tf_op jit(solution)/shard_map/ppermute | solution.py:108
  17.5 5.1 %collective-permute-start.7 = (f32[192,128]{1,0:T(8,128)S(1)}, f32[192,128]{1,0:T(8,128)S(1)}, u32[]{:S(2)}, u32[]{:S(2)}) collective-permute-start(f32[192,128]{1,0:T(8,128)S(1)} %get-tuple-element.57), channel_id=1, source_target_pairs={{0,1},{1,2},{2,3},{3,0},{4,5},{5,10},{6,7},{7,4},{8,9},{9,6},{10,1... | collective-permute-start | bytes 294920 | tf_op jit(solution)/shard_map/ppermute | solution.py:108
  17.8 9.0 %collective-permute-start.19 = (f32[384,128]{1,0:T(8,128)S(1)}, f32[384,128]{1,0:T(8,128)S(1)}, u32[]{:S(2)}, u32[]{:S(2)}) collective-permute-start(f32[384,128]{1,0:T(8,128)S(1)} %get-tuple-element.75), channel_id=1, source_target_pairs={{0,1},{1,2},{2,3},{3,0},{4,5},{5,6},{6,7},{7,4},{8,9},{9,10},{10,1... | collective-permute-start | bytes 589832 | tf_op jit(solution)/shard_map/ppermute | solution.py:108
  18.9 6.8 %collective-permute-start.20 = (f32[192,128]{1,0:T(8,128)S(1)}, f32[192,128]{1,0:T(8,128)S(1)}, u32[]{:S(2)}, u32[]{:S(2)}) collective-permute-start(f32[192,128]{1,0:T(8,128)S(1)} %get-tuple-element.76), channel_id=1, source_target_pairs={{0,1},{1,6},{2,3},{3,0},{4,5},{5,2},{6,7},{7,4},{8,9},{9,14},{10,1... | collective-permute-start | bytes 294920 | tf_op jit(solution)/shard_map/ppermute | solution.py:108
  21.5 5.3 %collective-permute-start.21 = (f32[192,128]{1,0:T(8,128)S(1)}, f32[192,128]{1,0:T(8,128)S(1)}, u32[]{:S(2)}, u32[]{:S(2)}) collective-permute-start(f32[192,128]{1,0:T(8,128)S(1)} %get-tuple-element.77), channel_id=1, source_target_pairs={{0,1},{1,2},{2,3},{3,0},{4,5},{5,10},{6,7},{7,4},{8,9},{9,6},{10,1... | collective-permute-start | bytes 294920 | tf_op jit(solution)/shard_map/ppermute | solution.py:108
  22.6 4.8 %collective-permute-start.8 = (f32[384,128]{1,0:T(8,128)S(1)}, f32[384,128]{1,0:T(8,128)S(1)}, u32[]{:S(2)}, u32[]{:S(2)}) collective-permute-start(f32[384,128]{1,0:T(8,128)S(1)} %get-tuple-element.58), channel_id=1, source_target_pairs={{0,1},{1,0},{2,3},{3,2},{4,5},{5,4},{6,7},{7,6},{8,9},{9,8},{10,11... | collective-permute-start | bytes 589832 | tf_op jit(solution)/shard_map/ppermute | solution.py:108
  22.6 4.7 %collective-permute-start.9 = (f32[192,128]{1,0:T(8,128)S(1)}, f32[192,128]{1,0:T(8,128)S(1)}, u32[]{:S(2)}, u32[]{:S(2)}) collective-permute-start(f32[192,128]{1,0:T(8,128)S(1)} %get-tuple-element.59), channel_id=1, source_target_pairs={{0,1},{1,0},{2,7},{3,2},{4,5},{5,4},{6,3},{7,6},{8,9},{9,8},{10,15... | collective-permute-start | bytes 294920 | tf_op jit(solution)/shard_map/ppermute | solution.py:108
  25.7 1.6 %collective-permute-start.10 = (f32[192,128]{1,0:T(8,128)S(1)}, f32[192,128]{1,0:T(8,128)S(1)}, u32[]{:S(2)}, u32[]{:S(2)}) collective-permute-start(f32[192,128]{1,0:T(8,128)S(1)} %get-tuple-element.60), channel_id=1, source_target_pairs={{0,1},{1,0},{2,3},{3,2},{4,5},{5,4},{6,11},{7,6},{8,9},{9,8},{10,7... | collective-permute-start | bytes 294920 | tf_op jit(solution)/shard_map/ppermute | solution.py:108
  26.8 4.7 %collective-permute-start.22 = (f32[384,128]{1,0:T(8,128)S(1)}, f32[384,128]{1,0:T(8,128)S(1)}, u32[]{:S(2)}, u32[]{:S(2)}) collective-permute-start(f32[384,128]{1,0:T(8,128)S(1)} %get-tuple-element.80), channel_id=1, source_target_pairs={{0,1},{1,0},{2,3},{3,2},{4,5},{5,4},{6,7},{7,6},{8,9},{9,8},{10,11... | collective-permute-start | bytes 589832 | tf_op jit(solution)/shard_map/ppermute | solution.py:108
  26.8 4.7 %collective-permute-start.23 = (f32[192,128]{1,0:T(8,128)S(1)}, f32[192,128]{1,0:T(8,128)S(1)}, u32[]{:S(2)}, u32[]{:S(2)}) collective-permute-start(f32[192,128]{1,0:T(8,128)S(1)} %get-tuple-element.81), channel_id=1, source_target_pairs={{0,1},{1,0},{2,7},{3,2},{4,5},{5,4},{6,3},{7,6},{8,9},{9,8},{10,15... | collective-permute-start | bytes 294920 | tf_op jit(solution)/shard_map/ppermute | solution.py:108
  27.3 4.2 %collective-permute-start.24 = (f32[192,128]{1,0:T(8,128)S(1)}, f32[192,128]{1,0:T(8,128)S(1)}, u32[]{:S(2)}, u32[]{:S(2)}) collective-permute-start(f32[192,128]{1,0:T(8,128)S(1)} %get-tuple-element.82), channel_id=1, source_target_pairs={{0,1},{1,0},{2,3},{3,2},{4,5},{5,4},{6,11},{7,6},{8,9},{9,8},{10,7... | collective-permute-start | bytes 294920 | tf_op jit(solution)/shard_map/ppermute | solution.py:108
  27.3 7.5 %collective-permute-start.11 = (f32[96,128]{1,0:T(8,128)S(1)}, f32[96,128]{1,0:T(8,128)S(1)}, u32[]{:S(2)}, u32[]{:S(2)}) collective-permute-start(f32[96,128]{1,0:T(8,128)S(1)} %get-tuple-element.61), channel_id=1, source_target_pairs={{0,1},{1,2},{2,3},{3,0},{4,5},{5,6},{6,7},{7,4},{8,9},{9,10},{10,1... | collective-permute-start | bytes 147464 | tf_op jit(solution)/shard_map/ppermute | solution.py:108
  27.8 7.0 %collective-permute-start.12 = (f32[96,128]{1,0:T(8,128)S(1)}, f32[96,128]{1,0:T(8,128)S(1)}, u32[]{:S(2)}, u32[]{:S(2)}) collective-permute-start(f32[96,128]{1,0:T(8,128)S(1)} %get-tuple-element.62), channel_id=1, source_target_pairs={{0,3},{1,0},{2,18},{3,1},{4,7},{5,4},{6,22},{7,5},{8,11},{9,8},{10... | collective-permute-start | bytes 147464 | tf_op jit(solution)/shard_map/ppermute | solution.py:108
  31.5 3.4 %collective-permute-start.13 = (f32[96,128]{1,0:T(8,128)S(1)}, f32[96,128]{1,0:T(8,128)S(1)}, u32[]{:S(2)}, u32[]{:S(2)}) collective-permute-start(f32[96,128]{1,0:T(8,128)S(1)} %get-tuple-element.63), channel_id=1, source_target_pairs={{0,1},{1,0},{2,3},{3,2},{4,5},{5,4},{6,7},{7,6},{8,9},{9,8},{10,11... | collective-permute-start | bytes 147464 | tf_op jit(solution)/shard_map/ppermute | solution.py:108
  31.5 5.0 %collective-permute-start.25 = (f32[96,128]{1,0:T(8,128)S(1)}, f32[96,128]{1,0:T(8,128)S(1)}, u32[]{:S(2)}, u32[]{:S(2)}) collective-permute-start(f32[96,128]{1,0:T(8,128)S(1)} %get-tuple-element.85), channel_id=1, source_target_pairs={{0,1},{1,2},{2,3},{3,0},{4,5},{5,6},{6,7},{7,4},{8,9},{9,10},{10,1... | collective-permute-start | bytes 147464 | tf_op jit(solution)/shard_map/ppermute | solution.py:108
  32.0 4.6 %collective-permute-start.26 = (f32[96,128]{1,0:T(8,128)S(1)}, f32[96,128]{1,0:T(8,128)S(1)}, u32[]{:S(2)}, u32[]{:S(2)}) collective-permute-start(f32[96,128]{1,0:T(8,128)S(1)} %get-tuple-element.86), channel_id=1, source_target_pairs={{0,3},{1,0},{2,18},{3,1},{4,7},{5,4},{6,22},{7,5},{8,11},{9,8},{10... | collective-permute-start | bytes 147464 | tf_op jit(solution)/shard_map/ppermute | solution.py:108
  34.8 1.8 %collective-permute-start.27 = (f32[96,128]{1,0:T(8,128)S(1)}, f32[96,128]{1,0:T(8,128)S(1)}, u32[]{:S(2)}, u32[]{:S(2)}) collective-permute-start(f32[96,128]{1,0:T(8,128)S(1)} %get-tuple-element.87), channel_id=1, source_target_pairs={{0,1},{1,0},{2,3},{3,2},{4,5},{5,4},{6,7},{7,6},{8,9},{9,8},{10,11... | collective-permute-start | bytes 147464 | tf_op jit(solution)/shard_map/ppermute | solution.py:108

commit v8 on v7

--- a/solution.py
+++ b/solution.py
@@ -29,8 +29,9 @@
 
 def section_hop(layer, sections, early=False):
     where = {}
-    if early and layer + 3 < sections:
-        idle_cycle(where, [layer, layer + 1, layer + 2, layer + 3])
+    spare = layer + 2 if layer == 0 else layer - 2
+    if early and spare + 1 < sections:
+        idle_cycle(where, [layer, layer + 1, spare, spare + 1])
     elif layer % 2 == 0:
         idle_cycle(where, [layer, layer + 1])
     elif layer + 2 < sections:
@@ -90,7 +91,7 @@
     if target == last - 1:
         idle_cycle(where, [last, target])
     elif target == 0:
-        idle_cycle(where, [last, 0, 1, last - 1])
+        idle_cycle(where, [last, 0, last - 1])
     else:
         idle_cycle(where, [last, target, target ^ 1])
 
@@ -377,12 +378,14 @@
 
     for layer in range(sections):
         if layer > 0:
-            early = layer == 1
             straight = hop_pairs(layer - 1, shape, lambda t: t)
-            cross_a = hop_pairs(layer - 1, shape, of_a, early)
+            cross_a = [
+                hop_pairs(layer - 1, shape, of_a, layer == 1 or (layer % 2 == 1 and f > 0))
+                for f in range(frames)
+            ]
             cross_b = hop_pairs(layer - 1, shape, of_b)
             main = [send(main[f], straight) for f in range(frames)]
-            near_a = [send(edge_a[f], cross_a) for f in range(frames)]
+            near_a = [send(edge_a[f], cross_a[f]) for f in range(frames)]
             near_b = [send(edge_b[f], cross_b) for f in range(frames)]
         patches, next_main, edge_a, edge_b = [], [], [], []
         for f in range(frames):

time: 37.4 us -> 37.1 us (level)
  starting transfers between devices: 22.4 us -> 22 us
    ppermute x28, starting transfers between devices: 22.4 us -> 22 us  [send(): return lax.ppermute(value, ('groups', 'tiles', 'section'), pairs)]
  transfers between devices with their start and end apart: 28 -> 28, of which waited for: 6 -> 7; matrix products, arithmetic and copies ran while one was open for 0% -> 0% of each run, Pallas kernels for 9% -> 9%
where the time goes in v8:
time: 37.1 us; the launch traced here: 37 us
  starting transfers between devices  22 us (59%)
  waiting for transfers between devices  9.65 us (26%)
  Pallas kernels  5.19 us (14%)
    ppermute x28, starting transfers between devices, send(): return lax.ppermute(value, ('groups', 'tiles', 'section'), pairs)  22 us
    ppermute x28, waiting for transfers between devices, send(): return lax.ppermute(value, ('groups', 'tiles', 'section'), pairs)  9.65 us
    pallas_call x8, Pallas kernels, frame_step(): pl.pallas_call(kernel, out_shape=tuple(out_shape), in_specs=[VMEM] * len(...  2.07 us
    pallas_call x1, Pallas kernels, opening(): pl.pallas_call(kernel, out_shape=tuple(out_shape), in_specs=[HBM, HBM], o...  1.23 us
  transfers between devices with their start and end apart: 28, of which 7 were waited for; matrix products, arithmetic and copies ran while one was open for 0% of the time, Pallas kernels for 9%

profile of v8, /device:TPU:0, one launch (start us, length us, event | category | flops | bytes accessed | tf_op | source)
XLA Modules:
  0.0 37.0 jit_solution(6636825635597265959)
XLA Ops:
  0.0 1.2 %opening.1 = (f32[2,384,128]{2,1,0:T(8,128)S(1)}, f32[192,128]{1,0:T(8,128)S(1)}, f32[192,128]{1,0:T(8,128)S(1)}, f32[192,128]{1,0:T(8,128)S(1)}, f32[192,128]{1,0:T(8,128)S(1)}, /*index=5*/f32[192,128]{1,0:T(8,128)S(1)}) custom-call(f32[2,384,128]{2,1,0:T(8,128)} %bitcast.4, f32[1,192]{1,0:T(1,128)} %gain_ref.1), custom_call_target="tpu_custom_call" | custom-call | flops 2000000000 | bytes 1048576 | tf_op jit(solution)/shard_map/opening/pallas_call | solution.py:187
  1.2 3.1 %collective-permute-start = (f32[192,128]{1,0:T(8,128)S(1)}, f32[192,128]{1,0:T(8,128)S(1)}, u32[]{:S(2)}, u32[]{:S(2)}) collective-permute-start(f32[192,128]{1,0:T(8,128)S(1)} %get-tuple-element.48), channel_id=1, source_target_pairs={{0,4},{1,17},{2,3},{3,2},{4,0},{5,21},{6,7},{7,6},{8,12},{9,25},{1... | collective-permute-start | bytes 294920 | tf_op jit(solution)/shard_map/ppermute | solution.py:109
  4.4 3.1 %collective-permute-start.14 = (f32[192,128]{1,0:T(8,128)S(1)}, f32[192,128]{1,0:T(8,128)S(1)}, u32[]{:S(2)}, u32[]{:S(2)}) collective-permute-start(f32[192,128]{1,0:T(8,128)S(1)} %get-tuple-element.65), channel_id=1, source_target_pairs={{0,4},{1,17},{2,3},{3,2},{4,0},{5,21},{6,7},{7,6},{8,12},{9,25},{1... | collective-permute-start | bytes 294920 | tf_op jit(solution)/shard_map/ppermute | solution.py:109
  7.5 0.5 %prepare.1 = (bf16[384,1792]{1,0:T(8,128)(2,1)S(1)}, bf16[384,1792]{1,0:T(8,128)(2,1)S(1)}) custom-call(f32[27,192,192]{2,1,0:T(8,128)S(1)} %bitcast.3), custom_call_target="tpu_custom_call" | custom-call | tf_op jit(solution)/shard_map/prepare/pallas_call | solution.py:140
  8.1 1.0 %frame_step.8 = (f32[384,128]{1,0:T(8,128)S(1)}, f32[192,128]{1,0:T(8,128)S(1)}, f32[192,128]{1,0:T(8,128)S(1)}, bf16[1792,256]{1,0:T(8,128)(2,1)S(1)}, bf16[1792,256]{1,0:T(8,128)(2,1)S(1)}) custom-call(f32[2,384,128]{2,1,0:T(8,128)S(1)} %get-tuple-element.47.refs_0_, f32[192,128]{1,0:T(8,128)S(1)} %collective-permute-done.refs_1_, ...), custom_call_target="tpu_custom_call" | custom-call | flops 528482304 | bytes 1048576 | tf_op jit(solution)/shard_map/frame_step/pallas_call | solution.py:308
  9.1 0.1 collective-permute-start.2
  9.2 2.1 %collective-permute-start.3 = (f32[192,128]{1,0:T(8,128)S(1)}, f32[192,128]{1,0:T(8,128)S(1)}, u32[]{:S(2)}, u32[]{:S(2)}) collective-permute-start(f32[192,128]{1,0:T(8,128)S(1)} %get-tuple-element.53), channel_id=1, source_target_pairs={{0,5},{1,2},{2,3},{3,0},{4,1},{5,6},{6,7},{7,4},{8,13},{9,10},{10,... | collective-permute-start | bytes 294920 | tf_op jit(solution)/shard_map/ppermute | solution.py:109
  11.3 0.7 %earlier_frames.4.refs_5_ = f32[192,256]{1,0:T(8,128)S(1)} custom-call(bf16[384,1792]{1,0:T(8,128)(2,1)S(1)} %get-tuple-element.67.refs_0_, bf16[1792,256]{1,0:T(8,128)(2,1)S(1)} %get-tuple-element.68.refs_1_, bf16[1792,256]{1,0:T(8,128)(2,1)S(1)} %get-tuple-element.69.refs_2_), custom_call_target="tpu_custom_call" | custom-call | flops 528482304 | bytes 1048576 | tf_op jit(solution)/shard_map/earlier_frames/pallas_call | solution.py:346
  12.0 1.0 %frame_step.12 = (f32[384,128]{1,0:T(8,128)S(1)}, f32[192,128]{1,0:T(8,128)S(1)}, f32[192,128]{1,0:T(8,128)S(1)}) custom-call(f32[2,384,128]{2,1,0:T(8,128)S(1)} %get-tuple-element.47.refs_0_, f32[192,128]{1,0:T(8,128)S(1)} %collective-permute-done.14.refs_1_, f32[192,128]{1,0:T(8,128)S(1)} %collective-permute-done.15.refs_2_, ...), custom_call_target="tpu_custom_call" | custom-call | flops 528482304 | bytes 1048576 | tf_op jit(solution)/shard_map/frame_step/pallas_call | solution.py:308
  13.1 0.1 collective-permute-start.16
  13.1 2.1 %collective-permute-start.17 = (f32[192,128]{1,0:T(8,128)S(1)}, f32[192,128]{1,0:T(8,128)S(1)}, u32[]{:S(2)}, u32[]{:S(2)}) collective-permute-start(f32[192,128]{1,0:T(8,128)S(1)} %get-tuple-element.71), channel_id=1, source_target_pairs={{0,5},{1,2},{2,3},{3,0},{4,1},{5,6},{6,7},{7,4},{8,13},{9,10},{10,... | collective-permute-start | bytes 294920 | tf_op jit(solution)/shard_map/ppermute | solution.py:109
  15.3 1.5 %collective-permute-start.5 = (f32[384,128]{1,0:T(8,128)S(1)}, f32[384,128]{1,0:T(8,128)S(1)}, u32[]{:S(2)}, u32[]{:S(2)}) collective-permute-start(f32[384,128]{1,0:T(8,128)S(1)} %get-tuple-element.55), channel_id=1, source_target_pairs={{0,1},{1,2},{2,3},{3,0},{4,5},{5,6},{6,7},{7,4},{8,9},{9,10},{10,1... | collective-permute-start | bytes 589832 | tf_op jit(solution)/shard_map/ppermute | solution.py:109
  16.8 0.1 collective-permute-start.6
  16.9 0.6 %collective-permute-done.17.refs_1_ = f32[192,128]{1,0:T(8,128)S(1)} collective-permute-done((f32[192,128]{1,0:T(8,128)S(1)}, f32[192,128]{1,0:T(8,128)S(1)}, u32[]{:S(2)}, u32[]{:S(2)}) %collective-permute-start.17) | collective-permute-done | bytes 98336 | tf_op jit(solution)/shard_map/ppermute | solution.py:109
  17.5 0.3 collective-permute-start.7
  17.8 1.1 %collective-permute-start.19 = (f32[384,128]{1,0:T(8,128)S(1)}, f32[384,128]{1,0:T(8,128)S(1)}, u32[]{:S(2)}, u32[]{:S(2)}) collective-permute-start(f32[384,128]{1,0:T(8,128)S(1)} %get-tuple-element.75), channel_id=1, source_target_pairs={{0,1},{1,2},{2,3},{3,0},{4,5},{5,6},{6,7},{7,4},{8,9},{9,10},{10,1... | collective-permute-start | bytes 589832 | tf_op jit(solution)/shard_map/ppermute | solution.py:109
  18.9 0.2 collective-permute-start.20
  19.1 2.4 %collective-permute-done.6.refs_1_ = f32[192,128]{1,0:T(8,128)S(1)} collective-permute-done((f32[192,128]{1,0:T(8,128)S(1)}, f32[192,128]{1,0:T(8,128)S(1)}, u32[]{:S(2)}, u32[]{:S(2)}) %collective-permute-start.6) | collective-permute-done | bytes 98336 | tf_op jit(solution)/shard_map/ppermute | solution.py:109
  21.5 1.1 %collective-permute-done.7.refs_2_ = f32[192,128]{1,0:T(8,128)S(1)} collective-permute-done((f32[192,128]{1,0:T(8,128)S(1)}, f32[192,128]{1,0:T(8,128)S(1)}, u32[]{:S(2)}, u32[]{:S(2)}) %collective-permute-start.7) | collective-permute-done | bytes 98336 | tf_op jit(solution)/shard_map/ppermute | solution.py:109
  22.6 0.1 collective-permute-start.8
  22.6 0.4 %collective-permute-start.9 = (f32[192,128]{1,0:T(8,128)S(1)}, f32[192,128]{1,0:T(8,128)S(1)}, u32[]{:S(2)}, u32[]{:S(2)}) collective-permute-start(f32[192,128]{1,0:T(8,128)S(1)} %get-tuple-element.59), channel_id=1, source_target_pairs={{0,1},{1,0},{2,7},{3,2},{4,5},{5,4},{6,3},{7,6},{8,9},{9,8},{10,15... | collective-permute-start | bytes 294920 | tf_op jit(solution)/shard_map/ppermute | solution.py:109
  23.1 2.6 %collective-permute-done.20.refs_1_ = f32[192,128]{1,0:T(8,128)S(1)} collective-permute-done((f32[192,128]{1,0:T(8,128)S(1)}, f32[192,128]{1,0:T(8,128)S(1)}, u32[]{:S(2)}, u32[]{:S(2)}) %collective-permute-start.20) | collective-permute-done | bytes 98336 | tf_op jit(solution)/shard_map/ppermute | solution.py:109
  25.7 1.0 %collective-permute-done.21.refs_2_ = f32[192,128]{1,0:T(8,128)S(1)} collective-permute-done((f32[192,128]{1,0:T(8,128)S(1)}, f32[192,128]{1,0:T(8,128)S(1)}, u32[]{:S(2)}, u32[]{:S(2)}) %collective-permute-start.21) | collective-permute-done | bytes 98336 | tf_op jit(solution)/shard_map/ppermute | solution.py:109
  26.8 0.5 %collective-permute-start.23 = (f32[192,128]{1,0:T(8,128)S(1)}, f32[192,128]{1,0:T(8,128)S(1)}, u32[]{:S(2)}, u32[]{:S(2)}) collective-permute-start(f32[192,128]{1,0:T(8,128)S(1)} %get-tuple-element.81), channel_id=1, source_target_pairs={{0,1},{1,2},{2,7},{3,0},{4,5},{5,6},{6,3},{7,4},{8,9},{9,10},{10,1... | collective-permute-start | bytes 294920 | tf_op jit(solution)/shard_map/ppermute | solution.py:109
  27.3 2.1 %collective-permute-start.24 = (f32[192,128]{1,0:T(8,128)S(1)}, f32[192,128]{1,0:T(8,128)S(1)}, u32[]{:S(2)}, u32[]{:S(2)}) collective-permute-start(f32[192,128]{1,0:T(8,128)S(1)} %get-tuple-element.82), channel_id=1, source_target_pairs={{0,1},{1,0},{2,3},{3,2},{4,5},{5,4},{6,11},{7,6},{8,9},{9,8},{10,7... | collective-permute-start | bytes 294920 | tf_op jit(solution)/shard_map/ppermute | solution.py:109
  29.4 1.2 %collective-permute-start.11 = (f32[96,128]{1,0:T(8,128)S(1)}, f32[96,128]{1,0:T(8,128)S(1)}, u32[]{:S(2)}, u32[]{:S(2)}) collective-permute-start(f32[96,128]{1,0:T(8,128)S(1)} %get-tuple-element.61), channel_id=1, source_target_pairs={{0,2},{1,17},{2,3},{3,0},{4,6},{5,21},{6,7},{7,4},{8,10},{9,25},{1... | collective-permute-start | bytes 147464 | tf_op jit(solution)/shard_map/ppermute | solution.py:109
  30.6 0.9 %collective-permute-start.12 = (f32[96,128]{1,0:T(8,128)S(1)}, f32[96,128]{1,0:T(8,128)S(1)}, u32[]{:S(2)}, u32[]{:S(2)}) collective-permute-start(f32[96,128]{1,0:T(8,128)S(1)} %get-tuple-element.62), channel_id=1, source_target_pairs={{0,3},{1,0},{2,18},{3,1},{4,7},{5,4},{6,22},{7,5},{8,11},{9,8},{10... | collective-permute-start | bytes 147464 | tf_op jit(solution)/shard_map/ppermute | solution.py:109
  31.5 0.2 collective-permute-done.23.refs_1_
  31.7 2.1 %collective-permute-start.25 = (f32[96,128]{1,0:T(8,128)S(1)}, f32[96,128]{1,0:T(8,128)S(1)}, u32[]{:S(2)}, u32[]{:S(2)}) collective-permute-start(f32[96,128]{1,0:T(8,128)S(1)} %get-tuple-element.85), channel_id=1, source_target_pairs={{0,2},{1,17},{2,3},{3,0},{4,6},{5,21},{6,7},{7,4},{8,10},{9,25},{1... | collective-permute-start | bytes 147464 | tf_op jit(solution)/shard_map/ppermute | solution.py:109
  33.8 0.8 %collective-permute-start.26 = (f32[96,128]{1,0:T(8,128)S(1)}, f32[96,128]{1,0:T(8,128)S(1)}, u32[]{:S(2)}, u32[]{:S(2)}) collective-permute-start(f32[96,128]{1,0:T(8,128)S(1)} %get-tuple-element.86), channel_id=1, source_target_pairs={{0,3},{1,0},{2,18},{3,1},{4,7},{5,4},{6,22},{7,5},{8,11},{9,8},{10... | collective-permute-start | bytes 147464 | tf_op jit(solution)/shard_map/ppermute | solution.py:109
  34.6 1.7 %collective-permute-done.25.refs_4_ = f32[96,128]{1,0:T(8,128)S(1)} collective-permute-done((f32[96,128]{1,0:T(8,128)S(1)}, f32[96,128]{1,0:T(8,128)S(1)}, u32[]{:S(2)}, u32[]{:S(2)}) %collective-permute-start.25) | collective-permute-done | bytes 49184 | tf_op jit(solution)/shard_map/ppermute | solution.py:109
  36.3 0.7 %assemble.1 = f32[2,96,128]{2,1,0:T(8,128)} custom-call(f32[96,128]{1,0:T(8,128)S(1)} %collective-permute-done.11.refs_0_, f32[96,128]{1,0:T(8,128)S(1)} %collective-permute-done.12.refs_1_, f32[96,128]{1,0:T(8,128)S(1)} %collective-permute-done.13.refs_2_, f32[96,128]{1,0:T(8,128)S(1)} %get-tuple-element.64.refs_3_, ...), custom_call_target="tpu_custom_call" | custom-call | tf_op jit(solution)/shard_map/assemble/pallas_call | solution.py:431
  (41 shorter events, 0.2 us)
Async XLA Ops:
  0.0 7.5 %copy-start = (f32[1,27,192,192]{3,2,1,0:T(8,128)S(1)}, f32[1,27,192,192]{3,2,1,0:T(8,128)}, u32[]{:S(2)}) copy-start(f32[1,27,192,192]{3,2,1,0:T(8,128)} %param.4) | copy-start | bytes 11943940
  1.2 6.8 %collective-permute-start = (f32[192,128]{1,0:T(8,128)S(1)}, f32[192,128]{1,0:T(8,128)S(1)}, u32[]{:S(2)}, u32[]{:S(2)}) collective-permute-start(f32[192,128]{1,0:T(8,128)S(1)} %get-tuple-element.48), channel_id=1, source_target_pairs={{0,4},{1,17},{2,3},{3,2},{4,0},{5,21},{6,7},{7,6},{8,12},{9,25},{1... | collective-permute-start | bytes 294920 | tf_op jit(solution)/shard_map/ppermute | solution.py:109
  4.4 3.7 %collective-permute-start.1 = (f32[192,128]{1,0:T(8,128)S(1)}, f32[192,128]{1,0:T(8,128)S(1)}, u32[]{:S(2)}, u32[]{:S(2)}) collective-permute-start(f32[192,128]{1,0:T(8,128)S(1)} %get-tuple-element.49), channel_id=1, source_target_pairs={{0,1},{1,0},{2,3},{3,2},{4,8},{5,21},{6,7},{7,6},{8,4},{9,25},{10,... | collective-permute-start | bytes 294920 | tf_op jit(solution)/shard_map/ppermute | solution.py:109
  4.4 7.6 %collective-permute-start.14 = (f32[192,128]{1,0:T(8,128)S(1)}, f32[192,128]{1,0:T(8,128)S(1)}, u32[]{:S(2)}, u32[]{:S(2)}) collective-permute-start(f32[192,128]{1,0:T(8,128)S(1)} %get-tuple-element.65), channel_id=1, source_target_pairs={{0,4},{1,17},{2,3},{3,2},{4,0},{5,21},{6,7},{7,6},{8,12},{9,25},{1... | collective-permute-start | bytes 294920 | tf_op jit(solution)/shard_map/ppermute | solution.py:109
  7.5 4.5 %collective-permute-start.15 = (f32[192,128]{1,0:T(8,128)S(1)}, f32[192,128]{1,0:T(8,128)S(1)}, u32[]{:S(2)}, u32[]{:S(2)}) collective-permute-start(f32[192,128]{1,0:T(8,128)S(1)} %get-tuple-element.66), channel_id=1, source_target_pairs={{0,1},{1,0},{2,3},{3,2},{4,8},{5,21},{6,7},{7,6},{8,4},{9,25},{10,... | collective-permute-start | bytes 294920 | tf_op jit(solution)/shard_map/ppermute | solution.py:109
  9.1 6.2 %collective-permute-start.2 = (f32[384,128]{1,0:T(8,128)S(1)}, f32[384,128]{1,0:T(8,128)S(1)}, u32[]{:S(2)}, u32[]{:S(2)}) collective-permute-start(f32[384,128]{1,0:T(8,128)S(1)} %get-tuple-element.52), channel_id=1, source_target_pairs={{0,1},{1,0},{2,3},{3,2},{4,5},{5,4},{6,7},{7,6},{8,9},{9,8},{10,11... | collective-permute-start | bytes 589832 | tf_op jit(solution)/shard_map/ppermute | solution.py:109
  9.2 6.1 %collective-permute-start.3 = (f32[192,128]{1,0:T(8,128)S(1)}, f32[192,128]{1,0:T(8,128)S(1)}, u32[]{:S(2)}, u32[]{:S(2)}) collective-permute-start(f32[192,128]{1,0:T(8,128)S(1)} %get-tuple-element.53), channel_id=1, source_target_pairs={{0,5},{1,2},{2,3},{3,0},{4,1},{5,6},{6,7},{7,4},{8,13},{9,10},{10,... | collective-permute-start | bytes 294920 | tf_op jit(solution)/shard_map/ppermute | solution.py:109
  11.3 4.0 %collective-permute-start.4 = (f32[192,128]{1,0:T(8,128)S(1)}, f32[192,128]{1,0:T(8,128)S(1)}, u32[]{:S(2)}, u32[]{:S(2)}) collective-permute-start(f32[192,128]{1,0:T(8,128)S(1)} %get-tuple-element.54), channel_id=1, source_target_pairs={{0,1},{1,0},{2,3},{3,2},{4,9},{5,4},{6,7},{7,6},{8,5},{9,8},{10,11... | collective-permute-start | bytes 294920 | tf_op jit(solution)/shard_map/ppermute | solution.py:109
  13.1 4.7 %collective-permute-start.16 = (f32[384,128]{1,0:T(8,128)S(1)}, f32[384,128]{1,0:T(8,128)S(1)}, u32[]{:S(2)}, u32[]{:S(2)}) collective-permute-start(f32[384,128]{1,0:T(8,128)S(1)} %get-tuple-element.70), channel_id=1, source_target_pairs={{0,1},{1,0},{2,3},{3,2},{4,5},{5,4},{6,7},{7,6},{8,9},{9,8},{10,11... | collective-permute-start | bytes 589832 | tf_op jit(solution)/shard_map/ppermute | solution.py:109
  13.1 4.3 %collective-permute-start.17 = (f32[192,128]{1,0:T(8,128)S(1)}, f32[192,128]{1,0:T(8,128)S(1)}, u32[]{:S(2)}, u32[]{:S(2)}) collective-permute-start(f32[192,128]{1,0:T(8,128)S(1)} %get-tuple-element.71), channel_id=1, source_target_pairs={{0,5},{1,2},{2,3},{3,0},{4,1},{5,6},{6,7},{7,4},{8,13},{9,10},{10,... | collective-permute-start | bytes 294920 | tf_op jit(solution)/shard_map/ppermute | solution.py:109
  15.3 2.5 %collective-permute-start.18 = (f32[192,128]{1,0:T(8,128)S(1)}, f32[192,128]{1,0:T(8,128)S(1)}, u32[]{:S(2)}, u32[]{:S(2)}) collective-permute-start(f32[192,128]{1,0:T(8,128)S(1)} %get-tuple-element.72), channel_id=1, source_target_pairs={{0,1},{1,0},{2,3},{3,2},{4,9},{5,4},{6,7},{7,6},{8,5},{9,8},{10,11... | collective-permute-start | bytes 294920 | tf_op jit(solution)/shard_map/ppermute | solution.py:109
  15.3 7.3 %collective-permute-start.5 = (f32[384,128]{1,0:T(8,128)S(1)}, f32[384,128]{1,0:T(8,128)S(1)}, u32[]{:S(2)}, u32[]{:S(2)}) collective-permute-start(f32[384,128]{1,0:T(8,128)S(1)} %get-tuple-element.55), channel_id=1, source_target_pairs={{0,1},{1,2},{2,3},{3,0},{4,5},{5,6},{6,7},{7,4},{8,9},{9,10},{10,1... | collective-permute-start | bytes 589832 | tf_op jit(solution)/shard_map/ppermute | solution.py:109
  16.8 4.7 %collective-permute-start.6 = (f32[192,128]{1,0:T(8,128)S(1)}, f32[192,128]{1,0:T(8,128)S(1)}, u32[]{:S(2)}, u32[]{:S(2)}) collective-permute-start(f32[192,128]{1,0:T(8,128)S(1)} %get-tuple-element.56), channel_id=1, source_target_pairs={{0,1},{1,6},{2,3},{3,0},{4,5},{5,2},{6,7},{7,4},{8,9},{9,14},{10,1... | collective-permute-start | bytes 294920 | tf_op jit(solution)/shard_map/ppermute | solution.py:109
  17.5 5.1 %collective-permute-start.7 = (f32[192,128]{1,0:T(8,128)S(1)}, f32[192,128]{1,0:T(8,128)S(1)}, u32[]{:S(2)}, u32[]{:S(2)}) collective-permute-start(f32[192,128]{1,0:T(8,128)S(1)} %get-tuple-element.57), channel_id=1, source_target_pairs={{0,1},{1,2},{2,3},{3,0},{4,5},{5,10},{6,7},{7,4},{8,9},{9,6},{10,1... | collective-permute-start | bytes 294920 | tf_op jit(solution)/shard_map/ppermute | solution.py:109
  17.8 9.0 %collective-permute-start.19 = (f32[384,128]{1,0:T(8,128)S(1)}, f32[384,128]{1,0:T(8,128)S(1)}, u32[]{:S(2)}, u32[]{:S(2)}) collective-permute-start(f32[384,128]{1,0:T(8,128)S(1)} %get-tuple-element.75), channel_id=1, source_target_pairs={{0,1},{1,2},{2,3},{3,0},{4,5},{5,6},{6,7},{7,4},{8,9},{9,10},{10,1... | collective-permute-start | bytes 589832 | tf_op jit(solution)/shard_map/ppermute | solution.py:109
  18.9 6.8 %collective-permute-start.20 = (f32[192,128]{1,0:T(8,128)S(1)}, f32[192,128]{1,0:T(8,128)S(1)}, u32[]{:S(2)}, u32[]{:S(2)}) collective-permute-start(f32[192,128]{1,0:T(8,128)S(1)} %get-tuple-element.76), channel_id=1, source_target_pairs={{0,1},{1,6},{2,3},{3,0},{4,5},{5,2},{6,7},{7,4},{8,9},{9,14},{10,1... | collective-permute-start | bytes 294920 | tf_op jit(solution)/shard_map/ppermute | solution.py:109
  21.5 5.3 %collective-permute-start.21 = (f32[192,128]{1,0:T(8,128)S(1)}, f32[192,128]{1,0:T(8,128)S(1)}, u32[]{:S(2)}, u32[]{:S(2)}) collective-permute-start(f32[192,128]{1,0:T(8,128)S(1)} %get-tuple-element.77), channel_id=1, source_target_pairs={{0,1},{1,2},{2,3},{3,0},{4,5},{5,10},{6,7},{7,4},{8,9},{9,6},{10,1... | collective-permute-start | bytes 294920 | tf_op jit(solution)/shard_map/ppermute | solution.py:109
  22.6 6.9 %collective-permute-start.8 = (f32[384,128]{1,0:T(8,128)S(1)}, f32[384,128]{1,0:T(8,128)S(1)}, u32[]{:S(2)}, u32[]{:S(2)}) collective-permute-start(f32[384,128]{1,0:T(8,128)S(1)} %get-tuple-element.58), channel_id=1, source_target_pairs={{0,1},{1,0},{2,3},{3,2},{4,5},{5,4},{6,7},{7,6},{8,9},{9,8},{10,11... | collective-permute-start | bytes 589832 | tf_op jit(solution)/shard_map/ppermute | solution.py:109
  22.6 4.7 %collective-permute-start.9 = (f32[192,128]{1,0:T(8,128)S(1)}, f32[192,128]{1,0:T(8,128)S(1)}, u32[]{:S(2)}, u32[]{:S(2)}) collective-permute-start(f32[192,128]{1,0:T(8,128)S(1)} %get-tuple-element.59), channel_id=1, source_target_pairs={{0,1},{1,0},{2,7},{3,2},{4,5},{5,4},{6,3},{7,6},{8,9},{9,8},{10,15... | collective-permute-start | bytes 294920 | tf_op jit(solution)/shard_map/ppermute | solution.py:109
  25.7 3.7 %collective-permute-start.10 = (f32[192,128]{1,0:T(8,128)S(1)}, f32[192,128]{1,0:T(8,128)S(1)}, u32[]{:S(2)}, u32[]{:S(2)}) collective-permute-start(f32[192,128]{1,0:T(8,128)S(1)} %get-tuple-element.60), channel_id=1, source_target_pairs={{0,1},{1,0},{2,3},{3,2},{4,5},{5,4},{6,11},{7,6},{8,9},{9,8},{10,7... | collective-permute-start | bytes 294920 | tf_op jit(solution)/shard_map/ppermute | solution.py:109
  26.8 4.9 %collective-permute-start.22 = (f32[384,128]{1,0:T(8,128)S(1)}, f32[384,128]{1,0:T(8,128)S(1)}, u32[]{:S(2)}, u32[]{:S(2)}) collective-permute-start(f32[384,128]{1,0:T(8,128)S(1)} %get-tuple-element.80), channel_id=1, source_target_pairs={{0,1},{1,0},{2,3},{3,2},{4,5},{5,4},{6,7},{7,6},{8,9},{9,8},{10,11... | collective-permute-start | bytes 589832 | tf_op jit(solution)/shard_map/ppermute | solution.py:109
  26.8 4.9 %collective-permute-start.23 = (f32[192,128]{1,0:T(8,128)S(1)}, f32[192,128]{1,0:T(8,128)S(1)}, u32[]{:S(2)}, u32[]{:S(2)}) collective-permute-start(f32[192,128]{1,0:T(8,128)S(1)} %get-tuple-element.81), channel_id=1, source_target_pairs={{0,1},{1,2},{2,7},{3,0},{4,5},{5,6},{6,3},{7,4},{8,9},{9,10},{10,1... | collective-permute-start | bytes 294920 | tf_op jit(solution)/shard_map/ppermute | solution.py:109
  27.3 4.4 %collective-permute-start.24 = (f32[192,128]{1,0:T(8,128)S(1)}, f32[192,128]{1,0:T(8,128)S(1)}, u32[]{:S(2)}, u32[]{:S(2)}) collective-permute-start(f32[192,128]{1,0:T(8,128)S(1)} %get-tuple-element.82), channel_id=1, source_target_pairs={{0,1},{1,0},{2,3},{3,2},{4,5},{5,4},{6,11},{7,6},{8,9},{9,8},{10,7... | collective-permute-start | bytes 294920 | tf_op jit(solution)/shard_map/ppermute | solution.py:109
  29.4 5.2 %collective-permute-start.11 = (f32[96,128]{1,0:T(8,128)S(1)}, f32[96,128]{1,0:T(8,128)S(1)}, u32[]{:S(2)}, u32[]{:S(2)}) collective-permute-start(f32[96,128]{1,0:T(8,128)S(1)} %get-tuple-element.61), channel_id=1, source_target_pairs={{0,2},{1,17},{2,3},{3,0},{4,6},{5,21},{6,7},{7,4},{8,10},{9,25},{1... | collective-permute-start | bytes 147464 | tf_op jit(solution)/shard_map/ppermute | solution.py:109
  30.6 4.0 %collective-permute-start.12 = (f32[96,128]{1,0:T(8,128)S(1)}, f32[96,128]{1,0:T(8,128)S(1)}, u32[]{:S(2)}, u32[]{:S(2)}) collective-permute-start(f32[96,128]{1,0:T(8,128)S(1)} %get-tuple-element.62), channel_id=1, source_target_pairs={{0,3},{1,0},{2,18},{3,1},{4,7},{5,4},{6,22},{7,5},{8,11},{9,8},{10... | collective-permute-start | bytes 147464 | tf_op jit(solution)/shard_map/ppermute | solution.py:109
  31.6 3.0 %collective-permute-start.13 = (f32[96,128]{1,0:T(8,128)S(1)}, f32[96,128]{1,0:T(8,128)S(1)}, u32[]{:S(2)}, u32[]{:S(2)}) collective-permute-start(f32[96,128]{1,0:T(8,128)S(1)} %get-tuple-element.63), channel_id=1, source_target_pairs={{0,1},{1,0},{2,3},{3,2},{4,5},{5,4},{6,7},{7,6},{8,9},{9,8},{10,11... | collective-permute-start | bytes 147464 | tf_op jit(solution)/shard_map/ppermute | solution.py:109
  31.7 4.6 %collective-permute-start.25 = (f32[96,128]{1,0:T(8,128)S(1)}, f32[96,128]{1,0:T(8,128)S(1)}, u32[]{:S(2)}, u32[]{:S(2)}) collective-permute-start(f32[96,128]{1,0:T(8,128)S(1)} %get-tuple-element.85), channel_id=1, source_target_pairs={{0,2},{1,17},{2,3},{3,0},{4,6},{5,21},{6,7},{7,4},{8,10},{9,25},{1... | collective-permute-start | bytes 147464 | tf_op jit(solution)/shard_map/ppermute | solution.py:109
  33.8 2.6 %collective-permute-start.26 = (f32[96,128]{1,0:T(8,128)S(1)}, f32[96,128]{1,0:T(8,128)S(1)}, u32[]{:S(2)}, u32[]{:S(2)}) collective-permute-start(f32[96,128]{1,0:T(8,128)S(1)} %get-tuple-element.86), channel_id=1, source_target_pairs={{0,3},{1,0},{2,18},{3,1},{4,7},{5,4},{6,22},{7,5},{8,11},{9,8},{10... | collective-permute-start | bytes 147464 | tf_op jit(solution)/shard_map/ppermute | solution.py:109
  34.6 1.8 %collective-permute-start.27 = (f32[96,128]{1,0:T(8,128)S(1)}, f32[96,128]{1,0:T(8,128)S(1)}, u32[]{:S(2)}, u32[]{:S(2)}) collective-permute-start(f32[96,128]{1,0:T(8,128)S(1)} %get-tuple-element.87), channel_id=1, source_target_pairs={{0,1},{1,0},{2,3},{3,2},{4,5},{5,4},{6,7},{7,6},{8,9},{9,8},{10,11... | collective-permute-start | bytes 147464 | tf_op jit(solution)/shard_map/ppermute | solution.py:109
